TPU v7x, 128 devices: a whole 4x4x4 slice. The times are simulated.
128 devices in a mesh: ctx: 16 (over z, x), head: 8 (over y, core).
Axes of the slice: x: 4, y: 4, z: 4, core: 2. Of those that a mesh axis runs over, the one named last changes fastest.
Arguments:
- queries: bfloat16 [16384, 2048], P(('ctx', 'head')), may hold values from -6 to 6
- keys: bfloat16 [16384, 2048], P(('ctx', 'head')), may hold values from -6 to 6
- values: bfloat16 [16384, 2048], P(('ctx', 'head')), may hold values from -6 to 6
- grads_out: bfloat16 [16384, 2048], P(('ctx', 'head')), may hold values from -6 to 6
- log_decay: float32 [16, 16384], P('head', 'ctx'), may hold values from -0.8 to 0
- ridge: float32 [16], P('head'), may hold values from 0.25 to 2
Outputs:
- grad_queries: bfloat16 [16384, 2048], P(('ctx', 'head'))
- grad_keys: bfloat16 [16384, 2048], P(('ctx', 'head'))
- grad_values: bfloat16 [16384, 2048], P(('ctx', 'head'))
All inputs are finite; a program needn't handle non-finite values.
Results may differ from a plain program's by a relative error of at most 0.0085.
Values may be sent and summed in bfloat16 or wider, within the bound.
No kernel may reach another device: no remote copies, remote signals or barrier semaphores. Data moves between devices by JAX's collectives and lax.ppermute only.
A program may use at most 128 MiB of HBM per device.

v0:
```python
import jax
import jax.numpy as jnp
from jax import lax
from jax.sharding import PartitionSpec as P

DH = 128
SPAN = 512
SOLVE_STEPS = 8


highest = lax.Precision.HIGHEST
epsilon = 1e-06


def laid_out(tiles, dim):
    tiles = jnp.moveaxis(tiles, 0, dim)
    lengths = tiles.shape
    return tiles.reshape(*lengths[:dim], lengths[dim] * lengths[dim + 1], *lengths[dim + 2 :])


def copy_for_each(array, axis):
    copies = jnp.broadcast_to(array, (lax.axis_size(axis), *array.shape))
    return lax.all_to_all(copies, axis, split_axis=0, concat_axis=0, tiled=True)


def collect(array, axis, dim):
    return laid_out(copy_for_each(array, axis), dim)


def side_by_side(arrays, axis, dim, along):
    ends, at = ([], 0)
    for a in arrays[:-1]:
        at += a.shape[along]
        ends.append(at)
    both = jnp.concatenate(arrays, axis=along)
    return tuple(jnp.split(lax.all_gather(both, axis, axis=dim, tiled=True), ends, axis=along))


def product(left, right):
    return jnp.dot(
        left.astype(jnp.float32),
        right.astype(jnp.float32),
        precision=highest,
        preferred_element_type=jnp.float32,
    )


def mixed(left, right):
    return jnp.dot(left, right, preferred_element_type=jnp.float32)


def block_decays(log_gate):
    cumul = jnp.cumsum(log_gate)
    size = log_gate.shape[0]
    rowpos = lax.broadcasted_iota(jnp.int32, (size, size), 0)
    column_position = lax.broadcasted_iota(jnp.int32, (size, size), 1)
    within = jnp.exp(
        jnp.where(rowpos >= column_position, cumul[:, None] - cumul[None, :], -jnp.inf)
    )
    return (cumul, within)


def multiply_by_matrix(direction, gram, keys, within, start_decay, ridge):
    scores = (within * mixed(direction.astype(jnp.bfloat16), keys.T)).astype(jnp.bfloat16)
    return start_decay[:, None] * product(direction, gram) + mixed(scores, keys) + ridge * direction


def conj_grad(rhs, gram, keys, within, start_decay, ridge):
    solution = jnp.zeros_like(rhs)
    residual = rhs
    direction = rhs
    rho_now = jnp.sum(rhs * rhs, axis=-1, keepdims=True)
    for sweep in range(SOLVE_STEPS):
        image = multiply_by_matrix(direction, gram, keys, within, start_decay, ridge)
        step_size = rho_now / (jnp.sum(direction * image, axis=-1, keepdims=True) + epsilon)
        solution = solution + step_size * direction
        residual = residual - step_size * image
        rho_next = jnp.sum(residual * residual, axis=-1, keepdims=True)
        direction = residual + rho_next / (rho_now + epsilon) * direction
        rho_now = rho_next
    return solution


def span_solve(gram, value_state, queries, keys, values, grads_out, log_gate, ridge):
    cumul, within = block_decays(log_gate)
    start_decay = jnp.exp(cumul)
    solved = conj_grad(queries.astype(jnp.float32), gram, keys, within, start_decay, ridge)
    scores = (within * mixed(grads_out, values.T)).astype(jnp.bfloat16)
    rhs = start_decay[:, None] * product(grads_out, value_state) + mixed(scores, keys)
    adjoint = conj_grad(rhs, gram, keys, within, start_decay, ridge)
    return (solved, adjoint)


def span_grads(value_memory_state, state_gram, keys, values, grads_out, solved, adjoint, log_gate):
    cumul, within = block_decays(log_gate)
    end_weight = jnp.exp(cumul[-1] - cumul)[:, None]
    solved_low = solved.astype(jnp.bfloat16)
    adjoint_low = adjoint.astype(jnp.bfloat16)
    solved_along_keys = (within * mixed(solved_low, keys.T)).astype(jnp.bfloat16)
    along_adjoint = (within * mixed(adjoint_low, keys.T)).astype(jnp.bfloat16)
    along_values = (within * mixed(grads_out, values.T)).astype(jnp.bfloat16)
    grad_values = mixed(solved_along_keys.T, grads_out) + end_weight * product(
        keys, value_memory_state.T
    )
    grad_keys = mixed(along_values.T, solved_low) + end_weight * product(values, value_memory_state)
    grad_keys = (
        grad_keys - mixed(solved_along_keys.T, adjoint_low) - mixed(along_adjoint.T, solved_low)
    )
    grad_keys = grad_keys + end_weight * product(keys, state_gram + state_gram.T)
    return (grad_keys, grad_values)


def split_heads(block, head_dev):
    rows = block.shape[0]
    return block.reshape(rows // SPAN, SPAN, head_dev, DH).transpose(2, 0, 1, 3)


def join_heads(block):
    head_dev, count, size, width = block.shape
    return block.transpose(1, 2, 0, 3).reshape(count * size, head_dev * width).astype(jnp.bfloat16)


def scale_mats(factor, mats):
    return factor[..., None, None] * mats


def shards(queries, keys, values, grads_out, log_decay, ridge):
    gathered = (
        lax.all_to_all(queries, "head", split_axis=1, concat_axis=0, tiled=True),
        lax.all_to_all(keys, "head", split_axis=1, concat_axis=0, tiled=True),
        lax.all_to_all(values, "head", split_axis=1, concat_axis=0, tiled=True),
        lax.all_to_all(grads_out, "head", split_axis=1, concat_axis=0, tiled=True),
    )
    head_dev = log_decay.shape[0]
    query_h = split_heads(gathered[0], head_dev)
    key_h = split_heads(gathered[1], head_dev)
    value_h = split_heads(gathered[2], head_dev)
    grad_h = split_heads(gathered[3], head_dev)
    count = query_h.shape[1]
    gates = log_decay.reshape(head_dev, count, SPAN)
    sums = jnp.sum(gates, axis=2)
    through_local = jnp.cumsum(sums, axis=1)
    starts = jnp.concatenate([jnp.zeros_like(sums[:, :1]), through_local[:, :-1]], axis=1)
    total_log = jnp.sum(sums, axis=1)
    cumul = jnp.cumsum(gates, axis=2)
    key_wide = key_h.astype(jnp.float32)
    scaled_lookup_vectors = jnp.exp(cumul[..., -1:] - cumul)[..., None] * key_wide
    gram_parts = jnp.einsum("hnck,hncl->hnkl", key_wide, scaled_lookup_vectors, precision=highest)
    value_parts = jnp.einsum(
        "hncv,hnck->hnvk", value_h.astype(jnp.float32), scaled_lookup_vectors, precision=highest
    )
    zeros = jnp.zeros((head_dev, DH, DH), jnp.float32)
    gram_carry, value_carry = (zeros, zeros)
    gram_local, value_local = ([], [])
    for block in range(count):
        gram_local.append(gram_carry)
        value_local.append(value_carry)
        decay = jnp.exp(sums[:, block])
        gram_carry = scale_mats(decay, gram_carry) + gram_parts[:, block]
        value_carry = scale_mats(decay, value_carry) + value_parts[:, block]
    position = lax.axis_index("ctx")
    totals = collect(total_log[None], "ctx", 0)
    through = jnp.cumsum(totals, axis=0)
    exclusive = jnp.concatenate([jnp.zeros_like(totals[:1]), through[:-1]], axis=0)
    mine_excl = lax.dynamic_slice_in_dim(exclusive, position, 1, 0)
    mine_through = lax.dynamic_slice_in_dim(through, position, 1, 0)
    piece = side_by_side((gram_carry[None], value_carry[None]), "ctx", 0, 1)
    number = piece[0].shape[0]
    index = jnp.arange(number, dtype=jnp.int32)
    gap = mine_excl - through
    weight = jnp.where((index < position)[:, None], jnp.exp(jnp.minimum(gap, 0.0)), 0.0)
    gram_in = jnp.einsum("jh,jhkl->hkl", weight, piece[0], precision=highest)
    value_in = jnp.einsum("jh,jhkl->hkl", weight, piece[1], precision=highest)
    entry = jnp.exp(starts)
    gram_start = scale_mats(entry, gram_in[:, None]) + jnp.stack(gram_local, axis=1)
    value_start = scale_mats(entry, value_in[:, None]) + jnp.stack(value_local, axis=1)
    solve_blocks = jax.vmap(
        jax.vmap(span_solve, in_axes=(0, 0, 0, 0, 0, 0, 0, None)), in_axes=(0, 0, 0, 0, 0, 0, 0, 0)
    )
    solved, adjoint = solve_blocks(
        gram_start, value_start, query_h, key_h, value_h, grad_h, gates, ridge
    )
    weighted_solved = jnp.exp(cumul)[..., None] * solved
    value_back = jnp.einsum(
        "hncv,hnck->hnvk", grad_h.astype(jnp.float32), weighted_solved, precision=highest
    )
    gram_back = -jnp.einsum("hnck,hncl->hnkl", adjoint, weighted_solved, precision=highest)
    value_delta = jnp.einsum("hn,hnvk->hvk", entry, value_back, precision=highest)
    gram_delta = jnp.einsum("hn,hnvk->hvk", entry, gram_back, precision=highest)
    piece = tuple(
        (
            part.astype(jnp.float32)
            for part in side_by_side(
                (value_delta[None].astype(jnp.bfloat16), gram_delta[None].astype(jnp.bfloat16)),
                "ctx",
                0,
                1,
            )
        )
    )
    number = piece[0].shape[0]
    index = jnp.arange(number, dtype=jnp.int32)
    gap = exclusive - mine_through
    weight = jnp.where((index > position)[:, None], jnp.exp(jnp.minimum(gap, 0.0)), 0.0)
    value_after = zeros + jnp.einsum("jh,jhkl->hkl", weight, piece[0], precision=highest)
    outer_product_suffix = zeros + jnp.einsum("jh,jhkl->hkl", weight, piece[1], precision=highest)
    value_next = [None] * count
    gram_next = [None] * count
    for block in reversed(range(count)):
        value_next[block] = value_after
        gram_next[block] = outer_product_suffix
        decay = jnp.exp(sums[:, block])
        value_after = scale_mats(decay, value_after) + value_back[:, block]
        outer_product_suffix = scale_mats(decay, outer_product_suffix) + gram_back[:, block]
    grad_blocks = jax.vmap(jax.vmap(span_grads))
    grad_keys, grad_values = grad_blocks(
        jnp.stack(value_next, axis=1),
        jnp.stack(gram_next, axis=1),
        key_h,
        value_h,
        grad_h,
        solved,
        adjoint,
        gates,
    )
    results = (
        lax.all_to_all(join_heads(adjoint), "head", split_axis=0, concat_axis=1, tiled=True),
        lax.all_to_all(join_heads(grad_keys), "head", split_axis=0, concat_axis=1, tiled=True),
        lax.all_to_all(join_heads(grad_values), "head", split_axis=0, concat_axis=1, tiled=True),
    )
    return (results[0], results[1], results[2])


def solution(mesh):
    return jax.shard_map(
        shards,
        mesh=mesh,
        in_specs=(
            P(("ctx", "head"), None),
            P(("ctx", "head"), None),
            P(("ctx", "head"), None),
            P(("ctx", "head"), None),
            P("head", "ctx"),
            P("head"),
        ),
        out_specs=(P(("ctx", "head"), None), P(("ctx", "head"), None), P(("ctx", "head"), None)),
        check_vma=False,
    )
```

profile of v0, /device:TPU:1, one launch (start us, length us, event | category | flops | bytes accessed | tf_op | source)
XLA Modules:
  0.0 367.7 jit_solution(8547833972179215033)
XLA Ops:
  9.0 6.0 %all-to-all-start.1 = ((bf16[128,8,256]{2,0,1:T(8,128)(2,1)}), bf16[128,8,256]{2,0,1:T(8,128)(2,1)S(1)}, u32[]{:S(2)}, u32[]{:S(2)}) async-start(bf16[128,8,256]{2,0,1:T(8,128)(2,1)} %bitcast.548), calls=%async_computation.1 | async-start | bytes 1048576 | tf_op jit(solution)/shard_map/all_to_all | solution.py:130
  20.0 4.3 %all-to-all-done.1 = bf16[128,8,256]{2,0,1:T(8,128)(2,1)S(1)} async-done(((bf16[128,8,256]{2,0,1:T(8,128)(2,1)}), bf16[128,8,256]{2,0,1:T(8,128)(2,1)S(1)}, u32[]{:S(2)}, u32[]{:S(2)}) %all-to-all-start.1) | async-done | bytes 524320 | tf_op jit(solution)/shard_map/all_to_all | solution.py:130
  24.3 4.4 %all-to-all-start.2 = ((bf16[128,8,256]{2,0,1:T(8,128)(2,1)}), bf16[128,8,256]{2,0,1:T(8,128)(2,1)S(1)}, u32[]{:S(2)}, u32[]{:S(2)}) async-start(bf16[128,8,256]{2,0,1:T(8,128)(2,1)} %bitcast.547), calls=%async_computation.2 | async-start | bytes 1048576 | tf_op jit(solution)/shard_map/all_to_all | solution.py:131
  30.1 8.0 %all-to-all-done.2 = bf16[128,8,256]{2,0,1:T(8,128)(2,1)S(1)} async-done(((bf16[128,8,256]{2,0,1:T(8,128)(2,1)}), bf16[128,8,256]{2,0,1:T(8,128)(2,1)S(1)}, u32[]{:S(2)}, u32[]{:S(2)}) %all-to-all-start.2) | async-done | bytes 524320 | tf_op jit(solution)/shard_map/all_to_all | solution.py:131
  42.7 7.6 %all-to-all-start = ((f32[16,1,2]{2,1,0:T(1,128)}), f32[16,1,2]{2,1,0:T(1,128)S(1)}, u32[]{:S(2)}, u32[]{:S(2)}) async-start(f32[16,1,2]{2,1,0:T(1,128)} %broadcast_in_dim.31), calls=%async_computation | async-start | bytes 16384 | tf_op jit(solution)/shard_map/all_to_all | solution.py:23
  51.1 5.5 %all-to-all-done = f32[16,1,2]{2,1,0:T(1,128)S(1)} async-done(((f32[16,1,2]{2,1,0:T(1,128)}), f32[16,1,2]{2,1,0:T(1,128)S(1)}, u32[]{:S(2)}, u32[]{:S(2)}) %all-to-all-start) | async-done | bytes 160 | tf_op jit(solution)/shard_map/all_to_all | solution.py:23
  56.6 5.8 %all-to-all-start.3 = ((bf16[128,8,256]{2,0,1:T(8,128)(2,1)}), bf16[128,8,256]{2,0,1:T(8,128)(2,1)S(1)}, u32[]{:S(2)}, u32[]{:S(2)}) async-start(bf16[128,8,256]{2,0,1:T(8,128)(2,1)} %bitcast.546), calls=%async_computation.3 | async-start | bytes 1048576 | tf_op jit(solution)/shard_map/all_to_all | solution.py:132
  63.5 8.3 %all-to-all-done.3 = bf16[128,8,256]{2,0,1:T(8,128)(2,1)S(1)} async-done(((bf16[128,8,256]{2,0,1:T(8,128)(2,1)}), bf16[128,8,256]{2,0,1:T(8,128)(2,1)S(1)}, u32[]{:S(2)}, u32[]{:S(2)}) %all-to-all-start.3) | async-done | bytes 524320 | tf_op jit(solution)/shard_map/all_to_all | solution.py:132
  71.8 4.4 %all-to-all-start.5 = ((bf16[128,8,256]{2,0,1:T(8,128)(2,1)}), bf16[128,8,256]{2,0,1:T(8,128)(2,1)S(1)}, u32[]{:S(2)}, u32[]{:S(2)}) async-start(bf16[128,8,256]{2,0,1:T(8,128)(2,1)} %bitcast.545), calls=%async_computation.5 | async-start | bytes 1048576 | tf_op jit(solution)/shard_map/all_to_all | solution.py:129
  79.5 6.0 %all-to-all-done.5 = bf16[128,8,256]{2,0,1:T(8,128)(2,1)S(1)} async-done(((bf16[128,8,256]{2,0,1:T(8,128)(2,1)}), bf16[128,8,256]{2,0,1:T(8,128)(2,1)S(1)}, u32[]{:S(2)}, u32[]{:S(2)}) %all-to-all-start.5) | async-done | bytes 524320 | tf_op jit(solution)/shard_map/all_to_all | solution.py:129
  86.7 3.9 %multiply_convert_fusion.18 = bf16[2,2,512,512]{3,2,1,0:T(8,128)(2,1)} fusion(f32[2,2,512]{2,1,0:T(2,128)S(1)} %reduce_window_sum.55, pred[512,512]{1,0:T(8,128)(4,1)} %iota_compare_fusion, bf16[2,512,2,128]{1,3,0,2:T(8,128)(2,1)} %copy.407, bf16[2,512,2,128]{3,2,1,0:T(2,128)(2,1)S(1)} %reshape.428), kind=kOutput, calls=%fused_computation.18 | convolution fusion | flops 272629760 | bytes 3416064 | tf_op jit(solution)/shard_map/vmap(vmap())/dot_general | solution.py:49
  90.5 2.8 fusion.12
  101.5 4.1 %multiply_reduce_fusion.28 = (f32[2,2,512]{2,1,0:T(2,128)S(1)}, f32[2,2,512]{2,1,0:T(2,128)S(1)}, f32[2,2,512,128]{2,3,1,0:T(8,128)}) fusion(f32[2,2,512,128]{2,3,1,0:T(8,128)S(1)} %get-tuple-element.59, f32[2]{0:T(128)S(1)} %copy-done.60, f32[2,2,512,128]{2,3,1,0:T(8,128)S(1)} %fusion.232, f32[2,2,512]{2,1,0:T(2,128)S(1)} %get-tuple-element.50, ...), kind=kOutput, calls=%fused_computation.220 | convolution fusion | flops 543420416 | bytes 4489224 | tf_op jit(solution)/shard_map/vmap(vmap())/dot_general | solution.py:49
  110.5 4.3 %multiply_reduce_fusion.26 = (f32[2,2,512]{2,1,0:T(2,128)S(1)}, f32[2,2,512,128]{2,3,1,0:T(8,128)}) fusion(f32[2,2,512,128]{2,3,1,0:T(8,128)S(1)} %multiply_add_fusion.19, f32[2]{0:T(128)S(1)} %copy-done.60, f32[2,2,512,128]{2,3,1,0:T(8,128)} %fusion.230, f32[2,2,512]{2,1,0:T(2,128)S(1)} %get-tuple-element.50, bf16[2,512,2,128]{3,2,1,0:T(2,128)(2,1)S(1)} %reshape.426, ...), kind=kOutput, calls=%fused_computation.215 | convolution fusion | flops 542898176 | bytes 4481032 | tf_op jit(solution)/shard_map/vmap(vmap())/dot_general | solution.py:49
  120.7 4.5 %multiply_reduce_fusion.24 = (f32[2,2,512]{2,1,0:T(2,128)S(1)}, f32[2,2,512,128]{2,3,1,0:T(8,128)}) fusion(f32[2,2,512,128]{2,3,1,0:T(8,128)S(1)} %multiply_add_fusion.17, f32[2]{0:T(128)S(1)} %copy-done.60, f32[2,2,512,128]{2,3,1,0:T(8,128)} %fusion.228, f32[2,2,512]{2,1,0:T(2,128)S(1)} %get-tuple-element.50, bf16[2,512,2,128]{3,2,1,0:T(2,128)(2,1)} %copy-done.17, ...), kind=kOutput, calls=%fused_computation.210 | convolution fusion | flops 542898176 | bytes 4481032 | tf_op jit(solution)/shard_map/vmap(vmap())/dot_general | solution.py:49
  131.9 5.3 %multiply_reduce_fusion.22 = (f32[2,2,512]{2,1,0:T(2,128)S(1)}, f32[2,2,512,128]{2,3,1,0:T(8,128)}) fusion(f32[2,2,512,128]{2,3,1,0:T(8,128)} %copy-done, f32[2]{0:T(128)S(1)} %copy-done.60, f32[2,2,512,128]{2,3,1,0:T(8,128)} %fusion.226, f32[2,2,512]{2,1,0:T(2,128)S(1)} %get-tuple-element.50, bf16[2,512,2,128]{3,2,1,0:T(2,128)(2,1)} %copy-done.17, ...), kind=kOutput, calls=%fused_computation.205 | convolution fusion | flops 542898176 | bytes 4481032 | tf_op jit(solution)/shard_map/vmap(vmap())/dot_general | solution.py:49
  137.2 2.8 multiply_reduce_fusion.21
  144.0 5.2 %multiply_reduce_fusion.20 = (f32[2,2,512]{2,1,0:T(2,128)S(1)}, f32[2,2,512,128]{2,3,1,0:T(8,128)}) fusion(f32[2,2,512,128]{2,3,1,0:T(8,128)} %copy-done.2, f32[2]{0:T(128)S(1)} %copy-done.60, f32[2,2,512,128]{2,3,1,0:T(8,128)} %fusion.224, f32[2,2,512]{2,1,0:T(2,128)S(1)} %get-tuple-element.50, bf16[2,512,2,128]{3,2,1,0:T(2,128)(2,1)} %copy-done.17, ...), kind=kOutput, calls=%fused_computation.200 | convolution fusion | flops 542898176 | bytes 4481032 | tf_op jit(solution)/shard_map/vmap(vmap())/dot_general | solution.py:49
  149.3 2.8 multiply_reduce_fusion.19
  156.3 5.3 %multiply_reduce_fusion.18 = (f32[2,2,512]{2,1,0:T(2,128)S(1)}, f32[2,2,512,128]{2,3,1,0:T(8,128)}) fusion(f32[2,2,512,128]{2,3,1,0:T(8,128)} %copy-done.4, f32[2]{0:T(128)S(1)} %copy-done.60, f32[2,2,512,128]{2,3,1,0:T(8,128)} %fusion.222, f32[2,2,512]{2,1,0:T(2,128)S(1)} %get-tuple-element.50, bf16[2,512,2,128]{3,2,1,0:T(2,128)(2,1)} %copy-done.17, ...), kind=kOutput, calls=%fused_computation.195 | convolution fusion | flops 542898176 | bytes 4481032 | tf_op jit(solution)/shard_map/vmap(vmap())/dot_general | solution.py:49
  161.7 2.8 multiply_reduce_fusion.17
  168.5 5.5 %multiply_reduce_fusion.16 = (f32[2,2,512]{2,1,0:T(2,128)S(1)}, f32[2,2,512,128]{2,3,1,0:T(8,128)}, f32[2,2,512,128]{2,3,1,0:T(8,128)}) fusion(f32[2,2,512,128]{2,3,1,0:T(8,128)} %copy-done.13, f32[2]{0:T(128)S(1)} %copy-done.60, f32[2,2,512,128]{2,3,1,0:T(8,128)} %fusion.220, f32[2,2,512]{2,1,0:T(2,128)S(1)} %get-tuple-element.50, ...), kind=kOutput, calls=%fused_computation.190 | convolution fusion | flops 542898176 | bytes 5529608 | tf_op jit(solution)/shard_map/vmap(vmap())/dot_general | solution.py:49
  175.9 3.3 multiply_add_fusion.7
  179.3 4.4 %fusion.11 = f32[2,2,512,128]{2,3,1,0:T(8,128)} fusion(f32[2,2,512]{2,1,0:T(2,128)S(1)} %copy-done.79, pred[512,512]{1,0:T(8,128)(4,1)} %iota_compare_fusion, bf16[2,512,2,128]{1,3,0,2:T(8,128)(2,1)} %copy.411, f32[2,2,512,128]{2,3,1,0:T(8,128)} %multiply_add_fusion.7, bf16[2,512,2,128]{3,2,1,0:T(2,128)(2,1)} %copy-done.17), kind=kOutput, calls=%fused_computation.41 | convolution fusion | flops 541327360 | bytes 3416064 | tf_op jit(solution)/shard_map/vmap(vmap())/dot_general | solution.py:49
  183.7 3.1 fusion.53
  186.9 4.8 %multiply_add_fusion = f32[2,2,512,128]{2,3,1,0:T(8,128)} fusion(f32[2,2,512,128]{2,3,1,0:T(8,128)} %multiply_add_fusion.7, f32[2,2,512,128]{2,3,1,0:T(8,128)} %copy-done.13, f32[2,2,512,128]{2,3,1,0:T(8,128)} %copy-done.4, f32[2,2,512,128]{2,3,1,0:T(8,128)} %copy-done.2, f32[2,2,512,128]{2,3,1,0:T(8,128)} %copy-done, ...), kind=kLoop, calls=%fused_computation.161 | loop fusion | flops 3932160 | bytes 9502720 | tf_op jit(solution)/shard_map/vmap(vmap())/add | solution.py:76
  193.3 2.8 fusion.13
  201.2 4.0 %fusion.14 = f32[2,2,512,128]{2,3,1,0:T(8,128)} fusion(f32[2,2,512]{2,1,0:T(2,128)} %copy-done.78, pred[512,512]{1,0:T(8,128)(4,1)} %iota_compare_fusion, bf16[2,512,2,128]{1,3,0,2:T(8,128)(2,1)} %copy.411, f32[2,2,512,128]{2,3,1,0:T(8,128)S(1)} %multiply_add_fusion.6, bf16[2,512,2,128]{3,2,1,0:T(2,128)(2,1)S(1)} %copy-done.18), kind=kOutput, calls=%fused_computation.44 | convolution fusion | flops 541327360 | bytes 3416064 | tf_op jit(solution)/shard_map/vmap(vmap())/dot_general | solution.py:49
  211.5 4.2 %fusion.15 = f32[2,2,512,128]{2,3,1,0:T(8,128)} fusion(f32[2,2,512]{2,1,0:T(2,128)} %copy-done.78, pred[512,512]{1,0:T(8,128)(4,1)} %iota_compare_fusion, bf16[2,512,2,128]{1,3,0,2:T(8,128)(2,1)} %copy.411, f32[2,2,512,128]{2,3,1,0:T(8,128)} %multiply_add_fusion.5, bf16[2,512,2,128]{3,2,1,0:T(2,128)(2,1)S(1)} %copy-done.18), kind=kOutput, calls=%fused_computation.45 | convolution fusion | flops 541327360 | bytes 3416064 | tf_op jit(solution)/shard_map/vmap(vmap())/dot_general | solution.py:49
  215.7 3.2 multiply_reduce_fusion.9
  222.6 4.5 %fusion.16 = f32[2,2,512,128]{2,3,1,0:T(8,128)} fusion(f32[2,2,512]{2,1,0:T(2,128)} %copy-done.78, pred[512,512]{1,0:T(8,128)(4,1)} %iota_compare_fusion, bf16[2,512,2,128]{1,3,0,2:T(8,128)(2,1)} %copy.411, f32[2,2,512,128]{2,3,1,0:T(8,128)} %multiply_add_fusion.4, bf16[2,512,2,128]{3,2,1,0:T(2,128)(2,1)S(1)} %copy-done.18), kind=kOutput, calls=%fused_computation.46 | convolution fusion | flops 541327360 | bytes 3416064 | tf_op jit(solution)/shard_map/vmap(vmap())/dot_general | solution.py:49
  227.1 3.2 multiply_reduce_fusion.7
  234.0 4.3 %fusion.17 = f32[2,2,512,128]{2,3,1,0:T(8,128)} fusion(f32[2,2,512]{2,1,0:T(2,128)} %copy-done.78, pred[512,512]{1,0:T(8,128)(4,1)} %iota_compare_fusion, bf16[2,512,2,128]{1,3,0,2:T(8,128)(2,1)} %copy.411, f32[2,2,512,128]{2,3,1,0:T(8,128)} %multiply_add_fusion.3, bf16[2,512,2,128]{3,2,1,0:T(2,128)(2,1)S(1)} %copy-done.18), kind=kOutput, calls=%fused_computation.47 | convolution fusion | flops 541327360 | bytes 3416064 | tf_op jit(solution)/shard_map/vmap(vmap())/dot_general | solution.py:49
  238.3 3.2 multiply_reduce_fusion.5
  245.2 4.3 %fusion.18 = f32[2,2,512,128]{2,3,1,0:T(8,128)} fusion(f32[2,2,512]{2,1,0:T(2,128)} %copy-done.78, pred[512,512]{1,0:T(8,128)(4,1)} %iota_compare_fusion, bf16[2,512,2,128]{1,3,0,2:T(8,128)(2,1)} %copy.411, f32[2,2,512,128]{2,3,1,0:T(8,128)} %multiply_add_fusion.2, bf16[2,512,2,128]{3,2,1,0:T(2,128)(2,1)S(1)} %copy-done.18), kind=kOutput, calls=%fused_computation.48 | convolution fusion | flops 541327360 | bytes 3416064 | tf_op jit(solution)/shard_map/vmap(vmap())/dot_general | solution.py:49
  249.5 3.2 multiply_reduce_fusion.3
  256.3 4.3 %fusion.19 = f32[2,2,512,128]{2,3,1,0:T(8,128)} fusion(f32[2,2,512]{2,1,0:T(2,128)} %copy-done.78, pred[512,512]{1,0:T(8,128)(4,1)} %iota_compare_fusion, bf16[2,512,2,128]{1,3,0,2:T(8,128)(2,1)} %copy.411, f32[2,2,512,128]{2,3,1,0:T(8,128)} %multiply_add_fusion.1, bf16[2,512,2,128]{3,2,1,0:T(2,128)(2,1)S(1)} %copy-done.18), kind=kOutput, calls=%fused_computation.49 | convolution fusion | flops 541327360 | bytes 3416064 | tf_op jit(solution)/shard_map/vmap(vmap())/dot_general | solution.py:49
  260.5 3.3 fusion.54
  264.6 4.4 %broadcast_multiply_fusion = (f32[2,2,512,128]{2,3,1,0:T(8,128)S(1)}, bf16[2,2,512,128]{2,3,1,0:T(8,128)(2,1)}) fusion(f32[2,2,512]{2,1,0:T(2,128)S(1)} %get-tuple-element.50, f32[2,2,512,128]{2,3,1,0:T(8,128)} %multiply_add_fusion.1, f32[2,2,512]{2,1,0:T(2,128)S(1)} %add_divide_fusion, f32[2,2,512,128]{2,3,1,0:T(8,128)} %multiply_add_fusion.2, ...), kind=kLoop, calls=%fused_computation.296 | loop fusion | flops 5767168 | bytes 9519104 | tf_op jit(solution)/shard_map/mul | solution.py:183
  276.3 7.4 %fusion.72 = bf16[2,512,2,128]{1,3,0,2:T(8,128)(2,1)} fusion(f32[2,2,512,128]{2,3,1,0:T(8,128)} %get-tuple-element.72, f32[2,2,512,128]{2,3,1,0:T(8,128)} %fusion.220, f32[2,2,512,128]{2,3,1,0:T(8,128)} %get-tuple-element.71, f32[2,2,512,128]{2,3,1,0:T(8,128)} %fusion.222, f32[2,2,512,128]{2,3,1,0:T(8,128)} %get-tuple-element.69, ...), kind=kLoop, calls=%fused_computation.124 | loop fusion | flops 19398656 | bytes 17432584 | tf_op jit(solution)/shard_map/convert_element_type | solution.py:120
  288.1 5.4 %all-to-all-start.4 = ((bf16[8,128,256]{2,1,0:T(8,128)(2,1)}), bf16[8,128,256]{2,1,0:T(8,128)(2,1)}, u32[]{:S(2)}, u32[]{:S(2)}) async-start(bf16[8,128,256]{2,1,0:T(8,128)(2,1)} %convert_element_type.176), calls=%async_computation.4 | async-start | bytes 1048576 | tf_op jit(solution)/shard_map/all_to_all | solution.py:227
  301.1 3.1 fusion.21
  304.2 14.8 %all-gather.5.cloned.1.call-done = bf16[16,4,128,128]{3,2,1,0:T(8,128)(2,1)} async-done(((bf16[1,4,128,128]{3,2,1,0:T(8,128)(2,1)}), bf16[16,4,128,128]{3,2,1,0:T(8,128)(2,1)}) %all-gather.5.cloned.1.call-update) | async-done | bytes 2097168 | tf_op jit(solution)/shard_map/all_gather | solution.py:36
  322.3 2.9 fusion.29
  329.4 6.5 %all-to-all-start.6 = ((bf16[8,128,256]{2,1,0:T(8,128)(2,1)}), bf16[8,128,256]{2,1,0:T(8,128)(2,1)}, u32[]{:S(2)}, u32[]{:S(2)}) async-start(bf16[8,128,256]{2,1,0:T(8,128)(2,1)} %convert_element_type.202), calls=%async_computation.6 | async-start | bytes 1048576 | tf_op jit(solution)/shard_map/all_to_all | solution.py:228
  339.2 6.2 %all-to-all-done.6 = bf16[8,128,256]{2,1,0:T(8,128)(2,1)} async-done(((bf16[8,128,256]{2,1,0:T(8,128)(2,1)}), bf16[8,128,256]{2,1,0:T(8,128)(2,1)}, u32[]{:S(2)}, u32[]{:S(2)}) %all-to-all-start.6) | async-done | bytes 524320 | tf_op jit(solution)/shard_map/all_to_all | solution.py:228
  345.4 4.4 %all-to-all-start.7 = ((bf16[8,128,256]{2,1,0:T(8,128)(2,1)}), bf16[8,128,256]{2,1,0:T(8,128)(2,1)S(1)}, u32[]{:S(2)}, u32[]{:S(2)}) async-start(bf16[8,128,256]{2,1,0:T(8,128)(2,1)} %convert_element_type.204), calls=%async_computation.7 | async-start | bytes 1048576 | tf_op jit(solution)/shard_map/all_to_all | solution.py:229
  354.4 4.7 %all-to-all-done.7 = bf16[8,128,256]{2,1,0:T(8,128)(2,1)S(1)} async-done(((bf16[8,128,256]{2,1,0:T(8,128)(2,1)}), bf16[8,128,256]{2,1,0:T(8,128)(2,1)S(1)}, u32[]{:S(2)}, u32[]{:S(2)}) %all-to-all-start.7) | async-done | bytes 524320 | tf_op jit(solution)/shard_map/all_to_all | solution.py:229
  (319 shorter events, 122.5 us)
Async XLA Ops:
  9.0 15.3 %all-to-all-start.1 = ((bf16[128,8,256]{2,0,1:T(8,128)(2,1)}), bf16[128,8,256]{2,0,1:T(8,128)(2,1)S(1)}, u32[]{:S(2)}, u32[]{:S(2)}) async-start(bf16[128,8,256]{2,0,1:T(8,128)(2,1)} %bitcast.548), calls=%async_computation.1 | async-start | bytes 1048576 | tf_op jit(solution)/shard_map/all_to_all | solution.py:130
  24.3 13.7 %all-to-all-start.2 = ((bf16[128,8,256]{2,0,1:T(8,128)(2,1)}), bf16[128,8,256]{2,0,1:T(8,128)(2,1)S(1)}, u32[]{:S(2)}, u32[]{:S(2)}) async-start(bf16[128,8,256]{2,0,1:T(8,128)(2,1)} %bitcast.547), calls=%async_computation.2 | async-start | bytes 1048576 | tf_op jit(solution)/shard_map/all_to_all | solution.py:131
  28.7 13.2 %copy-start.77 = (f32[2,1024]{1,0:T(2,128)S(1)}, f32[2,1024]{1,0:T(2,128)}, u32[]{:S(2)}) copy-start(f32[2,1024]{1,0:T(2,128)} %param.10) | copy-start | bytes 24580
  28.7 21.6 %copy-start.51 = (bf16[128,2048]{1,0:T(8,128)(2,1)S(1)}, bf16[128,2048]{1,0:T(8,128)(2,1)}, u32[]{:S(2)}) copy-start(bf16[128,2048]{1,0:T(8,128)(2,1)} %param.9) | copy-start | bytes 1572868
  28.7 65.3 %all-gather.3.cloned.1.call-start = ((), (), s32[]{:S(2)}) async-start(), calls=%async_computation.8 | async-start | bytes 4456448 | tf_op jit(solution)/shard_map/all_gather | solution.py:36
  28.9 139.7 %copy-start.78 = (f32[2,2,512]{2,1,0:T(2,128)}, f32[2,2,512]{2,1,0:T(2,128)S(1)}, u32[]{:S(2)}) copy-start(f32[2,2,512]{2,1,0:T(2,128)S(1)} %reduce_window_sum.55) | copy-start | bytes 24580
  29.3 21.8 %copy-start.83 = (f32[2]{0:T(128)}, f32[2]{0:T(128)S(1)}, u32[]{:S(2)}) copy-start(f32[2]{0:T(128)S(1)} %get-tuple-element.20) | copy-start | bytes 28
  30.1 80.4 %copy-start.17 = (bf16[2,512,2,128]{3,2,1,0:T(2,128)(2,1)}, bf16[2,512,2,128]{3,2,1,0:T(2,128)(2,1)S(1)}, u32[]{:S(2)}) copy-start(bf16[2,512,2,128]{3,2,1,0:T(2,128)(2,1)S(1)} %reshape.426) | copy-start | bytes 1572868
  38.2 38.9 %copy-start.41 = (bf16[2,512,2,128]{3,2,1,0:T(2,128)(2,1)}, bf16[2,512,2,128]{3,2,1,0:T(2,128)(2,1)S(1)}, u32[]{:S(2)}) copy-start(bf16[2,512,2,128]{3,2,1,0:T(2,128)(2,1)S(1)} %reshape.427) | copy-start | bytes 1572868
  38.2 24.4 %copy-start.52 = (bf16[128,2048]{1,0:T(8,128)(2,1)S(1)}, bf16[128,2048]{1,0:T(8,128)(2,1)}, u32[]{:S(2)}) copy-start(bf16[128,2048]{1,0:T(8,128)(2,1)} %param.6) | copy-start | bytes 1572868
  42.7 14.0 %all-to-all-start = ((f32[16,1,2]{2,1,0:T(1,128)}), f32[16,1,2]{2,1,0:T(1,128)S(1)}, u32[]{:S(2)}, u32[]{:S(2)}) async-start(f32[16,1,2]{2,1,0:T(1,128)} %broadcast_in_dim.31), calls=%async_computation | async-start | bytes 16384 | tf_op jit(solution)/shard_map/all_to_all | solution.py:23
  56.6 15.2 %all-to-all-start.3 = ((bf16[128,8,256]{2,0,1:T(8,128)(2,1)}), bf16[128,8,256]{2,0,1:T(8,128)(2,1)S(1)}, u32[]{:S(2)}, u32[]{:S(2)}) async-start(bf16[128,8,256]{2,0,1:T(8,128)(2,1)} %bitcast.546), calls=%async_computation.3 | async-start | bytes 1048576 | tf_op jit(solution)/shard_map/all_to_all | solution.py:132
  71.8 13.7 %all-to-all-start.5 = ((bf16[128,8,256]{2,0,1:T(8,128)(2,1)}), bf16[128,8,256]{2,0,1:T(8,128)(2,1)S(1)}, u32[]{:S(2)}, u32[]{:S(2)}) async-start(bf16[128,8,256]{2,0,1:T(8,128)(2,1)} %bitcast.545), calls=%async_computation.5 | async-start | bytes 1048576 | tf_op jit(solution)/shard_map/all_to_all | solution.py:129
  76.2 242.8 %all-gather.5.cloned.1.call-start = ((), (), s32[]{:S(2)}) async-start(), calls=%async_computation.9 | async-start | bytes 2228224 | tf_op jit(solution)/shard_map/all_gather | solution.py:36
  79.5 17.5 %copy-start.34 = (bf16[2,512,2,128]{3,2,1,0:T(2,128)(2,1)}, bf16[2,512,2,128]{3,2,1,0:T(2,128)(2,1)S(1)}, u32[]{:S(2)}) copy-start(bf16[2,512,2,128]{3,2,1,0:T(2,128)(2,1)S(1)} %reshape.428) | copy-start | bytes 1572868
  86.6 6.8 %copy-start.6 = (bf16[2,512,2,128]{1,3,0,2:T(8,128)(2,1)}, bf16[2,512,2,128]{1,3,0,2:T(8,128)(2,1)S(1)}, u32[]{:S(2)}) copy-start(bf16[2,512,2,128]{1,3,0,2:T(8,128)(2,1)S(1)} %copy.445) | copy-start | bytes 1572868
  152.1 9.6 %copy-start.61 = (f32[2,2,512]{2,1,0:T(2,128)}, f32[2,2,512]{2,1,0:T(2,128)S(1)}, u32[]{:S(2)}) copy-start(f32[2,2,512]{2,1,0:T(2,128)S(1)} %add_divide_fusion.20) | copy-start | bytes 24580
  164.5 9.6 %copy-start.63 = (f32[2,2,512]{2,1,0:T(2,128)}, f32[2,2,512]{2,1,0:T(2,128)S(1)}, u32[]{:S(2)}) copy-start(f32[2,2,512]{2,1,0:T(2,128)S(1)} %add_divide_fusion.18) | copy-start | bytes 24580
  175.9 7.8 %copy-start.65 = (f32[2,2,512]{2,1,0:T(2,128)}, f32[2,2,512]{2,1,0:T(2,128)S(1)}, u32[]{:S(2)}) copy-start(f32[2,2,512]{2,1,0:T(2,128)S(1)} %add_divide_fusion.16) | copy-start | bytes 24580
  215.7 5.7 %copy-start.9 = (f32[2,2,512,128]{2,3,1,0:T(8,128)S(1)}, f32[2,2,512,128]{2,3,1,0:T(8,128)}, u32[]{:S(2)}) copy-start(f32[2,2,512,128]{2,3,1,0:T(8,128)} %multiply_add_fusion.5) | copy-start | bytes 3145732
  227.1 5.7 %copy-start.10 = (f32[2,2,512,128]{2,3,1,0:T(8,128)S(1)}, f32[2,2,512,128]{2,3,1,0:T(8,128)}, u32[]{:S(2)}) copy-start(f32[2,2,512,128]{2,3,1,0:T(8,128)} %multiply_add_fusion.4) | copy-start | bytes 3145732
  238.3 5.7 %copy-start.11 = (f32[2,2,512,128]{2,3,1,0:T(8,128)S(1)}, f32[2,2,512,128]{2,3,1,0:T(8,128)}, u32[]{:S(2)}) copy-start(f32[2,2,512,128]{2,3,1,0:T(8,128)} %multiply_add_fusion.3) | copy-start | bytes 3145732
  249.5 5.4 %copy-start.12 = (f32[2,2,512,128]{2,3,1,0:T(8,128)S(1)}, f32[2,2,512,128]{2,3,1,0:T(8,128)}, u32[]{:S(2)}) copy-start(f32[2,2,512,128]{2,3,1,0:T(8,128)} %multiply_add_fusion.2) | copy-start | bytes 3145732
  249.5 5.4 %copy-start.15 = (f32[2,2,512,128]{2,3,1,0:T(8,128)S(1)}, f32[2,2,512,128]{2,3,1,0:T(8,128)}, u32[]{:S(2)}) copy-start(f32[2,2,512,128]{2,3,1,0:T(8,128)} %copy-done.14) | copy-start | bytes 3145732
  256.2 8.4 %copy-start.70 = (f32[2,2,512]{2,1,0:T(2,128)S(1)}, f32[2,2,512]{2,1,0:T(2,128)}, u32[]{:S(2)}) copy-start(f32[2,2,512]{2,1,0:T(2,128)} %copy-done.69) | copy-start | bytes 24580
  264.6 5.1 %copy-start.28 = (f32[2,2,512,128]{2,3,1,0:T(8,128)S(1)}, f32[2,2,512,128]{2,3,1,0:T(8,128)}, u32[]{:S(2)}) copy-start(f32[2,2,512,128]{2,3,1,0:T(8,128)} %multiply_add_fusion) | copy-start | bytes 3145732
  269.0 7.3 %copy-start.24 = (f32[2,2,512,128]{2,3,1,0:T(8,128)S(1)}, f32[2,2,512,128]{2,3,1,0:T(8,128)}, u32[]{:S(2)}) copy-start(f32[2,2,512,128]{2,3,1,0:T(8,128)} %copy-done.23) | copy-start | bytes 3145732
  269.0 7.3 %copy-start.26 = (f32[2,2,128,512]{3,2,1,0:T(8,128)S(1)}, f32[2,2,128,512]{3,2,1,0:T(8,128)}, u32[]{:S(2)}) copy-start(f32[2,2,128,512]{3,2,1,0:T(8,128)} %copy-done.25) | copy-start | bytes 3145732
  269.0 7.3 %copy-start.62 = (f32[2,2,512]{2,1,0:T(2,128)S(1)}, f32[2,2,512]{2,1,0:T(2,128)}, u32[]{:S(2)}) copy-start(f32[2,2,512]{2,1,0:T(2,128)} %copy-done.61) | copy-start | bytes 24580
  269.0 7.3 %copy-start.64 = (f32[2,2,512]{2,1,0:T(2,128)S(1)}, f32[2,2,512]{2,1,0:T(2,128)}, u32[]{:S(2)}) copy-start(f32[2,2,512]{2,1,0:T(2,128)} %copy-done.63) | copy-start | bytes 24580
  269.0 7.3 %copy-start.66 = (f32[2,2,512]{2,1,0:T(2,128)S(1)}, f32[2,2,512]{2,1,0:T(2,128)}, u32[]{:S(2)}) copy-start(f32[2,2,512]{2,1,0:T(2,128)} %copy-done.65) | copy-start | bytes 24580
  269.0 7.3 %copy-start.68 = (f32[2,2,512]{2,1,0:T(2,128)S(1)}, f32[2,2,512]{2,1,0:T(2,128)}, u32[]{:S(2)}) copy-start(f32[2,2,512]{2,1,0:T(2,128)} %copy-done.67) | copy-start | bytes 24580
  269.7 6.5 %copy-start.43 = (f32[2,2,128,128]{2,3,1,0:T(8,128)}, f32[2,2,128,128]{2,3,1,0:T(8,128)S(1)}, u32[]{:S(2)}) copy-start(f32[2,2,128,128]{2,3,1,0:T(8,128)S(1)} %convolution_bitcast_fusion.6) | copy-start | bytes 786436
  270.9 5.4 %copy-start.45 = (f32[2,2,128,128]{2,3,0,1:T(8,128)}, f32[2,2,128,128]{2,3,0,1:T(8,128)S(1)}, u32[]{:S(2)}) copy-start(f32[2,2,128,128]{2,3,0,1:T(8,128)S(1)} %convolution_negate_fusion) | copy-start | bytes 786436
  276.3 17.2 %copy-start.42 = (bf16[2,2,512,128]{2,3,1,0:T(8,128)(2,1)S(1)}, bf16[2,2,512,128]{2,3,1,0:T(8,128)(2,1)}, u32[]{:S(2)}) copy-start(bf16[2,2,512,128]{2,3,1,0:T(8,128)(2,1)} %get-tuple-element.23) | copy-start | bytes 1572868
  283.7 9.8 %copy-start.38 = (bf16[2,2,512,512]{3,2,1,0:T(8,128)(2,1)S(1)}, bf16[2,2,512,512]{3,2,1,0:T(8,128)(2,1)}, u32[]{:S(2)}) copy-start(bf16[2,2,512,512]{3,2,1,0:T(8,128)(2,1)} %multiply_convert_fusion.18) | copy-start | bytes 6291460
  283.7 11.7 %copy-start.59 = (pred[512,512]{1,0:T(8,128)(4,1)S(1)}, pred[512,512]{1,0:T(8,128)(4,1)}, u32[]{:S(2)}) copy-start(pred[512,512]{1,0:T(8,128)(4,1)} %iota_compare_fusion) | copy-start | bytes 786436
  283.7 11.7 %copy-start.81 = (f32[2,2,512]{2,1,0:T(2,128)S(1)}, f32[2,2,512]{2,1,0:T(2,128)}, u32[]{:S(2)}) copy-start(f32[2,2,512]{2,1,0:T(2,128)} %copy-done.78) | copy-start | bytes 24580
  288.1 41.3 %all-to-all-start.4 = ((bf16[8,128,256]{2,1,0:T(8,128)(2,1)}), bf16[8,128,256]{2,1,0:T(8,128)(2,1)}, u32[]{:S(2)}, u32[]{:S(2)}) async-start(bf16[8,128,256]{2,1,0:T(8,128)(2,1)} %convert_element_type.176), calls=%async_computation.4 | async-start | bytes 1048576 | tf_op jit(solution)/shard_map/all_to_all | solution.py:227
  295.4 5.7 %copy-start.56 = (bf16[2,512,2,128]{1,3,0,2:T(8,128)(2,1)S(1)}, bf16[2,512,2,128]{1,3,0,2:T(8,128)(2,1)}, u32[]{:S(2)}) copy-start(bf16[2,512,2,128]{1,3,0,2:T(8,128)(2,1)} %copy.411) | copy-start | bytes 1572868
  301.1 17.9 %copy-start.82 = (f32[2,16]{0,1:T(8,128)S(1)}, f32[2,16]{0,1:T(8,128)}, u32[]{:S(2)}) copy-start(f32[2,16]{0,1:T(8,128)} %select_bitcast_fusion) | copy-start | bytes 388
  301.1 20.2 %copy-start.44 = (f32[2,2,128,128]{2,3,1,0:T(8,128)S(1)}, f32[2,2,128,128]{2,3,1,0:T(8,128)}, u32[]{:S(2)}) copy-start(f32[2,2,128,128]{2,3,1,0:T(8,128)} %copy-done.43) | copy-start | bytes 786436
  301.1 20.2 %copy-start.46 = (f32[2,2,128,128]{2,3,0,1:T(8,128)S(1)}, f32[2,2,128,128]{2,3,0,1:T(8,128)}, u32[]{:S(2)}) copy-start(f32[2,2,128,128]{2,3,0,1:T(8,128)} %copy-done.45) | copy-start | bytes 786436
  301.1 20.2 %copy-start.84 = (f32[2]{0:T(128)S(1)}, f32[2]{0:T(128)}, u32[]{:S(2)}) copy-start(f32[2]{0:T(128)} %copy-done.83) | copy-start | bytes 28
  322.3 13.7 %copy-start.36 = (bf16[2,512,2,128]{3,2,1,0:T(2,128)(2,1)S(1)}, bf16[2,512,2,128]{3,2,1,0:T(2,128)(2,1)}, u32[]{:S(2)}) copy-start(bf16[2,512,2,128]{3,2,1,0:T(2,128)(2,1)} %copy-done.34) | copy-start | bytes 1572868
  322.3 13.7 %copy-start.40 = (bf16[2,2,512,512]{3,2,1,0:T(8,128)(2,1)S(1)}, bf16[2,2,512,512]{3,2,1,0:T(8,128)(2,1)}, u32[]{:S(2)}) copy-start(bf16[2,2,512,512]{3,2,1,0:T(8,128)(2,1)} %copy-done.39) | copy-start | bytes 6291460
  329.4 16.0 %all-to-all-start.6 = ((bf16[8,128,256]{2,1,0:T(8,128)(2,1)}), bf16[8,128,256]{2,1,0:T(8,128)(2,1)}, u32[]{:S(2)}, u32[]{:S(2)}) async-start(bf16[8,128,256]{2,1,0:T(8,128)(2,1)} %convert_element_type.202), calls=%async_computation.6 | async-start | bytes 1048576 | tf_op jit(solution)/shard_map/all_to_all | solution.py:228
  345.4 13.7 %all-to-all-start.7 = ((bf16[8,128,256]{2,1,0:T(8,128)(2,1)}), bf16[8,128,256]{2,1,0:T(8,128)(2,1)S(1)}, u32[]{:S(2)}, u32[]{:S(2)}) async-start(bf16[8,128,256]{2,1,0:T(8,128)(2,1)} %convert_element_type.204), calls=%async_computation.7 | async-start | bytes 1048576 | tf_op jit(solution)/shard_map/all_to_all | solution.py:229
  (47 other events, 99.8 us)
Sparse Core Ops, SparseCore 0:
  42.0 51.9 all-gather.2
  275.7 43.2 all-gather.4
where the time goes:
time: 374 us; the launch traced here: 368 us
  matrix products  137 us (37%)
  other arithmetic  64.8 us (17%)
  waiting for transfers between devices  58.6 us (16%)
  local copies, waits for them, and re-layouts  46.9 us (13%)
  starting transfers between devices  44.4 us (12%)
  between operations  15.9 us (4%)
    dot_general x23, matrix products, mixed(): return jnp.dot(left, right, preferred_element_type=jnp.float32)  85.6 us
    dot_general x20, matrix products, product(): jnp.dot(left.astype(jnp.float32), right.astype(jnp.float32), precision=hi...  44.1 us
    reduce_sum x14, other arithmetic, conj_grad(): rho_next = jnp.sum(residual * residual, axis=-1, keepdims=True)  24.7 us
    unnamed x174, local copies, waits for them, and re-layouts  19.9 us
    all_gather x2, waiting for transfers between devices, side_by_side(): lax.all_gather(both, axis, axis=dim, tiled=True)  15.5 us
    add x13, other arithmetic, conj_grad(): direction = residual + rho_next / (rho_now + epsilon) * direction  12.2 us
    convert_element_type x6, local copies, waits for them, and re-layouts, join_heads(): block.transpose(1, 2, 0, 3).reshape(count * size, head_dev * width)  9.52 us
    all_to_all x1, waiting for transfers between devices, shards(): lax.all_to_all(grads_out, 'head', split_axis=1, concat_axis=0, tiled=True)  8.28 us
  transfers between devices with their start and end apart: 10, of which 9 were waited for; matrix products, arithmetic and copies ran while one was open for 16% of the time, Pallas kernels for 0%

commit v1 on v0

v1 whole, which is shorter than its diff:
```python
import jax
import jax.numpy as jnp
from jax import lax
from jax.experimental import pallas as pl
from jax.experimental.pallas import tpu as pltpu
from jax.sharding import PartitionSpec as P

DH = 128
SPAN = 512
HALF = SPAN // 2
SOLVE_STEPS = 8
EPSILON = 1e-06

F32 = jnp.float32
BF16 = jnp.bfloat16


def dot(left, right):
    return jnp.dot(left, right, preferred_element_type=F32)


def dot_t(left, right):
    return lax.dot_general(left, right, (((1,), (1,)), ((), ())), preferred_element_type=F32)


def split(value):
    high = value.astype(BF16)
    low = (value - high.astype(F32)).astype(BF16)
    return high, low


def column_of(row):
    return jnp.broadcast_to(row, (DH, row.shape[1])).T


def decay_tile(row, column, start_row, rows, start_col, cols):
    tile = jnp.broadcast_to(row[:, start_col : start_col + cols], (rows, cols))
    wide = jnp.concatenate([column[start_row : start_row + rows]] * (cols // DH), axis=1)
    gap = tile - wide
    if start_row + rows <= start_col:
        return jnp.exp(gap)
    key_pos = start_row + lax.broadcasted_iota(jnp.int32, (rows, cols), 0)
    query_pos = start_col + lax.broadcasted_iota(jnp.int32, (rows, cols), 1)
    return jnp.exp(jnp.where(key_pos <= query_pos, gap, -jnp.inf))


def pack_kernel(a_ref, b_ref, out_ref):
    count = out_ref.shape[0]
    width = a_ref.shape[1] // count
    for j in range(count):
        out_ref[j, :, :width] = a_ref[:, j * width : (j + 1) * width]
        out_ref[j, :, width:] = b_ref[:, j * width : (j + 1) * width]


def pack(a, b, count):
    rows, columns = a.shape
    return pl.pallas_call(
        pack_kernel,
        name="pack",
        out_shape=jax.ShapeDtypeStruct((count, rows, 2 * columns // count), a.dtype),
    )(a, b)


def unpack_kernel(in_ref, a_ref, b_ref):
    count = in_ref.shape[0]
    width = in_ref.shape[2] // 2
    for j in range(count):
        a_ref[:, j * width : (j + 1) * width] = in_ref[j, :, :width]
        b_ref[:, j * width : (j + 1) * width] = in_ref[j, :, width:]


def unpack(packed):
    count, rows, width = packed.shape
    shape = jax.ShapeDtypeStruct((rows, count * width // 2), packed.dtype)
    return pl.pallas_call(unpack_kernel, name="unpack", out_shape=(shape, shape))(packed)


def spread_kernel(in_ref, a_ref):
    count, _, width = in_ref.shape
    for j in range(count):
        a_ref[:, j * width : (j + 1) * width] = in_ref[j]


def spread(packed):
    count, rows, width = packed.shape
    shape = jax.ShapeDtypeStruct((rows, count * width), packed.dtype)
    return pl.pallas_call(spread_kernel, name="spread", out_shape=shape)(packed)


def gram_kernel(key_ref, value_ref, cumul_ref, out_ref, first_ref):
    block = pl.program_id(1)
    keys = key_ref[...]
    row = cumul_ref[0]
    last = row[:, SPAN - 1 :]
    weighted = keys.astype(F32).T * jnp.exp(last - row)
    high, low = split(weighted)
    both = jnp.concatenate([keys, value_ref[...]], axis=1)
    part = dot(high, both) + dot(low, both)
    pieces, piece = out_ref.shape[0], DH // out_ref.shape[0]

    @pl.when(block == 0)
    def _():
        first_ref[0] = part
        out_ref[:, :piece, :] = part.reshape(pieces, piece, 2 * DH)
        out_ref[:, piece:, :] = jnp.broadcast_to(last[None], (pieces, 8, 2 * DH))

    @pl.when(block == 1)
    def _():
        total = jnp.exp(last) * first_ref[0] + part
        out_ref[:, :piece, :] = total.reshape(pieces, piece, 2 * DH)
        out_ref[:, piece:, :] += jnp.broadcast_to(last[None], (pieces, 8, 2 * DH))


def scan_kernel(in_ref, out_ref, total_ref):
    number, piece = out_ref.shape[0], out_ref.shape[1]
    carry = jnp.zeros(out_ref.shape[1:], F32)
    for j in range(number):
        out_ref[j] = carry
        factor = jnp.exp(in_ref[j, piece:, :])
        total_ref[j] = factor
        carry = factor[:1] * carry + in_ref[j, :piece, :]


def scan_back_kernel(in_ref, total_ref, out_ref):
    carry = jnp.zeros(out_ref.shape[1:], F32)
    for j in reversed(range(out_ref.shape[0])):
        out_ref[j] = carry
        carry = total_ref[j, :1, :] * carry + in_ref[j]


def solve_kernel(
    key_ref,
    value_ref,
    query_ref,
    grad_ref,
    cumul_ref,
    ridge_ref,
    state_ref,
    first_ref,
    adjoint_ref,
    solved_ref,
    delta_ref,
    second_ref,
    early,
    late,
    stream,
    keys_t,
    weights,
    solution,
    residual,
    direction,
):
    head, block = pl.program_id(0), pl.program_id(1)
    keys, values, grads = key_ref[...], value_ref[...], grad_ref[...]
    row = cumul_ref[0, pl.ds(block, 1), :]
    first_total = cumul_ref[0, 0:1, SPAN - 1 :]
    column = column_of(row)
    start_decay = jnp.exp(row)
    ridge = ridge_ref[head]

    early[...] = decay_tile(row, column, 0, HALF, 0, HALF)
    late[:HALF] = decay_tile(row, column, HALF, HALF, HALF, HALF)
    late[HALF:] = decay_tile(row, column, 0, HALF, HALF, HALF)

    is_late = block == 1
    entry = jnp.where(is_late, jnp.exp(first_total), 1.0)
    local = jnp.where(is_late, 1.0, 0.0)
    state = entry * state_ref[...] + local * first_ref[0]
    gram_high, gram_low = split(state[:, :DH])
    value_high, value_low = split(state[:, DH:])
    zero = jnp.zeros((HALF, DH), BF16)
    stream[0:HALF] = jnp.concatenate([keys[HALF:], zero], axis=1)
    stream[HALF:SPAN] = jnp.concatenate([keys[:HALF], zero], axis=1)
    stream[SPAN : SPAN + DH] = jnp.concatenate([gram_high, gram_high], axis=1)
    stream[SPAN + DH :] = jnp.concatenate([gram_low, gram_low], axis=1)
    key_t = keys.astype(F32).T.astype(BF16)
    keys_t[:, :HALF] = key_t[:, HALF:]
    keys_t[:, HALF:] = key_t[:, :HALF]

    def starts(which, half, rhs):
        cols = slice(half * HALF, (half + 1) * HALF)
        solution[which, :, cols] = jnp.zeros((DH, HALF), F32)
        residual[which, :, cols] = rhs
        direction[which, :, cols] = rhs
        high, low = split(rhs)
        weights[which, :DH, cols] = high
        weights[which, DH:, cols] = low
        return jnp.sum(rhs * rhs, axis=0, keepdims=True)

    query_t = query_ref[...].astype(F32).T
    value_rows = jnp.concatenate([value_high, value_low], axis=0)
    rhos = [starts(0, half, query_t[:, half * HALF : (half + 1) * HALF]) for half in range(2)]
    for half in range(2):
        cols = slice(half * HALF, (half + 1) * HALF)
        grad_half = grads[cols]
        seen = dot_t(value_rows, grad_half)
        rhs = start_decay[:, cols] * (seen[:DH] + seen[DH:])
        if half == 0:
            masked = (early[...] * dot_t(values[:HALF], grad_half)).astype(BF16)
            rhs = rhs + dot(keys_t[:, HALF:], masked)
        else:
            turned = jnp.concatenate([values[HALF:], values[:HALF]], axis=0)
            masked = (late[...] * dot_t(turned, grad_half)).astype(BF16)
            rhs = rhs + dot(keys_t[...], masked)
        rhos.append(starts(1, half, rhs))

    def sweep(_, rhos):
        later = []
        for which in range(2):
            for half in range(2):
                cols = slice(half * HALF, (half + 1) * HALF)
                rho = rhos[2 * which + half]
                weight = weights[which, :, cols]
                if half == 0:
                    seen = dot(stream[HALF:], weight)
                    scores = (early[...] * seen[:HALF]).astype(BF16)
                    image = dot(keys_t[:, HALF:], scores)
                    gram = seen[HALF : HALF + DH] + seen[HALF + DH :]
                else:
                    seen = dot(stream[...], weight)
                    scores = (late[...] * seen[:SPAN]).astype(BF16)
                    image = dot(keys_t[...], scores)
                    gram = seen[SPAN : SPAN + DH] + seen[SPAN + DH :]
                way = direction[which, :, cols]
                image = image + start_decay[:, cols] * gram + ridge * way
                step = rho / (jnp.sum(way * image, axis=0, keepdims=True) + EPSILON)
                solution[which, :, cols] += step * way
                rest = residual[which, :, cols] - step * image
                residual[which, :, cols] = rest
                rho_next = jnp.sum(rest * rest, axis=0, keepdims=True)
                way = rest + rho_next / (rho + EPSILON) * way
                direction[which, :, cols] = way
                high, low = split(way)
                weights[which, :DH, cols] = high
                weights[which, DH:, cols] = low
                later.append(rho_next)
        return tuple(later)

    lax.fori_loop(0, SOLVE_STEPS, sweep, tuple(rhos))

    solved_t = solution[0]
    adjoint = solution[1].T.astype(BF16)
    adjoint_ref[...] = adjoint
    solved_ref[...] = solved_t.T.astype(BF16)
    high, low = split(start_decay * solved_t)
    both = jnp.concatenate([grads, -adjoint], axis=1)
    back = dot(high, both) + dot(low, both)

    @pl.when(block == 0)
    def _():
        delta_ref[...] = back

    @pl.when(block == 1)
    def _():
        delta_ref[...] += jnp.exp(first_total) * back
        second_ref[0] = back


def local_kernel(key_ref, value_ref, grad_ref, solved_ref, adjoint_ref, cumul_ref, key_out, value_out):
    block = pl.program_id(1)
    keys, values, grads = key_ref[...], value_ref[...], grad_ref[...]
    solved, adjoint = solved_ref[...], adjoint_ref[...]
    row = cumul_ref[0, pl.ds(block, 1), :]
    column = column_of(row)
    left = jnp.concatenate([values, keys], axis=1)
    right = jnp.concatenate([grads, -adjoint], axis=1)
    both = jnp.concatenate([grads, adjoint], axis=1)
    for half in range(2):
        mine = slice(half * HALF, (half + 1) * HALF)
        after = slice(half * HALF, SPAN)
        within = decay_tile(row, column, half * HALF, HALF, half * HALF, SPAN - half * HALF)
        along_solved = (within * dot_t(keys[mine], solved[after])).astype(BF16)
        along = (within * dot_t(left[mine], right[after])).astype(BF16)
        seen = dot(along_solved, both[after])
        value_out[mine] = seen[:, :DH]
        key_out[mine] = dot(along, solved[after]) - seen[:, DH:]


def final_kernel(key_ref, value_ref, state_ref, second_ref, cumul_ref, key_local, value_local, out_ref):
    block, head = pl.program_id(0), pl.program_id(1)
    row = cumul_ref[0, pl.ds(block, 1), :]
    last = cumul_ref[0, 1:2, SPAN - 1 :]
    weight = column_of(jnp.exp(row[:, SPAN - 1 :] - row))
    is_early = block == 0
    entry = jnp.where(is_early, jnp.exp(last), 1.0)
    local = jnp.where(is_early, 1.0, 0.0)
    state = entry * state_ref[...] + local * second_ref[0]
    value_t, gram = state[:, :DH], state[:, DH:]
    upper = jnp.concatenate([value_t, gram + gram.T], axis=1)
    lower = jnp.concatenate([jnp.zeros((DH, DH), F32), value_t.T], axis=1)
    high, low = split(jnp.concatenate([upper, lower], axis=0))
    both = jnp.concatenate([key_ref[...], value_ref[...]], axis=1)
    seen = dot(both, high) + dot(both, low)
    key_part = (key_local[...] + weight * seen[:, DH:]).astype(BF16)
    value_part = (value_local[...] + weight * seen[:, :DH]).astype(BF16)

    @pl.when(head == 0)
    def _():
        out_ref[:, :DH] = key_part
        out_ref[:, 2 * DH : 3 * DH] = value_part

    @pl.when(head == 1)
    def _():
        out_ref[:, DH : 2 * DH] = key_part
        out_ref[:, 3 * DH :] = value_part


def swap(pieces, axis):
    return lax.all_to_all(pieces, axis, split_axis=0, concat_axis=0, tiled=True)


def shards(queries, keys, values, grads_out, log_decay, ridge):
    heads = lax.axis_size("head")
    number = lax.axis_size("ctx")
    head_dev = log_decay.shape[0]
    tokens = log_decay.shape[1]
    count = tokens // SPAN
    piece = head_dev * DH // number
    grid = (head_dev, count)
    params = pltpu.CompilerParams(dimension_semantics=("arbitrary", "arbitrary"))

    first = swap(pack(keys, values, heads), "head").reshape(tokens, 2 * head_dev * DH)
    second = swap(pack(queries, grads_out, heads), "head").reshape(tokens, 2 * head_dev * DH)
    cumul = jnp.cumsum(log_decay.reshape(head_dev, count, SPAN), axis=2)

    low_spec = pl.BlockSpec((SPAN, DH), lambda h, b: (b, h))
    high_spec = pl.BlockSpec((SPAN, DH), lambda h, b: (b, head_dev + h))
    cumul_spec = pl.BlockSpec((1, count, SPAN), lambda h, b: (h, 0, 0))
    state_spec = pl.BlockSpec((DH, 2 * DH), lambda h, b: (h, 0))
    local_spec = pl.BlockSpec((1, DH, 2 * DH), lambda h, b: (h, 0, 0))
    state_shape = jax.ShapeDtypeStruct((head_dev * DH, 2 * DH), F32)
    local_shape = jax.ShapeDtypeStruct((head_dev, DH, 2 * DH), F32)

    out, first_state = pl.pallas_call(
        gram_kernel,
        name="gram",
        grid=grid,
        in_specs=[
            low_spec,
            high_spec,
            pl.BlockSpec((1, 1, SPAN), lambda h, b: (h * count + b, 0, 0)),
        ],
        out_specs=[
            pl.BlockSpec((number // head_dev, piece + 8, 2 * DH), lambda h, b: (h, 0, 0)),
            local_spec,
        ],
        out_shape=[jax.ShapeDtypeStruct((number, piece + 8, 2 * DH), F32), local_shape],
        compiler_params=params,
    )(first, first, cumul.reshape(head_dev * count, 1, SPAN))
    prefix, factors = pl.pallas_call(
        scan_kernel,
        name="scan",
        out_shape=(
            jax.ShapeDtypeStruct((number, piece, 2 * DH), F32),
            jax.ShapeDtypeStruct((number, 8, 2 * DH), F32),
        ),
    )(swap(out, "ctx"))
    state = swap(prefix, "ctx").reshape(head_dev * DH, 2 * DH)

    adjoint, solved, delta, second_state = pl.pallas_call(
        solve_kernel,
        name="solve",
        grid=grid,
        in_specs=[
            low_spec,
            high_spec,
            low_spec,
            high_spec,
            cumul_spec,
            pl.BlockSpec(memory_space=pltpu.SMEM),
            state_spec,
            local_spec,
        ],
        out_specs=[low_spec, low_spec, state_spec, local_spec],
        out_shape=[
            jax.ShapeDtypeStruct((tokens, head_dev * DH), BF16),
            jax.ShapeDtypeStruct((tokens, head_dev * DH), BF16),
            state_shape,
            local_shape,
        ],
        scratch_shapes=[
            pltpu.VMEM((HALF, HALF), F32),
            pltpu.VMEM((SPAN, HALF), F32),
            pltpu.VMEM((SPAN + 2 * DH, 2 * DH), BF16),
            pltpu.VMEM((DH, SPAN), BF16),
            pltpu.VMEM((2, 2 * DH, SPAN), BF16),
            pltpu.VMEM((2, DH, SPAN), F32),
            pltpu.VMEM((2, DH, SPAN), F32),
            pltpu.VMEM((2, DH, SPAN), F32),
        ],
        compiler_params=params,
    )(first, first, second, second, cumul, ridge, state, first_state)

    grad_queries = spread(swap(adjoint.reshape(heads, tokens // heads, head_dev * DH), "head"))

    key_local, value_local = pl.pallas_call(
        local_kernel,
        name="local",
        grid=grid,
        in_specs=[low_spec, high_spec, high_spec, low_spec, low_spec, cumul_spec],
        out_specs=[low_spec, low_spec],
        out_shape=[jax.ShapeDtypeStruct((tokens, head_dev * DH), F32)] * 2,
        compiler_params=params,
    )(first, first, second, solved, adjoint, cumul)

    suffix = pl.pallas_call(
        scan_back_kernel,
        name="scan_back",
        out_shape=jax.ShapeDtypeStruct((number, piece, 2 * DH), F32),
    )(swap(delta.reshape(number, piece, 2 * DH), "ctx"), factors)
    state_after = swap(suffix, "ctx").reshape(head_dev * DH, 2 * DH)

    def turned(spec):
        return pl.BlockSpec(spec.block_shape, lambda b, h: spec.index_map(h, b))

    grads = pl.pallas_call(
        final_kernel,
        name="final",
        grid=(count, head_dev),
        in_specs=[
            turned(spec)
            for spec in (
                low_spec,
                high_spec,
                state_spec,
                local_spec,
                cumul_spec,
                low_spec,
                low_spec,
            )
        ],
        out_specs=pl.BlockSpec((SPAN, 2 * head_dev * DH), lambda b, h: (b, 0)),
        out_shape=jax.ShapeDtypeStruct((tokens, 2 * head_dev * DH), BF16),
        compiler_params=params,
    )(first, first, state_after, second_state, cumul, key_local, value_local)
    grads = swap(grads.reshape(heads, tokens // heads, 2 * head_dev * DH), "head")
    grad_keys, grad_values = unpack(grads)
    return (grad_queries, grad_keys, grad_values)


def solution(mesh):
    return jax.shard_map(
        shards,
        mesh=mesh,
        in_specs=(
            P(("ctx", "head"), None),
            P(("ctx", "head"), None),
            P(("ctx", "head"), None),
            P(("ctx", "head"), None),
            P("head", "ctx"),
            P("head"),
        ),
        out_specs=(P(("ctx", "head"), None), P(("ctx", "head"), None), P(("ctx", "head"), None)),
        check_vma=False,
    )
```

time: 374 us -> 193 us (0.52); the launches traced: 368 us -> 191 us
  matrix products: 137 us -> 0 us
  Pallas kernels: 0 us -> 72 us
  other arithmetic: 64.8 us -> 2.24 us
  local copies, waits for them, and re-layouts: 46.9 us -> 4.99 us
  blocking collectives: 0 us -> 23.5 us
  between operations: 15.9 us -> 0.68 us
  starting transfers between devices: 44.4 us -> 35.5 us
  waiting for transfers between devices: 58.6 us -> 52.4 us
    dot_general x49 -> x0, matrix products: 137 us -> none  [the longest x23 85.6 us: mixed(): return jnp.dot(left, right, preferred_element_type=jnp.float32)]
    pallas_call x0 -> x10, Pallas kernels: none -> 72 us  [the longest x1 44.8 us: shards(): pl.pallas_call(solve_kernel, name='solve', grid=grid, in_specs=[low_spec,...]
    reduce_sum x16 -> x0, other arithmetic: 24.9 us -> none  [the longest x14 24.7 us: conj_grad(): rho_next = jnp.sum(residual * residual, axis=-1, keepdims=True)]
    all_to_all x0 -> x2, blocking collectives: none -> 23.5 us  [swap(): return lax.all_to_all(pieces, axis, split_axis=0, concat_axis=0, tiled=True)]
    add x17 -> x0, other arithmetic: 17.2 us -> none  [the longest x13 12.2 us: conj_grad(): direction = residual + rho_next / (rho_now + epsilon) * direction]
    unnamed x174 -> x16, local copies, waits for them, and re-layouts: 19.9 us -> 4.2 us
    all_gather x2 -> x0, waiting for transfers between devices: 15.5 us -> none  [side_by_side(): lax.all_gather(both, axis, axis=dim, tiled=True)]
    convert_element_type x6 -> x0, local copies, waits for them, and re-layouts: 9.52 us -> none  [join_heads(): block.transpose(1, 2, 0, 3).reshape(count * size, head_dev * width)]
  transfers between devices with their start and end apart: 10 -> 6, of which waited for: 9 -> 5; matrix products, arithmetic and copies ran while one was open for 16% -> 2% of each run, Pallas kernels for 0% -> 9%
where the time goes in v1:
time: 193 us; the launch traced here: 191 us
  Pallas kernels  72 us (37%)
  waiting for transfers between devices  52.4 us (27%)
  starting transfers between devices  35.5 us (18%)
  blocking collectives  23.5 us (12%)
  local copies, waits for them, and re-layouts  4.99 us (3%)
  other arithmetic  2.24 us (1%)
    all_to_all x6, waiting for transfers between devices, swap(): return lax.all_to_all(pieces, axis, split_axis=0, concat_axis=0, tiled=True)  52.4 us
    pallas_call x1, Pallas kernels, shards(): pl.pallas_call(solve_kernel, name='solve', grid=grid, in_specs=[low_spec,...  44.8 us
    all_to_all x6, starting transfers between devices, swap(): return lax.all_to_all(pieces, axis, split_axis=0, concat_axis=0, tiled=True)  35.5 us
    all_to_all x2, blocking collectives, swap(): return lax.all_to_all(pieces, axis, split_axis=0, concat_axis=0, tiled=True)  23.5 us
    pallas_call x1, Pallas kernels, shards(): pl.pallas_call(local_kernel, name='local', grid=grid, in_specs=[low_spec,...  5.44 us
    pallas_call x1, Pallas kernels, shards(): pl.pallas_call(final_kernel, name='final', grid=(count, head_dev), in_spe...  5.31 us
    pallas_call x2, Pallas kernels, pack(): pl.pallas_call(pack_kernel, name='pack', out_shape=jax.ShapeDtypeStruct((...  4.53 us
    unnamed x16, local copies, waits for them, and re-layouts  4.2 us
  transfers between devices with their start and end apart: 6, of which 5 were waited for; matrix products, arithmetic and copies ran while one was open for 2% of the time, Pallas kernels for 9%

profile of v1, /device:TPU:1, one launch (start us, length us, event | category | flops | bytes accessed | tf_op | source)
XLA Modules:
  0.0 191.3 jit_solution(13075154667461705262)
XLA Ops:
  0.6 2.3 %pack.2 = bf16[8,128,512]{2,1,0:T(8,128)(2,1)} custom-call(bf16[128,2048]{1,0:T(8,128)(2,1)} %a_ref.2, bf16[128,2048]{1,0:T(8,128)(2,1)} %b_ref.2), custom_call_target="tpu_custom_call" | custom-call | tf_op jit(solution)/shard_map/pack/pallas_call | solution.py:57
  2.9 0.0 copy-start.7
  2.9 6.1 %all-to-all-start = ((bf16[8,128,512]{2,1,0:T(8,128)(2,1)}), bf16[8,128,512]{2,1,0:T(8,128)(2,1)S(1)}, u32[]{:S(2)}, u32[]{:S(2)}) async-start(bf16[8,128,512]{2,1,0:T(8,128)(2,1)} %pack.2), calls=%async_computation | async-start | bytes 2097152 | tf_op jit(solution)/shard_map/all_to_all | solution.py:309
  9.0 0.0 copy-done.7
  9.0 1.2 reduce-window.6
  10.2 0.2 slice_reduce_fusion
  10.4 0.3 reduce-window.9
  10.7 0.7 broadcast_add_fusion
  11.4 12.5 %all-to-all-done = bf16[8,128,512]{2,1,0:T(8,128)(2,1)S(1)} async-done(((bf16[8,128,512]{2,1,0:T(8,128)(2,1)}), bf16[8,128,512]{2,1,0:T(8,128)(2,1)S(1)}, u32[]{:S(2)}, u32[]{:S(2)}) %all-to-all-start) | async-done | bytes 1048608 | tf_op jit(solution)/shard_map/all_to_all | solution.py:309
  23.9 0.0 copy-start
  24.0 1.0 copy-done
  24.9 4.2 %gram.1 = (f32[16,24,256]{2,1,0:T(8,128)}, f32[2,128,256]{2,1,0:T(8,128)}) custom-call(bf16[1024,512]{1,0:T(8,128)(2,1)} %bitcast.9, bf16[1024,512]{1,0:T(8,128)(2,1)} %bitcast.10, f32[4,1,512]{2,1,0:T(1,128)} %bitcast.24), custom_call_target="tpu_custom_call" | custom-call | tf_op jit(solution)/shard_map/gram/pallas_call | solution.py:334
  29.1 7.6 %all-to-all-start.2 = ((f32[16,24,256]{2,1,0:T(8,128)}), f32[16,24,256]{2,1,0:T(8,128)S(1)}, u32[]{:S(2)}, u32[]{:S(2)}) async-start(f32[16,24,256]{2,1,0:T(8,128)} %get-tuple-element.15), calls=%async_computation.2 | async-start | bytes 786432 | tf_op jit(solution)/shard_map/all_to_all | solution.py:309
  36.7 2.3 %pack.3 = bf16[8,128,512]{2,1,0:T(8,128)(2,1)} custom-call(bf16[128,2048]{1,0:T(8,128)(2,1)} %a_ref.3, bf16[128,2048]{1,0:T(8,128)(2,1)} %b_ref.3), custom_call_target="tpu_custom_call" | custom-call | tf_op jit(solution)/shard_map/pack/pallas_call | solution.py:57
  39.0 6.7 %all-to-all-done.2.in_ref = f32[16,24,256]{2,1,0:T(8,128)S(1)} async-done(((f32[16,24,256]{2,1,0:T(8,128)}), f32[16,24,256]{2,1,0:T(8,128)S(1)}, u32[]{:S(2)}, u32[]{:S(2)}) %all-to-all-start.2) | async-done | bytes 393248 | tf_op jit(solution)/shard_map/all_to_all | solution.py:309
  45.7 0.0 copy-start.4
  45.7 0.7 copy-done.4
  46.4 5.6 %all-to-all-start.1 = ((bf16[8,128,512]{2,1,0:T(8,128)(2,1)}), bf16[8,128,512]{2,1,0:T(8,128)(2,1)S(1)}, u32[]{:S(2)}, u32[]{:S(2)}) async-start(bf16[8,128,512]{2,1,0:T(8,128)(2,1)} %pack.3), calls=%async_computation.1 | async-start | bytes 2097152 | tf_op jit(solution)/shard_map/all_to_all | solution.py:309
  52.0 1.8 scan.1
  53.7 13.2 %all-to-all-done.1 = bf16[8,128,512]{2,1,0:T(8,128)(2,1)S(1)} async-done(((bf16[8,128,512]{2,1,0:T(8,128)(2,1)}), bf16[8,128,512]{2,1,0:T(8,128)(2,1)S(1)}, u32[]{:S(2)}, u32[]{:S(2)}) %all-to-all-start.1) | async-done | bytes 1048608 | tf_op jit(solution)/shard_map/all_to_all | solution.py:309
  67.0 0.0 copy-start.1
  67.0 0.0 copy-start.6
  67.0 3.7 %all-to-all-start.3 = ((f32[16,16,256]{2,1,0:T(8,128)}), f32[16,16,256]{2,1,0:T(8,128)S(1)}, u32[]{:S(2)}, u32[]{:S(2)}) async-start(f32[16,16,256]{2,1,0:T(8,128)} %get-tuple-element.16), calls=%async_computation.3 | async-start | bytes 524288 | tf_op jit(solution)/shard_map/all_to_all | solution.py:309
  70.6 0.0 copy-done.6
  70.6 0.6 reduce_window_sum.26.cumul_ref
  71.3 6.9 %all-to-all-done.3 = f32[16,16,256]{2,1,0:T(8,128)S(1)} async-done(((f32[16,16,256]{2,1,0:T(8,128)}), f32[16,16,256]{2,1,0:T(8,128)S(1)}, u32[]{:S(2)}, u32[]{:S(2)}) %all-to-all-start.3) | async-done | bytes 262176 | tf_op jit(solution)/shard_map/all_to_all | solution.py:309
  78.1 0.0 copy-start.5
  78.2 0.0 copy-done.1
  78.2 0.7 copy-done.5
  78.9 44.8 %solve.1 = (bf16[1024,256]{1,0:T(8,128)(2,1)}, bf16[1024,256]{1,0:T(8,128)(2,1)}, f32[256,256]{1,0:T(8,128)}, f32[2,128,256]{2,1,0:T(8,128)}) custom-call(bf16[1024,512]{1,0:T(8,128)(2,1)} %bitcast.11, bf16[1024,512]{1,0:T(8,128)(2,1)} %bitcast.12, bf16[1024,512]{1,0:T(8,128)(2,1)} %bitcast.17, bf16[1024,512]{1,0:T(8,128)(2,1)} %bitcast.18, ...), custom_call_target="tpu_custom_call" | custom-call | tf_op jit(solution)/shard_map/solve/pallas_call | solution.py:360
  123.7 11.7 %all_to_all.40.in_ref = f32[16,16,256]{2,1,0:T(8,128)} all-to-all(f32[16,16,256]{2,1,0:T(8,128)} %bitcast.23), channel_id=1, replica_groups=mesh['ctx'=16,'head'=8] {'ctx'}, dimensions={0} | all-to-all | bytes 524288 | tf_op jit(solution)/shard_map/all_to_all | solution.py:309
  135.4 1.7 scan_back.1
  137.1 11.7 %all_to_all.41 = f32[16,16,256]{2,1,0:T(8,128)} all-to-all(f32[16,16,256]{2,1,0:T(8,128)} %scan_back.1), channel_id=1, replica_groups=mesh['ctx'=16,'head'=8] {'ctx'}, dimensions={0} | all-to-all | bytes 524288 | tf_op jit(solution)/shard_map/all_to_all | solution.py:309
  148.9 7.8 %all-to-all-start.4 = ((bf16[8,128,256]{2,1,0:T(8,128)(2,1)}), bf16[8,128,256]{2,1,0:T(8,128)(2,1)S(1)}, u32[]{:S(2)}, u32[]{:S(2)}) async-start(bf16[8,128,256]{2,1,0:T(8,128)(2,1)} %bitcast.4), calls=%async_computation.4 | async-start | bytes 1048576 | tf_op jit(solution)/shard_map/all_to_all | solution.py:309
  156.7 5.4 %local.1 = (f32[1024,256]{1,0:T(8,128)}, f32[1024,256]{1,0:T(8,128)}) custom-call(bf16[1024,512]{1,0:T(8,128)(2,1)} %bitcast.13, bf16[1024,512]{1,0:T(8,128)(2,1)} %bitcast.14, bf16[1024,512]{1,0:T(8,128)(2,1)} %bitcast.19, bf16[1024,256]{1,0:T(8,128)(2,1)} %get-tuple-element.22.solved_ref, bf16[1024,256]{1,0:T(8,128)(2,1)} %get-tuple-element.18.adjoint_ref, ...), custom_call_target="tpu_custom_call" | custom-call | tf_op jit(solution)/shard_map/local/pallas_call | solution.py:396
  162.1 5.3 %final.1 = bf16[1024,512]{1,0:T(8,128)(2,1)} custom-call(bf16[1024,512]{1,0:T(8,128)(2,1)} %bitcast.15, bf16[1024,512]{1,0:T(8,128)(2,1)} %bitcast.16, f32[256,256]{1,0:T(8,128)} %bitcast.22, f32[2,128,256]{2,1,0:T(8,128)} %get-tuple-element.21.second_ref, f32[2,2,512]{2,1,0:T(2,128)} %reduce_window_sum.26.cumul_ref, ...), custom_call_target="tpu_custom_call" | custom-call | tf_op jit(solution)/shard_map/final/pallas_call | solution.py:416
  167.4 0.0 all-to-all-done.4.in_ref
  167.4 0.0 copy-start.3
  167.4 0.8 copy-done.3
  168.2 4.8 %all-to-all-start.7 = ((bf16[8,128,512]{2,1,0:T(8,128)(2,1)}), bf16[8,128,512]{2,1,0:T(8,128)(2,1)S(1)}, u32[]{:S(2)}, u32[]{:S(2)}) async-start(bf16[8,128,512]{2,1,0:T(8,128)(2,1)} %bitcast.20), calls=%async_computation.7 | async-start | bytes 2097152 | tf_op jit(solution)/shard_map/all_to_all | solution.py:309
  173.0 1.9 spread.1
  174.9 13.1 %all-to-all-done.7.in_ref = bf16[8,128,512]{2,1,0:T(8,128)(2,1)S(1)} async-done(((bf16[8,128,512]{2,1,0:T(8,128)(2,1)}), bf16[8,128,512]{2,1,0:T(8,128)(2,1)S(1)}, u32[]{:S(2)}, u32[]{:S(2)}) %all-to-all-start.7) | async-done | bytes 1048608 | tf_op jit(solution)/shard_map/all_to_all | solution.py:309
  188.0 0.0 copy-start.2
  188.0 1.0 copy-done.2
  189.0 2.3 %unpack.1 = (bf16[128,2048]{1,0:T(8,128)(2,1)}, bf16[128,2048]{1,0:T(8,128)(2,1)}) custom-call(bf16[8,128,512]{2,1,0:T(8,128)(2,1)} %copy-done.2), custom_call_target="tpu_custom_call" | custom-call | tf_op jit(solution)/shard_map/unpack/pallas_call | solution.py:75
  (1 shorter events, 0.0 us)
Async XLA Ops:
  2.9 6.1 %copy-start.7 = (f32[2,1024]{1,0:T(2,128)S(1)}, f32[2,1024]{1,0:T(2,128)}, u32[]{:S(2)}) copy-start(f32[2,1024]{1,0:T(2,128)} %param.10) | copy-start | bytes 24580
  2.9 21.1 %all-to-all-start = ((bf16[8,128,512]{2,1,0:T(8,128)(2,1)}), bf16[8,128,512]{2,1,0:T(8,128)(2,1)S(1)}, u32[]{:S(2)}, u32[]{:S(2)}) async-start(bf16[8,128,512]{2,1,0:T(8,128)(2,1)} %pack.2), calls=%async_computation | async-start | bytes 2097152 | tf_op jit(solution)/shard_map/all_to_all | solution.py:309
  23.9 1.0 copy-start
  29.1 16.5 %all-to-all-start.2 = ((f32[16,24,256]{2,1,0:T(8,128)}), f32[16,24,256]{2,1,0:T(8,128)S(1)}, u32[]{:S(2)}, u32[]{:S(2)}) async-start(f32[16,24,256]{2,1,0:T(8,128)} %get-tuple-element.15), calls=%async_computation.2 | async-start | bytes 786432 | tf_op jit(solution)/shard_map/all_to_all | solution.py:309
  45.7 0.7 copy-start.4
  46.4 20.6 %all-to-all-start.1 = ((bf16[8,128,512]{2,1,0:T(8,128)(2,1)}), bf16[8,128,512]{2,1,0:T(8,128)(2,1)S(1)}, u32[]{:S(2)}, u32[]{:S(2)}) async-start(bf16[8,128,512]{2,1,0:T(8,128)(2,1)} %pack.3), calls=%async_computation.1 | async-start | bytes 2097152 | tf_op jit(solution)/shard_map/all_to_all | solution.py:309
  67.0 11.2 %copy-start.1 = (bf16[8,128,512]{2,1,0:T(8,128)(2,1)}, bf16[8,128,512]{2,1,0:T(8,128)(2,1)S(1)}, u32[]{:S(2)}) copy-start(bf16[8,128,512]{2,1,0:T(8,128)(2,1)S(1)} %all-to-all-done.1) | copy-start | bytes 3145732
  67.0 3.7 %copy-start.6 = (f32[2,2,4,128]{3,2,1,0:T(4,128)S(1)}, f32[2,2,4,128]{3,2,1,0:T(4,128)}, u32[]{:S(2)}) copy-start(f32[2,2,4,128]{3,2,1,0:T(4,128)} %broadcast_add_fusion) | copy-start | bytes 24580
  67.0 11.2 %all-to-all-start.3 = ((f32[16,16,256]{2,1,0:T(8,128)}), f32[16,16,256]{2,1,0:T(8,128)S(1)}, u32[]{:S(2)}, u32[]{:S(2)}) async-start(f32[16,16,256]{2,1,0:T(8,128)} %get-tuple-element.16), calls=%async_computation.3 | async-start | bytes 524288 | tf_op jit(solution)/shard_map/all_to_all | solution.py:309
  78.1 0.7 copy-start.5
  148.9 18.6 %all-to-all-start.4 = ((bf16[8,128,256]{2,1,0:T(8,128)(2,1)}), bf16[8,128,256]{2,1,0:T(8,128)(2,1)S(1)}, u32[]{:S(2)}, u32[]{:S(2)}) async-start(bf16[8,128,256]{2,1,0:T(8,128)(2,1)} %bitcast.4), calls=%async_computation.4 | async-start | bytes 1048576 | tf_op jit(solution)/shard_map/all_to_all | solution.py:309
  167.4 0.8 copy-start.3
  168.2 19.8 %all-to-all-start.7 = ((bf16[8,128,512]{2,1,0:T(8,128)(2,1)}), bf16[8,128,512]{2,1,0:T(8,128)(2,1)S(1)}, u32[]{:S(2)}, u32[]{:S(2)}) async-start(bf16[8,128,512]{2,1,0:T(8,128)(2,1)} %bitcast.20), calls=%async_computation.7 | async-start | bytes 2097152 | tf_op jit(solution)/shard_map/all_to_all | solution.py:309
  188.0 1.0 copy-start.2

commit v2 on v1

--- a/solution.py
+++ b/solution.py
@@ -5,14 +5,27 @@
 from jax.experimental.pallas import tpu as pltpu
 from jax.sharding import PartitionSpec as P
 
+
 DH = 128
 SPAN = 512
 HALF = SPAN // 2
 SOLVE_STEPS = 8
 EPSILON = 1e-06
 
+
 F32 = jnp.float32
 BF16 = jnp.bfloat16
+
+
+MIB = 1 << 20
+
+
+def grant(mib, **options):
+    return pltpu.CompilerParams(vmem_limit_bytes=mib * MIB, **options)
+
+
+def in_hbm(array):
+    return pltpu.with_memory_space_constraint(array, pltpu.HBM)
 
 
 def dot(left, right):
@@ -61,6 +74,50 @@
     )(a, b)
 
 
+def parts_kernel(own_ref, a_ref, b_ref, *outs):
+    width = a_ref.shape[1] // len(outs)
+    for d, out_ref in enumerate(outs):
+        cols = pl.ds(pl.multiple_of((own_ref[0] ^ d) * width, width), width)
+        out_ref[:, :width] = a_ref[:, cols]
+        out_ref[:, width:] = b_ref[:, cols]
+
+
+def column_parts(own, a, b, count):
+    rows, columns = a.shape
+    return pl.pallas_call(
+        parts_kernel,
+        name="column_parts",
+        compiler_params=grant(4),
+        in_specs=[pl.BlockSpec(memory_space=pltpu.SMEM)] + [pl.BlockSpec(memory_space=pltpu.VMEM)] * 2,
+        out_shape=[jax.ShapeDtypeStruct((rows, 2 * columns // count), a.dtype)] * count,
+    )(own, a, b)
+
+
+def rows_kernel(own_ref, a_ref, *outs):
+    rows = a_ref.shape[0] // len(outs)
+    for d, out_ref in enumerate(outs):
+        out_ref[...] = a_ref[pl.ds(pl.multiple_of((own_ref[0] ^ d) * rows, rows), rows), :]
+
+
+def row_parts(own, a, count):
+    rows, columns = a.shape
+    return pl.pallas_call(
+        rows_kernel,
+        name="row_parts",
+        compiler_params=grant(3),
+        in_specs=[pl.BlockSpec(memory_space=pltpu.SMEM), pl.BlockSpec(memory_space=pltpu.VMEM)],
+        out_shape=[jax.ShapeDtypeStruct((rows // count, columns), a.dtype)] * count,
+    )(own, a)
+
+
+def trade(parts, axis):
+    count = len(parts)
+    out = [parts[0]]
+    for d in range(1, count):
+        out.append(lax.ppermute(parts[d], axis, [(i, i ^ d) for i in range(count)]))
+    return out
+
+
 def unpack_kernel(in_ref, a_ref, b_ref):
     count = in_ref.shape[0]
     width = in_ref.shape[2] // 2
@@ -72,19 +129,26 @@
 def unpack(packed):
     count, rows, width = packed.shape
     shape = jax.ShapeDtypeStruct((rows, count * width // 2), packed.dtype)
-    return pl.pallas_call(unpack_kernel, name="unpack", out_shape=(shape, shape))(packed)
-
-
-def spread_kernel(in_ref, a_ref):
-    count, _, width = in_ref.shape
-    for j in range(count):
-        a_ref[:, j * width : (j + 1) * width] = in_ref[j]
-
-
-def spread(packed):
-    count, rows, width = packed.shape
-    shape = jax.ShapeDtypeStruct((rows, count * width), packed.dtype)
-    return pl.pallas_call(spread_kernel, name="spread", out_shape=shape)(packed)
+    return pl.pallas_call(unpack_kernel, name="unpack", compiler_params=grant(4), out_shape=(shape, shape))(packed)
+
+
+def spread_kernel(own_ref, *refs):
+    out_ref = refs[-1]
+    for d, in_ref in enumerate(refs[:-1]):
+        width = in_ref.shape[1]
+        out_ref[:, pl.ds(pl.multiple_of((own_ref[0] ^ d) * width, width), width)] = in_ref[...]
+
+
+def spread(own, parts):
+    rows, width = parts[0].shape
+    return pl.pallas_call(
+        spread_kernel,
+        name="spread",
+        compiler_params=grant(3),
+        in_specs=[pl.BlockSpec(memory_space=pltpu.SMEM)]
+        + [pl.BlockSpec(memory_space=pltpu.VMEM)] * len(parts),
+        out_shape=jax.ShapeDtypeStruct((rows, len(parts) * width), parts[0].dtype),
+    )(own, *parts)
 
 
 def gram_kernel(key_ref, value_ref, cumul_ref, out_ref, first_ref):
@@ -129,29 +193,33 @@
 
 
 def solve_kernel(
+    own_ref,
     key_ref,
     value_ref,
-    query_ref,
-    grad_ref,
     cumul_ref,
     ridge_ref,
     state_ref,
     first_ref,
-    adjoint_ref,
-    solved_ref,
-    delta_ref,
-    second_ref,
-    early,
-    late,
-    stream,
-    keys_t,
-    weights,
-    solution,
-    residual,
-    direction,
+    *rest,
 ):
+    parts, rest = rest[:8], rest[8:]
+    adjoint_ref, solved_ref, grad_ref, delta_ref, second_ref = rest[:5]
+    early, late, stream, keys_t, weights, solution, residual, direction, images, gathered, sems = rest[5:]
     head, block = pl.program_id(0), pl.program_id(1)
-    keys, values, grads = key_ref[...], value_ref[...], grad_ref[...]
+    count = len(parts)
+    copies = []
+    for d in range(count):
+        start = pl.multiple_of((own_ref[0] ^ d) * parts[d].shape[0], parts[d].shape[0])
+        target = gathered.at[pl.ds(start, parts[d].shape[0]), :]
+        copies.append(pltpu.make_async_copy(parts[d], target, sems.at[d]))
+    is_first = jnp.logical_and(head == 0, block == 0)
+
+    @pl.when(is_first)
+    def _():
+        for copy in copies:
+            copy.start()
+
+    keys, values = key_ref[...], value_ref[...]
     row = cumul_ref[0, pl.ds(block, 1), :]
     first_total = cumul_ref[0, 0:1, SPAN - 1 :]
     column = column_of(row)
@@ -177,19 +245,18 @@
     keys_t[:, :HALF] = key_t[:, HALF:]
     keys_t[:, HALF:] = key_t[:, :HALF]
 
-    def starts(which, half, rhs):
-        cols = slice(half * HALF, (half + 1) * HALF)
-        solution[which, :, cols] = jnp.zeros((DH, HALF), F32)
-        residual[which, :, cols] = rhs
-        direction[which, :, cols] = rhs
-        high, low = split(rhs)
-        weights[which, :DH, cols] = high
-        weights[which, DH:, cols] = low
-        return jnp.sum(rhs * rhs, axis=0, keepdims=True)
-
-    query_t = query_ref[...].astype(F32).T
+    @pl.when(is_first)
+    def _():
+        for copy in copies:
+            copy.wait()
+
+    rows = pl.ds(pl.multiple_of(block * SPAN, SPAN), SPAN)
+    queries = gathered[rows, pl.ds(pl.multiple_of(head * DH, DH), DH)]
+    grads = gathered[rows, pl.ds(pl.multiple_of((head + 2) * DH, DH), DH)]
+    grad_ref[...] = grads
+
+    query_t = queries.astype(F32).T
     value_rows = jnp.concatenate([value_high, value_low], axis=0)
-    rhos = [starts(0, half, query_t[:, half * HALF : (half + 1) * HALF]) for half in range(2)]
     for half in range(2):
         cols = slice(half * HALF, (half + 1) * HALF)
         grad_half = grads[cols]
@@ -202,44 +269,78 @@
             turned = jnp.concatenate([values[HALF:], values[:HALF]], axis=0)
             masked = (late[...] * dot_t(turned, grad_half)).astype(BF16)
             rhs = rhs + dot(keys_t[...], masked)
-        rhos.append(starts(1, half, rhs))
+        both = jnp.concatenate([query_t[:, cols], rhs], axis=1)
+        solution[half] = jnp.zeros((DH, SPAN), F32)
+        residual[half] = both
+        direction[half] = both
+        high, low = split(both)
+        weights[half, :DH] = high
+        weights[half, DH:] = low
+
+    chunks = [slice(c * DH, (c + 1) * DH) for c in range(SPAN // DH)]
+
+    def norms(half):
+        return tuple(
+            jnp.sum(residual[half, :, c] * residual[half, :, c], axis=0, keepdims=True)
+            for c in chunks
+        )
+
+    def multiply(half):
+        weight = weights[half]
+        tile, begin = (early, HALF) if half == 0 else (late, 0)
+        count = SPAN - begin
+        seen = dot(stream[begin:], weight)
+        within = tile[...]
+        scores = jnp.concatenate(
+            [
+                (within * seen[:count, :HALF]).astype(BF16),
+                (within * seen[:count, HALF:]).astype(BF16),
+            ],
+            axis=1,
+        )
+        image = dot(keys_t[:, begin:], scores)
+        gram = seen[count : count + DH] + seen[count + DH :]
+        decay = start_decay[:, half * HALF : (half + 1) * HALF]
+        images[half] = image + jnp.concatenate([decay, decay], axis=1) * gram
+
+    def update(half, rhos, last=False):
+        later = []
+        for c, rho in zip(chunks, rhos):
+            way = direction[half, :, c]
+            image = images[half, :, c] + ridge * way
+            step = rho / (jnp.sum(way * image, axis=0, keepdims=True) + EPSILON)
+            solution[half, :, c] += step * way
+            if last:
+                continue
+            left = residual[half, :, c] - step * image
+            residual[half, :, c] = left
+            rho_next = jnp.sum(left * left, axis=0, keepdims=True)
+            way = left + rho_next / (rho + EPSILON) * way
+            direction[half, :, c] = way
+            high, low = split(way)
+            weights[half, :DH, c] = high
+            weights[half, DH:, c] = low
+            later.append(rho_next)
+        return tuple(later)
+
+    multiply(0)
 
     def sweep(_, rhos):
-        later = []
-        for which in range(2):
-            for half in range(2):
-                cols = slice(half * HALF, (half + 1) * HALF)
-                rho = rhos[2 * which + half]
-                weight = weights[which, :, cols]
-                if half == 0:
-                    seen = dot(stream[HALF:], weight)
-                    scores = (early[...] * seen[:HALF]).astype(BF16)
-                    image = dot(keys_t[:, HALF:], scores)
-                    gram = seen[HALF : HALF + DH] + seen[HALF + DH :]
-                else:
-                    seen = dot(stream[...], weight)
-                    scores = (late[...] * seen[:SPAN]).astype(BF16)
-                    image = dot(keys_t[...], scores)
-                    gram = seen[SPAN : SPAN + DH] + seen[SPAN + DH :]
-                way = direction[which, :, cols]
-                image = image + start_decay[:, cols] * gram + ridge * way
-                step = rho / (jnp.sum(way * image, axis=0, keepdims=True) + EPSILON)
-                solution[which, :, cols] += step * way
-                rest = residual[which, :, cols] - step * image
-                residual[which, :, cols] = rest
-                rho_next = jnp.sum(rest * rest, axis=0, keepdims=True)
-                way = rest + rho_next / (rho + EPSILON) * way
-                direction[which, :, cols] = way
-                high, low = split(way)
-                weights[which, :DH, cols] = high
-                weights[which, DH:, cols] = low
-                later.append(rho_next)
-        return tuple(later)
-
-    lax.fori_loop(0, SOLVE_STEPS, sweep, tuple(rhos))
-
-    solved_t = solution[0]
-    adjoint = solution[1].T.astype(BF16)
+        rho_early, rho_late = rhos
+        multiply(1)
+        rho_early = update(0, rho_early)
+        multiply(0)
+        rho_late = update(1, rho_late)
+        return rho_early, rho_late
+
+    rho_early, rho_late = lax.fori_loop(0, SOLVE_STEPS - 1, sweep, (norms(0), norms(1)))
+    multiply(1)
+    update(0, rho_early, True)
+    update(1, rho_late, True)
+
+    solved_t = jnp.concatenate([solution[0, :, :HALF], solution[1, :, :HALF]], axis=1)
+    adjoint_t = jnp.concatenate([solution[0, :, HALF:], solution[1, :, HALF:]], axis=1)
+    adjoint = adjoint_t.T.astype(BF16)
     adjoint_ref[...] = adjoint
     solved_ref[...] = solved_t.T.astype(BF16)
     high, low = split(start_decay * solved_t)
@@ -317,10 +418,10 @@
     count = tokens // SPAN
     piece = head_dev * DH // number
     grid = (head_dev, count)
-    params = pltpu.CompilerParams(dimension_semantics=("arbitrary", "arbitrary"))
 
     first = swap(pack(keys, values, heads), "head").reshape(tokens, 2 * head_dev * DH)
-    second = swap(pack(queries, grads_out, heads), "head").reshape(tokens, 2 * head_dev * DH)
+    own = lax.axis_index("head").astype(jnp.int32).reshape(1)
+    parts = trade(column_parts(own, queries, grads_out, heads), "head")
     cumul = jnp.cumsum(log_decay.reshape(head_dev, count, SPAN), axis=2)
 
     low_spec = pl.BlockSpec((SPAN, DH), lambda h, b: (b, h))
@@ -329,7 +430,7 @@
     state_spec = pl.BlockSpec((DH, 2 * DH), lambda h, b: (h, 0))
     local_spec = pl.BlockSpec((1, DH, 2 * DH), lambda h, b: (h, 0, 0))
     state_shape = jax.ShapeDtypeStruct((head_dev * DH, 2 * DH), F32)
-    local_shape = jax.ShapeDtypeStruct((head_dev, DH, 2 * DH), F32)
+    local_hbm = pltpu.HBM((head_dev, DH, 2 * DH), F32)
 
     out, first_state = pl.pallas_call(
         gram_kernel,
@@ -344,12 +445,13 @@
             pl.BlockSpec((number // head_dev, piece + 8, 2 * DH), lambda h, b: (h, 0, 0)),
             local_spec,
         ],
-        out_shape=[jax.ShapeDtypeStruct((number, piece + 8, 2 * DH), F32), local_shape],
-        compiler_params=params,
+        out_shape=[jax.ShapeDtypeStruct((number, piece + 8, 2 * DH), F32), local_hbm],
+        compiler_params=grant(6),
     )(first, first, cumul.reshape(head_dev * count, 1, SPAN))
     prefix, factors = pl.pallas_call(
         scan_kernel,
         name="scan",
+        compiler_params=grant(2),
         out_shape=(
             jax.ShapeDtypeStruct((number, piece, 2 * DH), F32),
             jax.ShapeDtypeStruct((number, 8, 2 * DH), F32),
@@ -357,27 +459,23 @@
     )(swap(out, "ctx"))
     state = swap(prefix, "ctx").reshape(head_dev * DH, 2 * DH)
 
-    adjoint, solved, delta, second_state = pl.pallas_call(
+    token_hbm = pltpu.HBM((tokens, head_dev * DH), BF16)
+    adjoint, solved, grads_local, delta, second_state = pl.pallas_call(
         solve_kernel,
         name="solve",
         grid=grid,
         in_specs=[
-            low_spec,
-            high_spec,
+            pl.BlockSpec(memory_space=pltpu.SMEM),
             low_spec,
             high_spec,
             cumul_spec,
             pl.BlockSpec(memory_space=pltpu.SMEM),
             state_spec,
             local_spec,
-        ],
-        out_specs=[low_spec, low_spec, state_spec, local_spec],
-        out_shape=[
-            jax.ShapeDtypeStruct((tokens, head_dev * DH), BF16),
-            jax.ShapeDtypeStruct((tokens, head_dev * DH), BF16),
-            state_shape,
-            local_shape,
-        ],
+        ]
+        + [pl.BlockSpec(memory_space=pl.ANY)] * heads,
+        out_specs=[low_spec, low_spec, low_spec, state_spec, local_spec],
+        out_shape=[token_hbm, token_hbm, token_hbm, state_shape, local_hbm],
         scratch_shapes=[
             pltpu.VMEM((HALF, HALF), F32),
             pltpu.VMEM((SPAN, HALF), F32),
@@ -387,25 +485,29 @@
             pltpu.VMEM((2, DH, SPAN), F32),
             pltpu.VMEM((2, DH, SPAN), F32),
             pltpu.VMEM((2, DH, SPAN), F32),
+            pltpu.VMEM((2, DH, SPAN), F32),
+            pltpu.VMEM((tokens, 2 * head_dev * DH), BF16),
+            pltpu.SemaphoreType.DMA((heads,)),
         ],
-        compiler_params=params,
-    )(first, first, second, second, cumul, ridge, state, first_state)
-
-    grad_queries = spread(swap(adjoint.reshape(heads, tokens // heads, head_dev * DH), "head"))
+        compiler_params=grant(12),
+    )(own, first, first, cumul, in_hbm(ridge), state, first_state, *parts)
+
+    grad_queries = spread(own, trade(row_parts(own, adjoint, heads), "head"))
 
     key_local, value_local = pl.pallas_call(
         local_kernel,
         name="local",
         grid=grid,
-        in_specs=[low_spec, high_spec, high_spec, low_spec, low_spec, cumul_spec],
+        in_specs=[low_spec, high_spec, low_spec, low_spec, low_spec, cumul_spec],
         out_specs=[low_spec, low_spec],
-        out_shape=[jax.ShapeDtypeStruct((tokens, head_dev * DH), F32)] * 2,
-        compiler_params=params,
-    )(first, first, second, solved, adjoint, cumul)
+        out_shape=[pltpu.HBM((tokens, head_dev * DH), F32)] * 2,
+        compiler_params=grant(10),
+    )(first, first, grads_local, solved, adjoint, cumul)
 
     suffix = pl.pallas_call(
         scan_back_kernel,
         name="scan_back",
+        compiler_params=grant(2),
         out_shape=jax.ShapeDtypeStruct((number, piece, 2 * DH), F32),
     )(swap(delta.reshape(number, piece, 2 * DH), "ctx"), factors)
     state_after = swap(suffix, "ctx").reshape(head_dev * DH, 2 * DH)
@@ -431,8 +533,8 @@
         ],
         out_specs=pl.BlockSpec((SPAN, 2 * head_dev * DH), lambda b, h: (b, 0)),
         out_shape=jax.ShapeDtypeStruct((tokens, 2 * head_dev * DH), BF16),
-        compiler_params=params,
-    )(first, first, state_after, second_state, cumul, key_local, value_local)
+        compiler_params=grant(10),
+    )(first, first, state_after, second_state, cumul, in_hbm(key_local), in_hbm(value_local))
     grads = swap(grads.reshape(heads, tokens // heads, 2 * head_dev * DH), "head")
     grad_keys, grad_values = unpack(grads)
     return (grad_queries, grad_keys, grad_values)

time: 193 us -> 169 us (0.88)
  Pallas kernels: 72 us -> 57.9 us
  starting transfers between devices: 35.5 us -> 45.9 us
  blocking collectives: 23.5 us -> 14.8 us
  waiting for transfers between devices: 52.4 us -> 46.6 us
  local copies, waits for them, and re-layouts: 4.99 us -> 0.89 us
    all_to_all x6 -> x5, waiting for transfers between devices: 52.4 us -> 22.3 us  [swap(): return lax.all_to_all(pieces, axis, split_axis=0, concat_axis=0, tiled=True)]
    ppermute x0 -> x14, waiting for transfers between devices: none -> 24.3 us  [trade(): out.append(lax.ppermute(parts[d], axis, [(i, i ^ d) for i in range(count)]))]
    ppermute x0 -> x14, starting transfers between devices: none -> 18.4 us  [trade(): out.append(lax.ppermute(parts[d], axis, [(i, i ^ d) for i in range(count)]))]
    pallas_call x5 -> x7, Pallas kernels: 52.5 us -> 43.6 us  [the longest x1 39.3 us: shards(): pl.pallas_call(solve_kernel, name='solve', grid=grid, in_specs=[pl.BlockS...]
    all_to_all x2 -> x1, blocking collectives: 23.5 us -> 14.8 us  [swap(): return lax.all_to_all(pieces, axis, split_axis=0, concat_axis=0, tiled=True)]
    all_to_all x6 -> x5, starting transfers between devices: 35.5 us -> 27.5 us  [swap(): return lax.all_to_all(pieces, axis, split_axis=0, concat_axis=0, tiled=True)]
    unnamed x16 -> x20, local copies, waits for them, and re-layouts: 4.2 us -> 0.7 us
    pallas_call x2 -> x1, Pallas kernels: 4.53 us -> 2.26 us  [pack(): pl.pallas_call(pack_kernel, name='pack', out_shape=jax.ShapeDtypeStruct((...]
  transfers between devices with their start and end apart: 6 -> 19, of which waited for: 5 -> 11; matrix products, arithmetic and copies ran while one was open for 2% -> 1% of each run, Pallas kernels for 9% -> 4%
where the time goes in v2:
time: 169 us
  Pallas kernels  57.9 us (34%)
  waiting for transfers between devices  46.6 us (28%)
  starting transfers between devices  45.9 us (27%)
  blocking collectives  14.8 us (9%)
    pallas_call x1, Pallas kernels, shards(): pl.pallas_call(solve_kernel, name='solve', grid=grid, in_specs=[pl.BlockS...  39.3 us
    all_to_all x5, starting transfers between devices, swap(): return lax.all_to_all(pieces, axis, split_axis=0, concat_axis=0, tiled=True)  27.5 us
    ppermute x14, waiting for transfers between devices, trade(): out.append(lax.ppermute(parts[d], axis, [(i, i ^ d) for i in range(count)]))  24.3 us
    all_to_all x5, waiting for transfers between devices, swap(): return lax.all_to_all(pieces, axis, split_axis=0, concat_axis=0, tiled=True)  22.3 us
    ppermute x14, starting transfers between devices, trade(): out.append(lax.ppermute(parts[d], axis, [(i, i ^ d) for i in range(count)]))  18.4 us
    all_to_all x1, blocking collectives, swap(): return lax.all_to_all(pieces, axis, split_axis=0, concat_axis=0, tiled=True)  14.8 us
    pallas_call x1, Pallas kernels, shards(): pl.pallas_call(final_kernel, name='final', grid=(count, head_dev), in_spe...  4.87 us
    pallas_call x1, Pallas kernels, shards(): pl.pallas_call(local_kernel, name='local', grid=grid, in_specs=[low_spec,...  4.19 us
  transfers between devices with their start and end apart: 19, of which 11 were waited for; matrix products, arithmetic and copies ran while one was open for 1% of the time, Pallas kernels for 4%

profile of v2, /device:TPU:1, one launch (start us, length us, event | category | flops | bytes accessed | tf_op | source)
XLA Modules:
  0.0 168.5 jit_solution(17531223725402606780)
XLA Ops:
  0.6 2.3 %pack.1 = bf16[8,128,512]{2,1,0:T(8,128)(2,1)} custom-call(bf16[128,2048]{1,0:T(8,128)(2,1)} %a_ref.2, bf16[128,2048]{1,0:T(8,128)(2,1)} %b_ref.2), custom_call_target="tpu_custom_call" | custom-call | tf_op jit(solution)/shard_map/pack/pallas_call | solution.py:70
  2.9 6.1 %all-to-all-start = ((bf16[8,128,512]{2,1,0:T(8,128)(2,1)}), bf16[8,128,512]{2,1,0:T(8,128)(2,1)S(1)}, u32[]{:S(2)}, u32[]{:S(2)}) async-start(bf16[8,128,512]{2,1,0:T(8,128)(2,1)} %pack.1), calls=%async_computation | async-start | bytes 2097152 | tf_op jit(solution)/shard_map/all_to_all | solution.py:410
  9.0 1.2 reduce-window.6
  10.2 0.2 slice_reduce_fusion
  10.4 0.3 reduce-window.9
  10.7 0.1 broadcast_add_fusion
  10.8 13.1 %all-to-all-done = bf16[8,128,512]{2,1,0:T(8,128)(2,1)S(1)} async-done(((bf16[8,128,512]{2,1,0:T(8,128)(2,1)}), bf16[8,128,512]{2,1,0:T(8,128)(2,1)S(1)}, u32[]{:S(2)}, u32[]{:S(2)}) %all-to-all-start) | async-done | bytes 1048608 | tf_op jit(solution)/shard_map/all_to_all | solution.py:410
  24.0 3.0 %gram.1 = (f32[16,24,256]{2,1,0:T(8,128)}, f32[2,128,256]{2,1,0:T(8,128)}) custom-call(bf16[1024,512]{1,0:T(8,128)(2,1)S(1)} %bitcast.8, bf16[1024,512]{1,0:T(8,128)(2,1)S(1)} %bitcast.9, f32[4,1,512]{2,1,0:T(1,128)S(1)} %bitcast.19), custom_call_target="tpu_custom_call" | custom-call | tf_op jit(solution)/shard_map/gram/pallas_call | solution.py:435
  26.9 7.7 %all-to-all-start.1 = ((f32[16,24,256]{2,1,0:T(8,128)}), f32[16,24,256]{2,1,0:T(8,128)S(1)}, u32[]{:S(2)}, u32[]{:S(2)}) async-start(f32[16,24,256]{2,1,0:T(8,128)} %get-tuple-element.32), calls=%async_computation.1 | async-start | bytes 786432 | tf_op jit(solution)/shard_map/all_to_all | solution.py:410
  34.7 0.8 column_parts.1
  35.5 0.7 copy-done.7
  36.2 1.2 collective-permute-start
  37.4 0.3 collective-permute-start.1
  37.7 5.9 %all-to-all-done.1.in_ref = f32[16,24,256]{2,1,0:T(8,128)S(1)} async-done(((f32[16,24,256]{2,1,0:T(8,128)}), f32[16,24,256]{2,1,0:T(8,128)S(1)}, u32[]{:S(2)}, u32[]{:S(2)}) %all-to-all-start.1) | async-done | bytes 393248 | tf_op jit(solution)/shard_map/all_to_all | solution.py:410
  43.6 0.7 scan.1
  44.3 3.7 %all-to-all-start.2 = ((f32[16,16,256]{2,1,0:T(8,128)}), f32[16,16,256]{2,1,0:T(8,128)S(1)}, u32[]{:S(2)}, u32[]{:S(2)}) async-start(f32[16,16,256]{2,1,0:T(8,128)} %get-tuple-element.33), calls=%async_computation.2 | async-start | bytes 524288 | tf_op jit(solution)/shard_map/all_to_all | solution.py:410
  48.0 2.4 %collective-permute-start.2 = (bf16[128,512]{1,0:T(8,128)(2,1)}, bf16[128,512]{1,0:T(8,128)(2,1)S(1)}, u32[]{:S(2)}, u32[]{:S(2)}) collective-permute-start(bf16[128,512]{1,0:T(8,128)(2,1)} %get-tuple-element.38), channel_id=1, source_target_pairs={{0,3},{1,2},{2,1},{3,0},{4,7},{5,6},{6,5},{7,4},{8,11},{9,10},{10,... | collective-permute-start | bytes 393224 | tf_op jit(solution)/shard_map/ppermute | solution.py:117
  50.4 1.8 %collective-permute-start.3 = (bf16[128,512]{1,0:T(8,128)(2,1)S(1)}, bf16[128,512]{1,0:T(8,128)(2,1)S(1)}, u32[]{:S(2)}, u32[]{:S(2)}) collective-permute-start(bf16[128,512]{1,0:T(8,128)(2,1)S(1)} %copy-done.8), channel_id=1, source_target_pairs={{0,4},{1,5},{2,6},{3,7},{4,0},{5,1},{6,2},{7,3},{8,12},{9,13},{10,... | collective-permute-start | bytes 393224 | tf_op jit(solution)/shard_map/ppermute | solution.py:117
  52.2 1.3 collective-permute-start.4
  53.4 0.9 collective-permute-start.5
  54.3 0.0 collective-permute-done.1.rest_2_
  54.3 2.3 %collective-permute-start.6 = (bf16[128,512]{1,0:T(8,128)(2,1)S(1)}, bf16[128,512]{1,0:T(8,128)(2,1)S(1)}, u32[]{:S(2)}, u32[]{:S(2)}) collective-permute-start(bf16[128,512]{1,0:T(8,128)(2,1)S(1)} %get-tuple-element.42), channel_id=1, source_target_pairs={{0,7},{1,6},{2,5},{3,4},{4,3},{5,2},{6,1},{7,0},{8,15},{9,14},{10,... | collective-permute-start | bytes 393224 | tf_op jit(solution)/shard_map/ppermute | solution.py:117
  56.6 1.5 collective-permute-done.3.rest_4_
  58.1 2.5 %collective-permute-done.4.rest_5_ = bf16[128,512]{1,0:T(8,128)(2,1)S(1)} collective-permute-done((bf16[128,512]{1,0:T(8,128)(2,1)S(1)}, bf16[128,512]{1,0:T(8,128)(2,1)S(1)}, u32[]{:S(2)}, u32[]{:S(2)}) %collective-permute-start.4) | collective-permute-done | bytes 131104 | tf_op jit(solution)/shard_map/ppermute | solution.py:117
  60.6 2.9 %collective-permute-done.5.rest_6_ = bf16[128,512]{1,0:T(8,128)(2,1)S(1)} collective-permute-done((bf16[128,512]{1,0:T(8,128)(2,1)S(1)}, bf16[128,512]{1,0:T(8,128)(2,1)S(1)}, u32[]{:S(2)}, u32[]{:S(2)}) %collective-permute-start.5) | collective-permute-done | bytes 131104 | tf_op jit(solution)/shard_map/ppermute | solution.py:117
  63.5 2.8 %collective-permute-done.6.rest_7_ = bf16[128,512]{1,0:T(8,128)(2,1)S(1)} collective-permute-done((bf16[128,512]{1,0:T(8,128)(2,1)S(1)}, bf16[128,512]{1,0:T(8,128)(2,1)S(1)}, u32[]{:S(2)}, u32[]{:S(2)}) %collective-permute-start.6) | collective-permute-done | bytes 131104 | tf_op jit(solution)/shard_map/ppermute | solution.py:117
  66.3 39.3 %solve.1 = (bf16[1024,256]{1,0:T(8,128)(2,1)}, bf16[1024,256]{1,0:T(8,128)(2,1)}, bf16[1024,256]{1,0:T(8,128)(2,1)}, f32[256,256]{1,0:T(8,128)S(1)}, f32[2,128,256]{2,1,0:T(8,128)}) custom-call(s32[1]{0:T(128)} %bitcast.own_ref, bf16[1024,512]{1,0:T(8,128)(2,1)S(1)} %bitcast.10, bf16[1024,512]{1,0:T(8,128)(2,1)S(1)} %bitcast.11, ...), custom_call_target="tpu_custom_call" | custom-call | tf_op jit(solution)/shard_map/solve/pallas_call | solution.py:463
  105.6 0.0 copy-start.2
  105.6 14.8 %all_to_all.30.in_ref = f32[16,16,256]{2,1,0:T(8,128)S(1)} all-to-all(f32[16,16,256]{2,1,0:T(8,128)S(1)} %bitcast.18), channel_id=1, replica_groups=mesh['ctx'=16,'head'=8] {'ctx'}, dimensions={0} | all-to-all | bytes 524288 | tf_op jit(solution)/shard_map/all_to_all | solution.py:410
  120.4 0.8 scan_back.1
  121.2 3.5 %all-to-all-start.4 = ((f32[16,16,256]{2,1,0:T(8,128)}), f32[16,16,256]{2,1,0:T(8,128)S(1)}, u32[]{:S(2)}, u32[]{:S(2)}) async-start(f32[16,16,256]{2,1,0:T(8,128)} %scan_back.1), calls=%async_computation.4 | async-start | bytes 524288 | tf_op jit(solution)/shard_map/all_to_all | solution.py:410
  124.8 4.2 %local.1 = (f32[1024,256]{1,0:T(8,128)}, f32[1024,256]{1,0:T(8,128)}) custom-call(bf16[1024,512]{1,0:T(8,128)(2,1)S(1)} %bitcast.12, bf16[1024,512]{1,0:T(8,128)(2,1)S(1)} %bitcast.13, bf16[1024,256]{1,0:T(8,128)(2,1)S(1)} %copy-done.2, bf16[1024,256]{1,0:T(8,128)(2,1)S(1)} %copy-done.1, bf16[1024,256]{1,0:T(8,128)(2,1)S(1)} %copy-done, ...), custom_call_target="tpu_custom_call" | custom-call | tf_op jit(solution)/shard_map/local/pallas_call | solution.py:497
  129.0 3.3 %all-to-all-done.4 = f32[16,16,256]{2,1,0:T(8,128)S(1)} async-done(((f32[16,16,256]{2,1,0:T(8,128)}), f32[16,16,256]{2,1,0:T(8,128)S(1)}, u32[]{:S(2)}, u32[]{:S(2)}) %all-to-all-start.4) | async-done | bytes 262176 | tf_op jit(solution)/shard_map/all_to_all | solution.py:410
  132.2 4.9 %final.1 = bf16[1024,512]{1,0:T(8,128)(2,1)} custom-call(bf16[1024,512]{1,0:T(8,128)(2,1)S(1)} %bitcast.14, bf16[1024,512]{1,0:T(8,128)(2,1)S(1)} %bitcast.15, f32[256,256]{1,0:T(8,128)S(1)} %bitcast.16, f32[2,128,256]{2,1,0:T(8,128)S(1)} %copy-done.5, f32[2,2,512]{2,1,0:T(2,128)S(1)} %reduce_window_sum.26.cumul_ref, ...), custom_call_target="tpu_custom_call" | custom-call | tf_op jit(solution)/shard_map/final/pallas_call | solution.py:518
  137.1 6.5 %all-to-all-start.5 = ((bf16[8,128,512]{2,1,0:T(8,128)(2,1)}), bf16[8,128,512]{2,1,0:T(8,128)(2,1)S(1)}, u32[]{:S(2)}, u32[]{:S(2)}) async-start(bf16[8,128,512]{2,1,0:T(8,128)(2,1)} %bitcast.6), calls=%async_computation.5 | async-start | bytes 2097152 | tf_op jit(solution)/shard_map/all_to_all | solution.py:410
  143.6 2.9 %collective-permute-start.10 = (bf16[128,256]{1,0:T(8,128)(2,1)S(1)}, bf16[128,256]{1,0:T(8,128)(2,1)S(1)}, u32[]{:S(2)}, u32[]{:S(2)}) collective-permute-start(bf16[128,256]{1,0:T(8,128)(2,1)S(1)} %get-tuple-element.48), channel_id=1, source_target_pairs={{0,4},{1,5},{2,6},{3,7},{4,0},{5,1},{6,2},{7,3},{8,12},{9,13},{10,... | collective-permute-start | bytes 196616 | tf_op jit(solution)/shard_map/ppermute | solution.py:117
  146.5 0.4 collective-permute-start.11
  146.9 2.9 %collective-permute-start.12 = (bf16[128,256]{1,0:T(8,128)(2,1)S(1)}, bf16[128,256]{1,0:T(8,128)(2,1)S(1)}, u32[]{:S(2)}, u32[]{:S(2)}) collective-permute-start(bf16[128,256]{1,0:T(8,128)(2,1)S(1)} %get-tuple-element.50), channel_id=1, source_target_pairs={{0,6},{1,7},{2,4},{3,5},{4,2},{5,3},{6,0},{7,1},{8,14},{9,15},{10,... | collective-permute-start | bytes 196616 | tf_op jit(solution)/shard_map/ppermute | solution.py:117
  149.8 0.3 collective-permute-start.13
  150.1 0.1 collective-permute-start.7
  150.2 9.8 %collective-permute-done.10.refs_4_ = bf16[128,256]{1,0:T(8,128)(2,1)S(1)} collective-permute-done((bf16[128,256]{1,0:T(8,128)(2,1)S(1)}, bf16[128,256]{1,0:T(8,128)(2,1)S(1)}, u32[]{:S(2)}, u32[]{:S(2)}) %collective-permute-start.10) | collective-permute-done | bytes 65568 | tf_op jit(solution)/shard_map/ppermute | solution.py:117
  160.0 0.3 collective-permute-start.8
  160.3 1.5 collective-permute-done.11.refs_5_
  161.7 1.5 collective-permute-start.9
  163.2 0.9 collective-permute-done.13.refs_7_
  164.1 2.4 %collective-permute-done.9.refs_3_ = bf16[128,256]{1,0:T(8,128)(2,1)S(1)} collective-permute-done((bf16[128,256]{1,0:T(8,128)(2,1)S(1)}, bf16[128,256]{1,0:T(8,128)(2,1)S(1)}, u32[]{:S(2)}, u32[]{:S(2)}) %collective-permute-start.9) | collective-permute-done | bytes 65568 | tf_op jit(solution)/shard_map/ppermute | solution.py:117
  166.6 0.8 spread.1
  167.4 1.1 unpack.1
  (28 shorter events, 0.1 us)
Async XLA Ops:
  2.9 6.1 %copy-start.9 = (f32[2,1024]{1,0:T(2,128)S(1)}, f32[2,1024]{1,0:T(2,128)}, u32[]{:S(2)}) copy-start(f32[2,1024]{1,0:T(2,128)} %param.10) | copy-start | bytes 24580
  2.9 21.1 %all-to-all-start = ((bf16[8,128,512]{2,1,0:T(8,128)(2,1)}), bf16[8,128,512]{2,1,0:T(8,128)(2,1)S(1)}, u32[]{:S(2)}, u32[]{:S(2)}) async-start(bf16[8,128,512]{2,1,0:T(8,128)(2,1)} %pack.1), calls=%async_computation | async-start | bytes 2097152 | tf_op jit(solution)/shard_map/all_to_all | solution.py:410
  24.0 10.7 %copy-start.4 = (bf16[128,2048]{1,0:T(8,128)(2,1)S(1)}, bf16[128,2048]{1,0:T(8,128)(2,1)}, u32[]{:S(2)}) copy-start(bf16[128,2048]{1,0:T(8,128)(2,1)} %b_ref.3) | copy-start | bytes 1572868
  26.9 7.8 %copy-start.3 = (bf16[128,2048]{1,0:T(8,128)(2,1)S(1)}, bf16[128,2048]{1,0:T(8,128)(2,1)}, u32[]{:S(2)}) copy-start(bf16[128,2048]{1,0:T(8,128)(2,1)} %a_ref.3) | copy-start | bytes 1572868
  26.9 16.7 %all-to-all-start.1 = ((f32[16,24,256]{2,1,0:T(8,128)}), f32[16,24,256]{2,1,0:T(8,128)S(1)}, u32[]{:S(2)}, u32[]{:S(2)}) async-start(f32[16,24,256]{2,1,0:T(8,128)} %get-tuple-element.32), calls=%async_computation.1 | async-start | bytes 786432 | tf_op jit(solution)/shard_map/all_to_all | solution.py:410
  35.5 0.7 copy-start.7
  36.2 17.2 %collective-permute-start = (bf16[128,512]{1,0:T(8,128)(2,1)}, bf16[128,512]{1,0:T(8,128)(2,1)S(1)}, u32[]{:S(2)}, u32[]{:S(2)}) collective-permute-start(bf16[128,512]{1,0:T(8,128)(2,1)} %get-tuple-element.36), channel_id=1, source_target_pairs={{0,1},{1,0},{2,3},{3,2},{4,5},{5,4},{6,7},{7,6},{8,9},{9,8},{10,11... | collective-permute-start | bytes 393224 | tf_op jit(solution)/shard_map/ppermute | solution.py:117
  37.4 16.9 %collective-permute-start.1 = (bf16[128,512]{1,0:T(8,128)(2,1)}, bf16[128,512]{1,0:T(8,128)(2,1)S(1)}, u32[]{:S(2)}, u32[]{:S(2)}) collective-permute-start(bf16[128,512]{1,0:T(8,128)(2,1)} %get-tuple-element.37), channel_id=1, source_target_pairs={{0,2},{1,3},{2,0},{3,1},{4,6},{5,7},{6,4},{7,5},{8,10},{9,11},{10,... | collective-permute-start | bytes 393224 | tf_op jit(solution)/shard_map/ppermute | solution.py:117
  44.3 6.0 %copy-start.8 = (bf16[128,512]{1,0:T(8,128)(2,1)S(1)}, bf16[128,512]{1,0:T(8,128)(2,1)}, u32[]{:S(2)}) copy-start(bf16[128,512]{1,0:T(8,128)(2,1)} %copy-done.7) | copy-start | bytes 393220
  44.3 22.0 %copy-start.6 = (f32[2,128,256]{2,1,0:T(8,128)S(1)}, f32[2,128,256]{2,1,0:T(8,128)}, u32[]{:S(2)}) copy-start(f32[2,128,256]{2,1,0:T(8,128)} %get-tuple-element.34.first_ref) | copy-start | bytes 786436
  44.3 22.0 %all-to-all-start.2 = ((f32[16,16,256]{2,1,0:T(8,128)}), f32[16,16,256]{2,1,0:T(8,128)S(1)}, u32[]{:S(2)}, u32[]{:S(2)}) async-start(f32[16,16,256]{2,1,0:T(8,128)} %get-tuple-element.33), calls=%async_computation.2 | async-start | bytes 524288 | tf_op jit(solution)/shard_map/all_to_all | solution.py:410
  48.0 8.6 %collective-permute-start.2 = (bf16[128,512]{1,0:T(8,128)(2,1)}, bf16[128,512]{1,0:T(8,128)(2,1)S(1)}, u32[]{:S(2)}, u32[]{:S(2)}) collective-permute-start(bf16[128,512]{1,0:T(8,128)(2,1)} %get-tuple-element.38), channel_id=1, source_target_pairs={{0,3},{1,2},{2,1},{3,0},{4,7},{5,6},{6,5},{7,4},{8,11},{9,10},{10,... | collective-permute-start | bytes 393224 | tf_op jit(solution)/shard_map/ppermute | solution.py:117
  50.4 7.7 %collective-permute-start.3 = (bf16[128,512]{1,0:T(8,128)(2,1)S(1)}, bf16[128,512]{1,0:T(8,128)(2,1)S(1)}, u32[]{:S(2)}, u32[]{:S(2)}) collective-permute-start(bf16[128,512]{1,0:T(8,128)(2,1)S(1)} %copy-done.8), channel_id=1, source_target_pairs={{0,4},{1,5},{2,6},{3,7},{4,0},{5,1},{6,2},{7,3},{8,12},{9,13},{10,... | collective-permute-start | bytes 393224 | tf_op jit(solution)/shard_map/ppermute | solution.py:117
  52.2 8.5 %collective-permute-start.4 = (bf16[128,512]{1,0:T(8,128)(2,1)S(1)}, bf16[128,512]{1,0:T(8,128)(2,1)S(1)}, u32[]{:S(2)}, u32[]{:S(2)}) collective-permute-start(bf16[128,512]{1,0:T(8,128)(2,1)S(1)} %get-tuple-element.40), channel_id=1, source_target_pairs={{0,5},{1,4},{2,7},{3,6},{4,1},{5,0},{6,3},{7,2},{8,13},{9,12},{10,... | collective-permute-start | bytes 393224 | tf_op jit(solution)/shard_map/ppermute | solution.py:117
  53.4 10.1 %collective-permute-start.5 = (bf16[128,512]{1,0:T(8,128)(2,1)S(1)}, bf16[128,512]{1,0:T(8,128)(2,1)S(1)}, u32[]{:S(2)}, u32[]{:S(2)}) collective-permute-start(bf16[128,512]{1,0:T(8,128)(2,1)S(1)} %get-tuple-element.41), channel_id=1, source_target_pairs={{0,6},{1,7},{2,4},{3,5},{4,2},{5,3},{6,0},{7,1},{8,14},{9,15},{10,... | collective-permute-start | bytes 393224 | tf_op jit(solution)/shard_map/ppermute | solution.py:117
  54.3 12.0 %collective-permute-start.6 = (bf16[128,512]{1,0:T(8,128)(2,1)S(1)}, bf16[128,512]{1,0:T(8,128)(2,1)S(1)}, u32[]{:S(2)}, u32[]{:S(2)}) collective-permute-start(bf16[128,512]{1,0:T(8,128)(2,1)S(1)} %get-tuple-element.42), channel_id=1, source_target_pairs={{0,7},{1,6},{2,5},{3,4},{4,3},{5,2},{6,1},{7,0},{8,15},{9,14},{10,... | collective-permute-start | bytes 393224 | tf_op jit(solution)/shard_map/ppermute | solution.py:117
  105.6 19.1 %copy-start.2 = (bf16[1024,256]{1,0:T(8,128)(2,1)S(1)}, bf16[1024,256]{1,0:T(8,128)(2,1)}, u32[]{:S(2)}) copy-start(bf16[1024,256]{1,0:T(8,128)(2,1)} %get-tuple-element.55.grad_ref) | copy-start | bytes 1572868
  120.4 4.3 %copy-start = (bf16[1024,256]{1,0:T(8,128)(2,1)S(1)}, bf16[1024,256]{1,0:T(8,128)(2,1)}, u32[]{:S(2)}) copy-start(bf16[1024,256]{1,0:T(8,128)(2,1)} %get-tuple-element.43.a_ref.adjoint_ref) | copy-start | bytes 1572868
  120.4 4.3 %copy-start.1 = (bf16[1024,256]{1,0:T(8,128)(2,1)S(1)}, bf16[1024,256]{1,0:T(8,128)(2,1)}, u32[]{:S(2)}) copy-start(bf16[1024,256]{1,0:T(8,128)(2,1)} %get-tuple-element.56.solved_ref) | copy-start | bytes 1572868
  121.2 11.0 %all-to-all-start.4 = ((f32[16,16,256]{2,1,0:T(8,128)}), f32[16,16,256]{2,1,0:T(8,128)S(1)}, u32[]{:S(2)}, u32[]{:S(2)}) async-start(f32[16,16,256]{2,1,0:T(8,128)} %scan_back.1), calls=%async_computation.4 | async-start | bytes 524288 | tf_op jit(solution)/shard_map/all_to_all | solution.py:410
  124.8 7.5 %copy-start.5 = (f32[2,128,256]{2,1,0:T(8,128)S(1)}, f32[2,128,256]{2,1,0:T(8,128)}, u32[]{:S(2)}) copy-start(f32[2,128,256]{2,1,0:T(8,128)} %get-tuple-element.54.second_ref) | copy-start | bytes 786436
  137.1 30.3 %all-to-all-start.5 = ((bf16[8,128,512]{2,1,0:T(8,128)(2,1)}), bf16[8,128,512]{2,1,0:T(8,128)(2,1)S(1)}, u32[]{:S(2)}, u32[]{:S(2)}) async-start(bf16[8,128,512]{2,1,0:T(8,128)(2,1)} %bitcast.6), calls=%async_computation.5 | async-start | bytes 2097152 | tf_op jit(solution)/shard_map/all_to_all | solution.py:410
  143.6 16.4 %collective-permute-start.10 = (bf16[128,256]{1,0:T(8,128)(2,1)S(1)}, bf16[128,256]{1,0:T(8,128)(2,1)S(1)}, u32[]{:S(2)}, u32[]{:S(2)}) collective-permute-start(bf16[128,256]{1,0:T(8,128)(2,1)S(1)} %get-tuple-element.48), channel_id=1, source_target_pairs={{0,4},{1,5},{2,6},{3,7},{4,0},{5,1},{6,2},{7,3},{8,12},{9,13},{10,... | collective-permute-start | bytes 196616 | tf_op jit(solution)/shard_map/ppermute | solution.py:117
  146.5 15.2 %collective-permute-start.11 = (bf16[128,256]{1,0:T(8,128)(2,1)S(1)}, bf16[128,256]{1,0:T(8,128)(2,1)S(1)}, u32[]{:S(2)}, u32[]{:S(2)}) collective-permute-start(bf16[128,256]{1,0:T(8,128)(2,1)S(1)} %get-tuple-element.49), channel_id=1, source_target_pairs={{0,5},{1,4},{2,7},{3,6},{4,1},{5,0},{6,3},{7,2},{8,13},{9,12},{10,... | collective-permute-start | bytes 196616 | tf_op jit(solution)/shard_map/ppermute | solution.py:117
  146.9 16.3 %collective-permute-start.12 = (bf16[128,256]{1,0:T(8,128)(2,1)S(1)}, bf16[128,256]{1,0:T(8,128)(2,1)S(1)}, u32[]{:S(2)}, u32[]{:S(2)}) collective-permute-start(bf16[128,256]{1,0:T(8,128)(2,1)S(1)} %get-tuple-element.50), channel_id=1, source_target_pairs={{0,6},{1,7},{2,4},{3,5},{4,2},{5,3},{6,0},{7,1},{8,14},{9,15},{10,... | collective-permute-start | bytes 196616 | tf_op jit(solution)/shard_map/ppermute | solution.py:117
  149.8 14.4 %collective-permute-start.13 = (bf16[128,256]{1,0:T(8,128)(2,1)S(1)}, bf16[128,256]{1,0:T(8,128)(2,1)S(1)}, u32[]{:S(2)}, u32[]{:S(2)}) collective-permute-start(bf16[128,256]{1,0:T(8,128)(2,1)S(1)} %get-tuple-element.51), channel_id=1, source_target_pairs={{0,7},{1,6},{2,5},{3,4},{4,3},{5,2},{6,1},{7,0},{8,15},{9,14},{10,... | collective-permute-start | bytes 196616 | tf_op jit(solution)/shard_map/ppermute | solution.py:117
  150.1 14.1 %collective-permute-start.7 = (bf16[128,256]{1,0:T(8,128)(2,1)S(1)}, bf16[128,256]{1,0:T(8,128)(2,1)S(1)}, u32[]{:S(2)}, u32[]{:S(2)}) collective-permute-start(bf16[128,256]{1,0:T(8,128)(2,1)S(1)} %get-tuple-element.45), channel_id=1, source_target_pairs={{0,1},{1,0},{2,3},{3,2},{4,5},{5,4},{6,7},{7,6},{8,9},{9,8},{10,11... | collective-permute-start | bytes 196616 | tf_op jit(solution)/shard_map/ppermute | solution.py:117
  160.0 4.2 %collective-permute-start.8 = (bf16[128,256]{1,0:T(8,128)(2,1)S(1)}, bf16[128,256]{1,0:T(8,128)(2,1)S(1)}, u32[]{:S(2)}, u32[]{:S(2)}) collective-permute-start(bf16[128,256]{1,0:T(8,128)(2,1)S(1)} %get-tuple-element.46), channel_id=1, source_target_pairs={{0,2},{1,3},{2,0},{3,1},{4,6},{5,7},{6,4},{7,5},{8,10},{9,11},{10,... | collective-permute-start | bytes 196616 | tf_op jit(solution)/shard_map/ppermute | solution.py:117
  161.7 4.8 %collective-permute-start.9 = (bf16[128,256]{1,0:T(8,128)(2,1)S(1)}, bf16[128,256]{1,0:T(8,128)(2,1)S(1)}, u32[]{:S(2)}, u32[]{:S(2)}) collective-permute-start(bf16[128,256]{1,0:T(8,128)(2,1)S(1)} %get-tuple-element.47), channel_id=1, source_target_pairs={{0,3},{1,2},{2,1},{3,0},{4,7},{5,6},{6,5},{7,4},{8,11},{9,10},{10,... | collective-permute-start | bytes 196616 | tf_op jit(solution)/shard_map/ppermute | solution.py:117

commit v3 on v2

--- a/solution.py
+++ b/solution.py
@@ -204,20 +204,17 @@
 ):
     parts, rest = rest[:8], rest[8:]
     adjoint_ref, solved_ref, grad_ref, delta_ref, second_ref = rest[:5]
-    early, late, stream, keys_t, weights, solution, residual, direction, images, gathered, sems = rest[5:]
+    early, late, stream, mixing, gathered = rest[5:10]
+    weights, scaled, solution, residual, direction, images, rhos = zip(rest[10:17], rest[17:])
     head, block = pl.program_id(0), pl.program_id(1)
     count = len(parts)
-    copies = []
-    for d in range(count):
-        start = pl.multiple_of((own_ref[0] ^ d) * parts[d].shape[0], parts[d].shape[0])
-        target = gathered.at[pl.ds(start, parts[d].shape[0]), :]
-        copies.append(pltpu.make_async_copy(parts[d], target, sems.at[d]))
-    is_first = jnp.logical_and(head == 0, block == 0)
-
-    @pl.when(is_first)
-    def _():
-        for copy in copies:
-            copy.start()
+
+    @pl.when(jnp.logical_and(head == 0, block == 0))
+    def _():
+        for d in range(count):
+            size = parts[d].shape[0]
+            start = pl.multiple_of((own_ref[0] ^ d) * size, size)
+            gathered[pl.ds(start, size), :] = parts[d][...]
 
     keys, values = key_ref[...], value_ref[...]
     row = cumul_ref[0, pl.ds(block, 1), :]
@@ -236,19 +233,12 @@
     state = entry * state_ref[...] + local * first_ref[0]
     gram_high, gram_low = split(state[:, :DH])
     value_high, value_low = split(state[:, DH:])
-    zero = jnp.zeros((HALF, DH), BF16)
-    stream[0:HALF] = jnp.concatenate([keys[HALF:], zero], axis=1)
-    stream[HALF:SPAN] = jnp.concatenate([keys[:HALF], zero], axis=1)
-    stream[SPAN : SPAN + DH] = jnp.concatenate([gram_high, gram_high], axis=1)
-    stream[SPAN + DH :] = jnp.concatenate([gram_low, gram_low], axis=1)
+    stream[:HALF] = keys[HALF:]
+    stream[HALF:] = keys[:HALF]
     key_t = keys.astype(F32).T.astype(BF16)
-    keys_t[:, :HALF] = key_t[:, HALF:]
-    keys_t[:, HALF:] = key_t[:, :HALF]
-
-    @pl.when(is_first)
-    def _():
-        for copy in copies:
-            copy.wait()
+    mixing[:, 3 * DH : 3 * DH + HALF] = key_t[:, HALF:]
+    mixing[:, 3 * DH + HALF :] = key_t[:, :HALF]
+    mixing[:, : 3 * DH] = jnp.concatenate([gram_high, gram_high, gram_low], axis=1)
 
     rows = pl.ds(pl.multiple_of(block * SPAN, SPAN), SPAN)
     queries = gathered[rows, pl.ds(pl.multiple_of(head * DH, DH), DH)]
@@ -264,82 +254,118 @@
         rhs = start_decay[:, cols] * (seen[:DH] + seen[DH:])
         if half == 0:
             masked = (early[...] * dot_t(values[:HALF], grad_half)).astype(BF16)
-            rhs = rhs + dot(keys_t[:, HALF:], masked)
+            rhs = rhs + dot(mixing[:, 3 * DH + HALF :], masked)
         else:
             turned = jnp.concatenate([values[HALF:], values[:HALF]], axis=0)
             masked = (late[...] * dot_t(turned, grad_half)).astype(BF16)
-            rhs = rhs + dot(keys_t[...], masked)
+            rhs = rhs + dot(mixing[:, 3 * DH :], masked)
         both = jnp.concatenate([query_t[:, cols], rhs], axis=1)
-        solution[half] = jnp.zeros((DH, SPAN), F32)
-        residual[half] = both
-        direction[half] = both
-        high, low = split(both)
-        weights[half, :DH] = high
-        weights[half, DH:] = low
-
-    chunks = [slice(c * DH, (c + 1) * DH) for c in range(SPAN // DH)]
+        solution[half][...] = jnp.zeros((DH, SPAN), F32)
+        residual[half][...] = both
+        direction[half][...] = both
+        decay = start_decay[:, cols]
+        high, low = split(jnp.concatenate([decay, decay], axis=1) * both)
+        weights[half][...] = both.astype(BF16)
+        scaled[half][:DH] = high
+        scaled[half][DH : 2 * DH] = low
+        scaled[half][2 * DH :] = high
+
+    groups = [slice(g * 16, (g + 1) * 16) for g in range(DH // 16)]
+
+    def column_sum(parts):
+        total = parts[0]
+        for part in parts[1:]:
+            total = total + part
+        return jnp.sum(total, axis=0, keepdims=True)
 
     def norms(half):
-        return tuple(
-            jnp.sum(residual[half, :, c] * residual[half, :, c], axis=0, keepdims=True)
-            for c in chunks
-        )
+        return column_sum([residual[half][g, :] * residual[half][g, :] for g in groups])
 
     def multiply(half):
-        weight = weights[half]
         tile, begin = (early, HALF) if half == 0 else (late, 0)
         count = SPAN - begin
-        seen = dot(stream[begin:], weight)
-        within = tile[...]
-        scores = jnp.concatenate(
-            [
-                (within * seen[:count, :HALF]).astype(BF16),
-                (within * seen[:count, HALF:]).astype(BF16),
-            ],
-            axis=1,
-        )
-        image = dot(keys_t[:, begin:], scores)
-        gram = seen[count : count + DH] + seen[count + DH :]
+        seen = dot(stream[begin:], weights[half][...])
+        yield
+        scores = []
+        for start in range(0, count, 16):
+            within = tile[start : start + 16]
+            part = seen[start : start + 16]
+            scores.append(
+                jnp.concatenate(
+                    [
+                        (within * part[:, :HALF]).astype(BF16),
+                        (within * part[:, HALF:]).astype(BF16),
+                    ],
+                    axis=1,
+                )
+            )
+            yield
+        if half == 0:
+            left = jnp.concatenate([mixing[:, : 3 * DH], mixing[:, 3 * DH + HALF :]], axis=1)
+        else:
+            left = mixing[...]
+        images[half][...] = dot(left, jnp.concatenate([scaled[half][...]] + scores, axis=0))
+        yield
+
+    def update(half, last=False):
+        rho = rhos[half][...]
         decay = start_decay[:, half * HALF : (half + 1) * HALF]
-        images[half] = image + jnp.concatenate([decay, decay], axis=1) * gram
-
-    def update(half, rhos, last=False):
-        later = []
-        for c, rho in zip(chunks, rhos):
-            way = direction[half, :, c]
-            image = images[half, :, c] + ridge * way
-            step = rho / (jnp.sum(way * image, axis=0, keepdims=True) + EPSILON)
-            solution[half, :, c] += step * way
-            if last:
-                continue
-            left = residual[half, :, c] - step * image
-            residual[half, :, c] = left
-            rho_next = jnp.sum(left * left, axis=0, keepdims=True)
-            way = left + rho_next / (rho + EPSILON) * way
-            direction[half, :, c] = way
-            high, low = split(way)
-            weights[half, :DH, c] = high
-            weights[half, DH:, c] = low
-            later.append(rho_next)
-        return tuple(later)
-
-    multiply(0)
-
-    def sweep(_, rhos):
-        rho_early, rho_late = rhos
-        multiply(1)
-        rho_early = update(0, rho_early)
-        multiply(0)
-        rho_late = update(1, rho_late)
-        return rho_early, rho_late
-
-    rho_early, rho_late = lax.fori_loop(0, SOLVE_STEPS - 1, sweep, (norms(0), norms(1)))
-    multiply(1)
-    update(0, rho_early, True)
-    update(1, rho_late, True)
-
-    solved_t = jnp.concatenate([solution[0, :, :HALF], solution[1, :, :HALF]], axis=1)
-    adjoint_t = jnp.concatenate([solution[0, :, HALF:], solution[1, :, HALF:]], axis=1)
+        decay = jnp.concatenate([decay, decay], axis=1)
+        along = 0.0
+        for g in groups:
+            way = direction[half][g, :]
+            image = images[half][g, :] + ridge * way
+            images[half][g, :] = image
+            along = along + way * image
+            yield
+        step = rho / (jnp.sum(along, axis=0, keepdims=True) + EPSILON)
+        norm = 0.0
+        for g in groups:
+            solution[half][g, :] += step * direction[half][g, :]
+            if not last:
+                left = residual[half][g, :] - step * images[half][g, :]
+                residual[half][g, :] = left
+                norm = norm + left * left
+            yield
+        if last:
+            return
+        rho_next = jnp.sum(norm, axis=0, keepdims=True)
+        rhos[half][...] = rho_next
+        turn = rho_next / (rho + EPSILON)
+        for g in groups:
+            way = residual[half][g, :] + turn * direction[half][g, :]
+            direction[half][g, :] = way
+            weights[half][g, :] = way.astype(BF16)
+            high, low = split(decay * way)
+            scaled[half][g, :] = high
+            scaled[half][DH + g.start : DH + g.stop, :] = low
+            scaled[half][2 * DH + g.start : 2 * DH + g.stop, :] = high
+            yield
+
+    def weave(multiplying, updating, ratio):
+        for _ in multiplying:
+            for _ in range(ratio):
+                next(updating, None)
+        for _ in updating:
+            pass
+
+    for half in range(2):
+        rhos[half][...] = norms(half)
+    for _ in multiply(0):
+        pass
+
+    def sweep(_, carry):
+        weave(multiply(1), update(0), 1)
+        weave(multiply(0), update(1), 1)
+        return carry
+
+    lax.fori_loop(0, SOLVE_STEPS - 1, sweep, 0, unroll=True)
+    weave(multiply(1), update(0, True), 1)
+    for _ in update(1, True):
+        pass
+
+    solved_t = jnp.concatenate([solution[0][:, :HALF], solution[1][:, :HALF]], axis=1)
+    adjoint_t = jnp.concatenate([solution[0][:, HALF:], solution[1][:, HALF:]], axis=1)
     adjoint = adjoint_t.T.astype(BF16)
     adjoint_ref[...] = adjoint
     solved_ref[...] = solved_t.T.astype(BF16)
@@ -473,22 +499,26 @@
             state_spec,
             local_spec,
         ]
-        + [pl.BlockSpec(memory_space=pl.ANY)] * heads,
+        + [pl.BlockSpec(memory_space=pltpu.VMEM)] * heads,
         out_specs=[low_spec, low_spec, low_spec, state_spec, local_spec],
         out_shape=[token_hbm, token_hbm, token_hbm, state_shape, local_hbm],
         scratch_shapes=[
             pltpu.VMEM((HALF, HALF), F32),
             pltpu.VMEM((SPAN, HALF), F32),
-            pltpu.VMEM((SPAN + 2 * DH, 2 * DH), BF16),
+            pltpu.VMEM((SPAN, DH), BF16),
+            pltpu.VMEM((DH, SPAN + 3 * DH), BF16),
+            pltpu.VMEM((tokens, 2 * head_dev * DH), BF16),
+        ]
+        + [
             pltpu.VMEM((DH, SPAN), BF16),
-            pltpu.VMEM((2, 2 * DH, SPAN), BF16),
-            pltpu.VMEM((2, DH, SPAN), F32),
-            pltpu.VMEM((2, DH, SPAN), F32),
-            pltpu.VMEM((2, DH, SPAN), F32),
-            pltpu.VMEM((2, DH, SPAN), F32),
-            pltpu.VMEM((tokens, 2 * head_dev * DH), BF16),
-            pltpu.SemaphoreType.DMA((heads,)),
-        ],
+            pltpu.VMEM((3 * DH, SPAN), BF16),
+            pltpu.VMEM((DH, SPAN), F32),
+            pltpu.VMEM((DH, SPAN), F32),
+            pltpu.VMEM((DH, SPAN), F32),
+            pltpu.VMEM((DH, SPAN), F32),
+            pltpu.VMEM((1, SPAN), F32),
+        ]
+        * 2,
         compiler_params=grant(12),
     )(own, first, first, cumul, in_hbm(ridge), state, first_state, *parts)
 

time: 169 us -> 156 us (0.923)
  Pallas kernels: 57.9 us -> 44.5 us
    pallas_call x1, Pallas kernels: 39.3 us -> 25.9 us  [shards(): pl.pallas_call(solve_kernel, name='solve', grid=grid, in_specs=[pl.BlockS...]
where the time goes in v3:
time: 156 us; the launch traced here: 155 us
  waiting for transfers between devices  46.6 us (30%)
  starting transfers between devices  45.9 us (29%)
  Pallas kernels  44.5 us (29%)
  blocking collectives  14.8 us (9%)
  other arithmetic  1.65 us (1%)
    all_to_all x5, starting transfers between devices, swap(): return lax.all_to_all(pieces, axis, split_axis=0, concat_axis=0, tiled=True)  27.5 us
    pallas_call x1, Pallas kernels, shards(): pl.pallas_call(solve_kernel, name='solve', grid=grid, in_specs=[pl.BlockS...  25.9 us
    ppermute x14, waiting for transfers between devices, trade(): out.append(lax.ppermute(parts[d], axis, [(i, i ^ d) for i in range(count)]))  24.3 us
    all_to_all x5, waiting for transfers between devices, swap(): return lax.all_to_all(pieces, axis, split_axis=0, concat_axis=0, tiled=True)  22.3 us
    ppermute x14, starting transfers between devices, trade(): out.append(lax.ppermute(parts[d], axis, [(i, i ^ d) for i in range(count)]))  18.4 us
    all_to_all x1, blocking collectives, swap(): return lax.all_to_all(pieces, axis, split_axis=0, concat_axis=0, tiled=True)  14.8 us
    pallas_call x1, Pallas kernels, shards(): pl.pallas_call(final_kernel, name='final', grid=(count, head_dev), in_spe...  4.87 us
    pallas_call x1, Pallas kernels, shards(): pl.pallas_call(local_kernel, name='local', grid=grid, in_specs=[low_spec,...  4.17 us
  transfers between devices with their start and end apart: 19, of which 11 were waited for; matrix products, arithmetic and copies ran while one was open for 1% of the time, Pallas kernels for 4%

profile of v3, /device:TPU:1, one launch (start us, length us, event | category | flops | bytes accessed | tf_op | source)
XLA Modules:
  0.0 155.1 jit_solution(7271524935651349638)
XLA Ops:
  0.6 2.3 %pack.1 = bf16[8,128,512]{2,1,0:T(8,128)(2,1)} custom-call(bf16[128,2048]{1,0:T(8,128)(2,1)} %a_ref.2, bf16[128,2048]{1,0:T(8,128)(2,1)} %b_ref.2), custom_call_target="tpu_custom_call" | custom-call | tf_op jit(solution)/shard_map/pack/pallas_call | solution.py:70
  2.9 6.1 %all-to-all-start = ((bf16[8,128,512]{2,1,0:T(8,128)(2,1)}), bf16[8,128,512]{2,1,0:T(8,128)(2,1)S(1)}, u32[]{:S(2)}, u32[]{:S(2)}) async-start(bf16[8,128,512]{2,1,0:T(8,128)(2,1)} %pack.1), calls=%async_computation | async-start | bytes 2097152 | tf_op jit(solution)/shard_map/all_to_all | solution.py:436
  9.0 1.2 reduce-window.6
  10.2 0.2 slice_reduce_fusion
  10.4 0.3 reduce-window.9
  10.7 0.1 broadcast_add_fusion
  10.8 13.1 %all-to-all-done = bf16[8,128,512]{2,1,0:T(8,128)(2,1)S(1)} async-done(((bf16[8,128,512]{2,1,0:T(8,128)(2,1)}), bf16[8,128,512]{2,1,0:T(8,128)(2,1)S(1)}, u32[]{:S(2)}, u32[]{:S(2)}) %all-to-all-start) | async-done | bytes 1048608 | tf_op jit(solution)/shard_map/all_to_all | solution.py:436
  24.0 3.0 %gram.1 = (f32[16,24,256]{2,1,0:T(8,128)}, f32[2,128,256]{2,1,0:T(8,128)}) custom-call(bf16[1024,512]{1,0:T(8,128)(2,1)S(1)} %bitcast.8, bf16[1024,512]{1,0:T(8,128)(2,1)S(1)} %bitcast.9, f32[4,1,512]{2,1,0:T(1,128)S(1)} %bitcast.19), custom_call_target="tpu_custom_call" | custom-call | tf_op jit(solution)/shard_map/gram/pallas_call | solution.py:461
  26.9 7.7 %all-to-all-start.1 = ((f32[16,24,256]{2,1,0:T(8,128)}), f32[16,24,256]{2,1,0:T(8,128)S(1)}, u32[]{:S(2)}, u32[]{:S(2)}) async-start(f32[16,24,256]{2,1,0:T(8,128)} %get-tuple-element.32), calls=%async_computation.1 | async-start | bytes 786432 | tf_op jit(solution)/shard_map/all_to_all | solution.py:436
  34.7 0.8 column_parts.1
  35.5 0.7 copy-done.7
  36.2 1.2 collective-permute-start
  37.4 0.3 collective-permute-start.1
  37.7 5.9 %all-to-all-done.1.in_ref = f32[16,24,256]{2,1,0:T(8,128)S(1)} async-done(((f32[16,24,256]{2,1,0:T(8,128)}), f32[16,24,256]{2,1,0:T(8,128)S(1)}, u32[]{:S(2)}, u32[]{:S(2)}) %all-to-all-start.1) | async-done | bytes 393248 | tf_op jit(solution)/shard_map/all_to_all | solution.py:436
  43.6 0.7 scan.1
  44.3 3.7 %all-to-all-start.2 = ((f32[16,16,256]{2,1,0:T(8,128)}), f32[16,16,256]{2,1,0:T(8,128)S(1)}, u32[]{:S(2)}, u32[]{:S(2)}) async-start(f32[16,16,256]{2,1,0:T(8,128)} %get-tuple-element.33), calls=%async_computation.2 | async-start | bytes 524288 | tf_op jit(solution)/shard_map/all_to_all | solution.py:436
  48.0 2.4 %collective-permute-start.2 = (bf16[128,512]{1,0:T(8,128)(2,1)}, bf16[128,512]{1,0:T(8,128)(2,1)S(1)}, u32[]{:S(2)}, u32[]{:S(2)}) collective-permute-start(bf16[128,512]{1,0:T(8,128)(2,1)} %get-tuple-element.38), channel_id=1, source_target_pairs={{0,3},{1,2},{2,1},{3,0},{4,7},{5,6},{6,5},{7,4},{8,11},{9,10},{10,... | collective-permute-start | bytes 393224 | tf_op jit(solution)/shard_map/ppermute | solution.py:117
  50.4 1.8 %collective-permute-start.3 = (bf16[128,512]{1,0:T(8,128)(2,1)S(1)}, bf16[128,512]{1,0:T(8,128)(2,1)S(1)}, u32[]{:S(2)}, u32[]{:S(2)}) collective-permute-start(bf16[128,512]{1,0:T(8,128)(2,1)S(1)} %copy-done.8), channel_id=1, source_target_pairs={{0,4},{1,5},{2,6},{3,7},{4,0},{5,1},{6,2},{7,3},{8,12},{9,13},{10,... | collective-permute-start | bytes 393224 | tf_op jit(solution)/shard_map/ppermute | solution.py:117
  52.2 1.3 collective-permute-start.4
  53.4 0.9 collective-permute-start.5
  54.3 0.0 collective-permute-done.1.rest_2_
  54.3 2.3 %collective-permute-start.6 = (bf16[128,512]{1,0:T(8,128)(2,1)S(1)}, bf16[128,512]{1,0:T(8,128)(2,1)S(1)}, u32[]{:S(2)}, u32[]{:S(2)}) collective-permute-start(bf16[128,512]{1,0:T(8,128)(2,1)S(1)} %get-tuple-element.42), channel_id=1, source_target_pairs={{0,7},{1,6},{2,5},{3,4},{4,3},{5,2},{6,1},{7,0},{8,15},{9,14},{10,... | collective-permute-start | bytes 393224 | tf_op jit(solution)/shard_map/ppermute | solution.py:117
  56.6 0.0 collective-permute-done.2.rest_3_
  56.6 1.5 collective-permute-done.3.rest_4_
  58.1 2.5 %collective-permute-done.4.rest_5_ = bf16[128,512]{1,0:T(8,128)(2,1)S(1)} collective-permute-done((bf16[128,512]{1,0:T(8,128)(2,1)S(1)}, bf16[128,512]{1,0:T(8,128)(2,1)S(1)}, u32[]{:S(2)}, u32[]{:S(2)}) %collective-permute-start.4) | collective-permute-done | bytes 131104 | tf_op jit(solution)/shard_map/ppermute | solution.py:117
  60.6 2.9 %collective-permute-done.5.rest_6_ = bf16[128,512]{1,0:T(8,128)(2,1)S(1)} collective-permute-done((bf16[128,512]{1,0:T(8,128)(2,1)S(1)}, bf16[128,512]{1,0:T(8,128)(2,1)S(1)}, u32[]{:S(2)}, u32[]{:S(2)}) %collective-permute-start.5) | collective-permute-done | bytes 131104 | tf_op jit(solution)/shard_map/ppermute | solution.py:117
  63.5 2.8 %collective-permute-done.6.rest_7_ = bf16[128,512]{1,0:T(8,128)(2,1)S(1)} collective-permute-done((bf16[128,512]{1,0:T(8,128)(2,1)S(1)}, bf16[128,512]{1,0:T(8,128)(2,1)S(1)}, u32[]{:S(2)}, u32[]{:S(2)}) %collective-permute-start.6) | collective-permute-done | bytes 131104 | tf_op jit(solution)/shard_map/ppermute | solution.py:117
  66.3 25.9 %solve.1 = (bf16[1024,256]{1,0:T(8,128)(2,1)}, bf16[1024,256]{1,0:T(8,128)(2,1)}, bf16[1024,256]{1,0:T(8,128)(2,1)}, f32[256,256]{1,0:T(8,128)S(1)}, f32[2,128,256]{2,1,0:T(8,128)}) custom-call(s32[1]{0:T(128)} %bitcast.own_ref, bf16[1024,512]{1,0:T(8,128)(2,1)S(1)} %bitcast.10, bf16[1024,512]{1,0:T(8,128)(2,1)S(1)} %bitcast.11, ...), custom_call_target="tpu_custom_call" | custom-call | tf_op jit(solution)/shard_map/solve/pallas_call | solution.py:489
  92.2 14.8 %all_to_all.30.in_ref = f32[16,16,256]{2,1,0:T(8,128)S(1)} all-to-all(f32[16,16,256]{2,1,0:T(8,128)S(1)} %bitcast.18), channel_id=1, replica_groups=mesh['ctx'=16,'head'=8] {'ctx'}, dimensions={0} | all-to-all | bytes 524288 | tf_op jit(solution)/shard_map/all_to_all | solution.py:436
  107.0 0.8 scan_back.1
  107.8 3.5 %all-to-all-start.4 = ((f32[16,16,256]{2,1,0:T(8,128)}), f32[16,16,256]{2,1,0:T(8,128)S(1)}, u32[]{:S(2)}, u32[]{:S(2)}) async-start(f32[16,16,256]{2,1,0:T(8,128)} %scan_back.1), calls=%async_computation.4 | async-start | bytes 524288 | tf_op jit(solution)/shard_map/all_to_all | solution.py:436
  111.4 4.2 %local.1 = (f32[1024,256]{1,0:T(8,128)}, f32[1024,256]{1,0:T(8,128)}) custom-call(bf16[1024,512]{1,0:T(8,128)(2,1)S(1)} %bitcast.12, bf16[1024,512]{1,0:T(8,128)(2,1)S(1)} %bitcast.13, bf16[1024,256]{1,0:T(8,128)(2,1)S(1)} %copy-done.2, bf16[1024,256]{1,0:T(8,128)(2,1)S(1)} %copy-done.1, bf16[1024,256]{1,0:T(8,128)(2,1)S(1)} %copy-done, ...), custom_call_target="tpu_custom_call" | custom-call | tf_op jit(solution)/shard_map/local/pallas_call | solution.py:527
  115.5 3.3 %all-to-all-done.4 = f32[16,16,256]{2,1,0:T(8,128)S(1)} async-done(((f32[16,16,256]{2,1,0:T(8,128)}), f32[16,16,256]{2,1,0:T(8,128)S(1)}, u32[]{:S(2)}, u32[]{:S(2)}) %all-to-all-start.4) | async-done | bytes 262176 | tf_op jit(solution)/shard_map/all_to_all | solution.py:436
  118.8 4.9 %final.1 = bf16[1024,512]{1,0:T(8,128)(2,1)} custom-call(bf16[1024,512]{1,0:T(8,128)(2,1)S(1)} %bitcast.14, bf16[1024,512]{1,0:T(8,128)(2,1)S(1)} %bitcast.15, f32[256,256]{1,0:T(8,128)S(1)} %bitcast.16, f32[2,128,256]{2,1,0:T(8,128)S(1)} %copy-done.5, f32[2,2,512]{2,1,0:T(2,128)S(1)} %reduce_window_sum.26.cumul_ref, ...), custom_call_target="tpu_custom_call" | custom-call | tf_op jit(solution)/shard_map/final/pallas_call | solution.py:548
  123.7 6.5 %all-to-all-start.5 = ((bf16[8,128,512]{2,1,0:T(8,128)(2,1)}), bf16[8,128,512]{2,1,0:T(8,128)(2,1)S(1)}, u32[]{:S(2)}, u32[]{:S(2)}) async-start(bf16[8,128,512]{2,1,0:T(8,128)(2,1)} %bitcast.6), calls=%async_computation.5 | async-start | bytes 2097152 | tf_op jit(solution)/shard_map/all_to_all | solution.py:436
  130.2 2.9 %collective-permute-start.10 = (bf16[128,256]{1,0:T(8,128)(2,1)S(1)}, bf16[128,256]{1,0:T(8,128)(2,1)S(1)}, u32[]{:S(2)}, u32[]{:S(2)}) collective-permute-start(bf16[128,256]{1,0:T(8,128)(2,1)S(1)} %get-tuple-element.48), channel_id=1, source_target_pairs={{0,4},{1,5},{2,6},{3,7},{4,0},{5,1},{6,2},{7,3},{8,12},{9,13},{10,... | collective-permute-start | bytes 196616 | tf_op jit(solution)/shard_map/ppermute | solution.py:117
  133.1 0.4 collective-permute-start.11
  133.5 2.9 %collective-permute-start.12 = (bf16[128,256]{1,0:T(8,128)(2,1)S(1)}, bf16[128,256]{1,0:T(8,128)(2,1)S(1)}, u32[]{:S(2)}, u32[]{:S(2)}) collective-permute-start(bf16[128,256]{1,0:T(8,128)(2,1)S(1)} %get-tuple-element.50), channel_id=1, source_target_pairs={{0,6},{1,7},{2,4},{3,5},{4,2},{5,3},{6,0},{7,1},{8,14},{9,15},{10,... | collective-permute-start | bytes 196616 | tf_op jit(solution)/shard_map/ppermute | solution.py:117
  136.4 0.3 collective-permute-start.13
  136.7 0.1 collective-permute-start.7
  136.8 9.8 %collective-permute-done.10.refs_4_ = bf16[128,256]{1,0:T(8,128)(2,1)S(1)} collective-permute-done((bf16[128,256]{1,0:T(8,128)(2,1)S(1)}, bf16[128,256]{1,0:T(8,128)(2,1)S(1)}, u32[]{:S(2)}, u32[]{:S(2)}) %collective-permute-start.10) | collective-permute-done | bytes 65568 | tf_op jit(solution)/shard_map/ppermute | solution.py:117
  146.6 0.3 collective-permute-start.8
  146.9 1.5 collective-permute-done.11.refs_5_
  148.3 1.5 collective-permute-start.9
  149.8 0.9 collective-permute-done.13.refs_7_
  150.7 2.4 %collective-permute-done.9.refs_3_ = bf16[128,256]{1,0:T(8,128)(2,1)S(1)} collective-permute-done((bf16[128,256]{1,0:T(8,128)(2,1)S(1)}, bf16[128,256]{1,0:T(8,128)(2,1)S(1)}, u32[]{:S(2)}, u32[]{:S(2)}) %collective-permute-start.9) | collective-permute-done | bytes 65568 | tf_op jit(solution)/shard_map/ppermute | solution.py:117
  153.2 0.8 spread.1
  154.0 1.1 unpack.1
  (28 shorter events, 0.1 us)
Async XLA Ops:
  2.9 6.1 %copy-start.9 = (f32[2,1024]{1,0:T(2,128)S(1)}, f32[2,1024]{1,0:T(2,128)}, u32[]{:S(2)}) copy-start(f32[2,1024]{1,0:T(2,128)} %param.10) | copy-start | bytes 24580
  2.9 21.1 %all-to-all-start = ((bf16[8,128,512]{2,1,0:T(8,128)(2,1)}), bf16[8,128,512]{2,1,0:T(8,128)(2,1)S(1)}, u32[]{:S(2)}, u32[]{:S(2)}) async-start(bf16[8,128,512]{2,1,0:T(8,128)(2,1)} %pack.1), calls=%async_computation | async-start | bytes 2097152 | tf_op jit(solution)/shard_map/all_to_all | solution.py:436
  24.0 10.7 %copy-start.4 = (bf16[128,2048]{1,0:T(8,128)(2,1)S(1)}, bf16[128,2048]{1,0:T(8,128)(2,1)}, u32[]{:S(2)}) copy-start(bf16[128,2048]{1,0:T(8,128)(2,1)} %b_ref.3) | copy-start | bytes 1572868
  26.9 7.8 %copy-start.3 = (bf16[128,2048]{1,0:T(8,128)(2,1)S(1)}, bf16[128,2048]{1,0:T(8,128)(2,1)}, u32[]{:S(2)}) copy-start(bf16[128,2048]{1,0:T(8,128)(2,1)} %a_ref.3) | copy-start | bytes 1572868
  26.9 16.7 %all-to-all-start.1 = ((f32[16,24,256]{2,1,0:T(8,128)}), f32[16,24,256]{2,1,0:T(8,128)S(1)}, u32[]{:S(2)}, u32[]{:S(2)}) async-start(f32[16,24,256]{2,1,0:T(8,128)} %get-tuple-element.32), calls=%async_computation.1 | async-start | bytes 786432 | tf_op jit(solution)/shard_map/all_to_all | solution.py:436
  35.5 0.7 copy-start.7
  36.2 17.2 %collective-permute-start = (bf16[128,512]{1,0:T(8,128)(2,1)}, bf16[128,512]{1,0:T(8,128)(2,1)S(1)}, u32[]{:S(2)}, u32[]{:S(2)}) collective-permute-start(bf16[128,512]{1,0:T(8,128)(2,1)} %get-tuple-element.36), channel_id=1, source_target_pairs={{0,1},{1,0},{2,3},{3,2},{4,5},{5,4},{6,7},{7,6},{8,9},{9,8},{10,11... | collective-permute-start | bytes 393224 | tf_op jit(solution)/shard_map/ppermute | solution.py:117
  37.4 16.9 %collective-permute-start.1 = (bf16[128,512]{1,0:T(8,128)(2,1)}, bf16[128,512]{1,0:T(8,128)(2,1)S(1)}, u32[]{:S(2)}, u32[]{:S(2)}) collective-permute-start(bf16[128,512]{1,0:T(8,128)(2,1)} %get-tuple-element.37), channel_id=1, source_target_pairs={{0,2},{1,3},{2,0},{3,1},{4,6},{5,7},{6,4},{7,5},{8,10},{9,11},{10,... | collective-permute-start | bytes 393224 | tf_op jit(solution)/shard_map/ppermute | solution.py:117
  44.3 6.0 %copy-start.8 = (bf16[128,512]{1,0:T(8,128)(2,1)S(1)}, bf16[128,512]{1,0:T(8,128)(2,1)}, u32[]{:S(2)}) copy-start(bf16[128,512]{1,0:T(8,128)(2,1)} %copy-done.7) | copy-start | bytes 393220
  44.3 22.0 %copy-start.6 = (f32[2,128,256]{2,1,0:T(8,128)S(1)}, f32[2,128,256]{2,1,0:T(8,128)}, u32[]{:S(2)}) copy-start(f32[2,128,256]{2,1,0:T(8,128)} %get-tuple-element.34.first_ref) | copy-start | bytes 786436
  44.3 22.0 %all-to-all-start.2 = ((f32[16,16,256]{2,1,0:T(8,128)}), f32[16,16,256]{2,1,0:T(8,128)S(1)}, u32[]{:S(2)}, u32[]{:S(2)}) async-start(f32[16,16,256]{2,1,0:T(8,128)} %get-tuple-element.33), calls=%async_computation.2 | async-start | bytes 524288 | tf_op jit(solution)/shard_map/all_to_all | solution.py:436
  48.0 8.6 %collective-permute-start.2 = (bf16[128,512]{1,0:T(8,128)(2,1)}, bf16[128,512]{1,0:T(8,128)(2,1)S(1)}, u32[]{:S(2)}, u32[]{:S(2)}) collective-permute-start(bf16[128,512]{1,0:T(8,128)(2,1)} %get-tuple-element.38), channel_id=1, source_target_pairs={{0,3},{1,2},{2,1},{3,0},{4,7},{5,6},{6,5},{7,4},{8,11},{9,10},{10,... | collective-permute-start | bytes 393224 | tf_op jit(solution)/shard_map/ppermute | solution.py:117
  50.4 7.7 %collective-permute-start.3 = (bf16[128,512]{1,0:T(8,128)(2,1)S(1)}, bf16[128,512]{1,0:T(8,128)(2,1)S(1)}, u32[]{:S(2)}, u32[]{:S(2)}) collective-permute-start(bf16[128,512]{1,0:T(8,128)(2,1)S(1)} %copy-done.8), channel_id=1, source_target_pairs={{0,4},{1,5},{2,6},{3,7},{4,0},{5,1},{6,2},{7,3},{8,12},{9,13},{10,... | collective-permute-start | bytes 393224 | tf_op jit(solution)/shard_map/ppermute | solution.py:117
  52.2 8.5 %collective-permute-start.4 = (bf16[128,512]{1,0:T(8,128)(2,1)S(1)}, bf16[128,512]{1,0:T(8,128)(2,1)S(1)}, u32[]{:S(2)}, u32[]{:S(2)}) collective-permute-start(bf16[128,512]{1,0:T(8,128)(2,1)S(1)} %get-tuple-element.40), channel_id=1, source_target_pairs={{0,5},{1,4},{2,7},{3,6},{4,1},{5,0},{6,3},{7,2},{8,13},{9,12},{10,... | collective-permute-start | bytes 393224 | tf_op jit(solution)/shard_map/ppermute | solution.py:117
  53.4 10.1 %collective-permute-start.5 = (bf16[128,512]{1,0:T(8,128)(2,1)S(1)}, bf16[128,512]{1,0:T(8,128)(2,1)S(1)}, u32[]{:S(2)}, u32[]{:S(2)}) collective-permute-start(bf16[128,512]{1,0:T(8,128)(2,1)S(1)} %get-tuple-element.41), channel_id=1, source_target_pairs={{0,6},{1,7},{2,4},{3,5},{4,2},{5,3},{6,0},{7,1},{8,14},{9,15},{10,... | collective-permute-start | bytes 393224 | tf_op jit(solution)/shard_map/ppermute | solution.py:117
  54.3 12.0 %collective-permute-start.6 = (bf16[128,512]{1,0:T(8,128)(2,1)S(1)}, bf16[128,512]{1,0:T(8,128)(2,1)S(1)}, u32[]{:S(2)}, u32[]{:S(2)}) collective-permute-start(bf16[128,512]{1,0:T(8,128)(2,1)S(1)} %get-tuple-element.42), channel_id=1, source_target_pairs={{0,7},{1,6},{2,5},{3,4},{4,3},{5,2},{6,1},{7,0},{8,15},{9,14},{10,... | collective-permute-start | bytes 393224 | tf_op jit(solution)/shard_map/ppermute | solution.py:117
  92.2 19.1 %copy-start.2 = (bf16[1024,256]{1,0:T(8,128)(2,1)S(1)}, bf16[1024,256]{1,0:T(8,128)(2,1)}, u32[]{:S(2)}) copy-start(bf16[1024,256]{1,0:T(8,128)(2,1)} %get-tuple-element.55.grad_ref) | copy-start | bytes 1572868
  107.0 4.3 %copy-start = (bf16[1024,256]{1,0:T(8,128)(2,1)S(1)}, bf16[1024,256]{1,0:T(8,128)(2,1)}, u32[]{:S(2)}) copy-start(bf16[1024,256]{1,0:T(8,128)(2,1)} %get-tuple-element.43.a_ref.adjoint_ref) | copy-start | bytes 1572868
  107.0 4.3 %copy-start.1 = (bf16[1024,256]{1,0:T(8,128)(2,1)S(1)}, bf16[1024,256]{1,0:T(8,128)(2,1)}, u32[]{:S(2)}) copy-start(bf16[1024,256]{1,0:T(8,128)(2,1)} %get-tuple-element.56.solved_ref) | copy-start | bytes 1572868
  107.8 11.0 %all-to-all-start.4 = ((f32[16,16,256]{2,1,0:T(8,128)}), f32[16,16,256]{2,1,0:T(8,128)S(1)}, u32[]{:S(2)}, u32[]{:S(2)}) async-start(f32[16,16,256]{2,1,0:T(8,128)} %scan_back.1), calls=%async_computation.4 | async-start | bytes 524288 | tf_op jit(solution)/shard_map/all_to_all | solution.py:436
  111.4 7.5 %copy-start.5 = (f32[2,128,256]{2,1,0:T(8,128)S(1)}, f32[2,128,256]{2,1,0:T(8,128)}, u32[]{:S(2)}) copy-start(f32[2,128,256]{2,1,0:T(8,128)} %get-tuple-element.54.second_ref) | copy-start | bytes 786436
  123.7 30.3 %all-to-all-start.5 = ((bf16[8,128,512]{2,1,0:T(8,128)(2,1)}), bf16[8,128,512]{2,1,0:T(8,128)(2,1)S(1)}, u32[]{:S(2)}, u32[]{:S(2)}) async-start(bf16[8,128,512]{2,1,0:T(8,128)(2,1)} %bitcast.6), calls=%async_computation.5 | async-start | bytes 2097152 | tf_op jit(solution)/shard_map/all_to_all | solution.py:436
  130.2 16.4 %collective-permute-start.10 = (bf16[128,256]{1,0:T(8,128)(2,1)S(1)}, bf16[128,256]{1,0:T(8,128)(2,1)S(1)}, u32[]{:S(2)}, u32[]{:S(2)}) collective-permute-start(bf16[128,256]{1,0:T(8,128)(2,1)S(1)} %get-tuple-element.48), channel_id=1, source_target_pairs={{0,4},{1,5},{2,6},{3,7},{4,0},{5,1},{6,2},{7,3},{8,12},{9,13},{10,... | collective-permute-start | bytes 196616 | tf_op jit(solution)/shard_map/ppermute | solution.py:117
  133.1 15.2 %collective-permute-start.11 = (bf16[128,256]{1,0:T(8,128)(2,1)S(1)}, bf16[128,256]{1,0:T(8,128)(2,1)S(1)}, u32[]{:S(2)}, u32[]{:S(2)}) collective-permute-start(bf16[128,256]{1,0:T(8,128)(2,1)S(1)} %get-tuple-element.49), channel_id=1, source_target_pairs={{0,5},{1,4},{2,7},{3,6},{4,1},{5,0},{6,3},{7,2},{8,13},{9,12},{10,... | collective-permute-start | bytes 196616 | tf_op jit(solution)/shard_map/ppermute | solution.py:117
  133.5 16.3 %collective-permute-start.12 = (bf16[128,256]{1,0:T(8,128)(2,1)S(1)}, bf16[128,256]{1,0:T(8,128)(2,1)S(1)}, u32[]{:S(2)}, u32[]{:S(2)}) collective-permute-start(bf16[128,256]{1,0:T(8,128)(2,1)S(1)} %get-tuple-element.50), channel_id=1, source_target_pairs={{0,6},{1,7},{2,4},{3,5},{4,2},{5,3},{6,0},{7,1},{8,14},{9,15},{10,... | collective-permute-start | bytes 196616 | tf_op jit(solution)/shard_map/ppermute | solution.py:117
  136.4 14.4 %collective-permute-start.13 = (bf16[128,256]{1,0:T(8,128)(2,1)S(1)}, bf16[128,256]{1,0:T(8,128)(2,1)S(1)}, u32[]{:S(2)}, u32[]{:S(2)}) collective-permute-start(bf16[128,256]{1,0:T(8,128)(2,1)S(1)} %get-tuple-element.51), channel_id=1, source_target_pairs={{0,7},{1,6},{2,5},{3,4},{4,3},{5,2},{6,1},{7,0},{8,15},{9,14},{10,... | collective-permute-start | bytes 196616 | tf_op jit(solution)/shard_map/ppermute | solution.py:117
  136.7 14.1 %collective-permute-start.7 = (bf16[128,256]{1,0:T(8,128)(2,1)S(1)}, bf16[128,256]{1,0:T(8,128)(2,1)S(1)}, u32[]{:S(2)}, u32[]{:S(2)}) collective-permute-start(bf16[128,256]{1,0:T(8,128)(2,1)S(1)} %get-tuple-element.45), channel_id=1, source_target_pairs={{0,1},{1,0},{2,3},{3,2},{4,5},{5,4},{6,7},{7,6},{8,9},{9,8},{10,11... | collective-permute-start | bytes 196616 | tf_op jit(solution)/shard_map/ppermute | solution.py:117
  146.6 4.2 %collective-permute-start.8 = (bf16[128,256]{1,0:T(8,128)(2,1)S(1)}, bf16[128,256]{1,0:T(8,128)(2,1)S(1)}, u32[]{:S(2)}, u32[]{:S(2)}) collective-permute-start(bf16[128,256]{1,0:T(8,128)(2,1)S(1)} %get-tuple-element.46), channel_id=1, source_target_pairs={{0,2},{1,3},{2,0},{3,1},{4,6},{5,7},{6,4},{7,5},{8,10},{9,11},{10,... | collective-permute-start | bytes 196616 | tf_op jit(solution)/shard_map/ppermute | solution.py:117
  148.3 4.8 %collective-permute-start.9 = (bf16[128,256]{1,0:T(8,128)(2,1)S(1)}, bf16[128,256]{1,0:T(8,128)(2,1)S(1)}, u32[]{:S(2)}, u32[]{:S(2)}) collective-permute-start(bf16[128,256]{1,0:T(8,128)(2,1)S(1)} %get-tuple-element.47), channel_id=1, source_target_pairs={{0,3},{1,2},{2,1},{3,0},{4,7},{5,6},{6,5},{7,4},{8,11},{9,10},{10,... | collective-permute-start | bytes 196616 | tf_op jit(solution)/shard_map/ppermute | solution.py:117

commit v4 on v3

--- a/solution.py
+++ b/solution.py
@@ -151,28 +151,32 @@
     )(own, *parts)
 
 
-def gram_kernel(key_ref, value_ref, cumul_ref, out_ref, first_ref):
-    block = pl.program_id(1)
-    keys = key_ref[...]
-    row = cumul_ref[0]
-    last = row[:, SPAN - 1 :]
-    weighted = keys.astype(F32).T * jnp.exp(last - row)
-    high, low = split(weighted)
-    both = jnp.concatenate([keys, value_ref[...]], axis=1)
-    part = dot(high, both) + dot(low, both)
-    pieces, piece = out_ref.shape[0], DH // out_ref.shape[0]
-
-    @pl.when(block == 0)
-    def _():
-        first_ref[0] = part
-        out_ref[:, :piece, :] = part.reshape(pieces, piece, 2 * DH)
-        out_ref[:, piece:, :] = jnp.broadcast_to(last[None], (pieces, 8, 2 * DH))
-
-    @pl.when(block == 1)
-    def _():
-        total = jnp.exp(last) * first_ref[0] + part
-        out_ref[:, :piece, :] = total.reshape(pieces, piece, 2 * DH)
-        out_ref[:, piece:, :] += jnp.broadcast_to(last[None], (pieces, 8, 2 * DH))
+def gram_kernel(rows_ref, cumul_ref, out_ref, first_ref):
+    heads, count = cumul_ref.shape[0], cumul_ref.shape[1]
+    pieces = out_ref.shape[0] // heads
+    piece = DH // pieces
+    for head in range(heads):
+        mine = slice(head * DH, (head + 1) * DH)
+        other = slice((heads + head) * DH, (heads + head + 1) * DH)
+        held = slice(head * pieces, (head + 1) * pieces)
+        carry, total = None, 0.0
+        for block in range(count):
+            rows = slice(block * SPAN, (block + 1) * SPAN)
+            keys = rows_ref[rows, mine]
+            row = cumul_ref[head, block : block + 1, :]
+            last = row[:, SPAN - 1 :]
+            weighted = keys.astype(F32).T * jnp.exp(last - row)
+            high, low = split(weighted)
+            both = jnp.concatenate([keys, rows_ref[rows, other]], axis=1)
+            part = dot(high, both) + dot(low, both)
+            if block == 0:
+                first_ref[head] = part
+                carry = part
+            else:
+                carry = jnp.exp(last) * carry + part
+            total = total + last
+        out_ref[held, :piece, :] = carry.reshape(pieces, piece, 2 * DH)
+        out_ref[held, piece:, :] = jnp.broadcast_to(total[None], (pieces, 8, 2 * DH))
 
 
 def scan_kernel(in_ref, out_ref, total_ref):
@@ -194,8 +198,7 @@
 
 def solve_kernel(
     own_ref,
-    key_ref,
-    value_ref,
+    rows_ref,
     cumul_ref,
     ridge_ref,
     state_ref,
@@ -204,8 +207,8 @@
 ):
     parts, rest = rest[:8], rest[8:]
     adjoint_ref, solved_ref, grad_ref, delta_ref, second_ref = rest[:5]
-    early, late, stream, mixing, gathered = rest[5:10]
-    weights, scaled, solution, residual, direction, images, rhos = zip(rest[10:17], rest[17:])
+    early, late, stream, keys_t, gathered = rest[5:10]
+    weights, solution, residual, direction, images, rhos = zip(rest[10:16], rest[16:])
     head, block = pl.program_id(0), pl.program_id(1)
     count = len(parts)
 
@@ -216,9 +219,12 @@
             start = pl.multiple_of((own_ref[0] ^ d) * size, size)
             gathered[pl.ds(start, size), :] = parts[d][...]
 
-    keys, values = key_ref[...], value_ref[...]
-    row = cumul_ref[0, pl.ds(block, 1), :]
-    first_total = cumul_ref[0, 0:1, SPAN - 1 :]
+    rows = pl.ds(pl.multiple_of(block * SPAN, SPAN), SPAN)
+    mine = pl.ds(pl.multiple_of(head * DH, DH), DH)
+    other = pl.ds(pl.multiple_of((head + 2) * DH, DH), DH)
+    keys, values = rows_ref[rows, mine], rows_ref[rows, other]
+    row = cumul_ref[head, pl.ds(block, 1), :]
+    first_total = cumul_ref[head, 0:1, SPAN - 1 :]
     column = column_of(row)
     start_decay = jnp.exp(row)
     ridge = ridge_ref[head]
@@ -230,19 +236,19 @@
     is_late = block == 1
     entry = jnp.where(is_late, jnp.exp(first_total), 1.0)
     local = jnp.where(is_late, 1.0, 0.0)
-    state = entry * state_ref[...] + local * first_ref[0]
+    state = entry * state_ref[mine] + local * first_ref[head]
     gram_high, gram_low = split(state[:, :DH])
     value_high, value_low = split(state[:, DH:])
-    stream[:HALF] = keys[HALF:]
-    stream[HALF:] = keys[:HALF]
+    zero = jnp.zeros((HALF, DH), BF16)
+    stream[0:HALF] = jnp.concatenate([keys[HALF:], zero], axis=1)
+    stream[HALF:SPAN] = jnp.concatenate([keys[:HALF], zero], axis=1)
+    stream[SPAN : SPAN + DH] = jnp.concatenate([gram_high, gram_high], axis=1)
+    stream[SPAN + DH :] = jnp.concatenate([gram_low, gram_low], axis=1)
     key_t = keys.astype(F32).T.astype(BF16)
-    mixing[:, 3 * DH : 3 * DH + HALF] = key_t[:, HALF:]
-    mixing[:, 3 * DH + HALF :] = key_t[:, :HALF]
-    mixing[:, : 3 * DH] = jnp.concatenate([gram_high, gram_high, gram_low], axis=1)
-
-    rows = pl.ds(pl.multiple_of(block * SPAN, SPAN), SPAN)
-    queries = gathered[rows, pl.ds(pl.multiple_of(head * DH, DH), DH)]
-    grads = gathered[rows, pl.ds(pl.multiple_of((head + 2) * DH, DH), DH)]
+    keys_t[:, :HALF] = key_t[:, HALF:]
+    keys_t[:, HALF:] = key_t[:, :HALF]
+
+    queries, grads = gathered[rows, mine], gathered[rows, other]
     grad_ref[...] = grads
 
     query_t = queries.astype(F32).T
@@ -254,21 +260,18 @@
         rhs = start_decay[:, cols] * (seen[:DH] + seen[DH:])
         if half == 0:
             masked = (early[...] * dot_t(values[:HALF], grad_half)).astype(BF16)
-            rhs = rhs + dot(mixing[:, 3 * DH + HALF :], masked)
+            rhs = rhs + dot(keys_t[:, HALF:], masked)
         else:
             turned = jnp.concatenate([values[HALF:], values[:HALF]], axis=0)
             masked = (late[...] * dot_t(turned, grad_half)).astype(BF16)
-            rhs = rhs + dot(mixing[:, 3 * DH :], masked)
+            rhs = rhs + dot(keys_t[...], masked)
         both = jnp.concatenate([query_t[:, cols], rhs], axis=1)
         solution[half][...] = jnp.zeros((DH, SPAN), F32)
         residual[half][...] = both
         direction[half][...] = both
-        decay = start_decay[:, cols]
-        high, low = split(jnp.concatenate([decay, decay], axis=1) * both)
-        weights[half][...] = both.astype(BF16)
-        scaled[half][:DH] = high
-        scaled[half][DH : 2 * DH] = low
-        scaled[half][2 * DH :] = high
+        high, low = split(both)
+        weights[half][:DH] = high
+        weights[half][DH:] = low
 
     groups = [slice(g * 16, (g + 1) * 16) for g in range(DH // 16)]
 
@@ -287,9 +290,9 @@
         seen = dot(stream[begin:], weights[half][...])
         yield
         scores = []
-        for start in range(0, count, 16):
-            within = tile[start : start + 16]
-            part = seen[start : start + 16]
+        for start in range(0, count, 32):
+            within = tile[start : start + 32]
+            part = seen[start : start + 32]
             scores.append(
                 jnp.concatenate(
                     [
@@ -300,23 +303,20 @@
                 )
             )
             yield
-        if half == 0:
-            left = jnp.concatenate([mixing[:, : 3 * DH], mixing[:, 3 * DH + HALF :]], axis=1)
-        else:
-            left = mixing[...]
-        images[half][...] = dot(left, jnp.concatenate([scaled[half][...]] + scores, axis=0))
+        decay = start_decay[:, half * HALF : (half + 1) * HALF]
+        decay = jnp.concatenate([decay, decay], axis=1)
+        image = dot(keys_t[:, begin:], jnp.concatenate(scores, axis=0))
+        for g in groups:
+            gram = seen[count + g.start : count + g.stop] + seen[count + DH + g.start : count + DH + g.stop]
+            images[half][g, :] = image[g] + decay * gram + ridge * direction[half][g, :]
         yield
 
     def update(half, last=False):
         rho = rhos[half][...]
-        decay = start_decay[:, half * HALF : (half + 1) * HALF]
-        decay = jnp.concatenate([decay, decay], axis=1)
         along = 0.0
         for g in groups:
             way = direction[half][g, :]
-            image = images[half][g, :] + ridge * way
-            images[half][g, :] = image
-            along = along + way * image
+            along = along + way * images[half][g, :]
             yield
         step = rho / (jnp.sum(along, axis=0, keepdims=True) + EPSILON)
         norm = 0.0
@@ -335,11 +335,9 @@
         for g in groups:
             way = residual[half][g, :] + turn * direction[half][g, :]
             direction[half][g, :] = way
-            weights[half][g, :] = way.astype(BF16)
-            high, low = split(decay * way)
-            scaled[half][g, :] = high
-            scaled[half][DH + g.start : DH + g.stop, :] = low
-            scaled[half][2 * DH + g.start : 2 * DH + g.stop, :] = high
+            high, low = split(way)
+            weights[half][g, :] = high
+            weights[half][DH + g.start : DH + g.stop, :] = low
             yield
 
     def weave(multiplying, updating, ratio):
@@ -356,7 +354,7 @@
 
     def sweep(_, carry):
         weave(multiply(1), update(0), 1)
-        weave(multiply(0), update(1), 1)
+        weave(multiply(0), update(1), 2)
         return carry
 
     lax.fori_loop(0, SOLVE_STEPS - 1, sweep, 0, unroll=True)
@@ -383,53 +381,51 @@
         second_ref[0] = back
 
 
-def local_kernel(key_ref, value_ref, grad_ref, solved_ref, adjoint_ref, cumul_ref, key_out, value_out):
-    block = pl.program_id(1)
-    keys, values, grads = key_ref[...], value_ref[...], grad_ref[...]
-    solved, adjoint = solved_ref[...], adjoint_ref[...]
-    row = cumul_ref[0, pl.ds(block, 1), :]
-    column = column_of(row)
-    left = jnp.concatenate([values, keys], axis=1)
-    right = jnp.concatenate([grads, -adjoint], axis=1)
-    both = jnp.concatenate([grads, adjoint], axis=1)
-    for half in range(2):
-        mine = slice(half * HALF, (half + 1) * HALF)
-        after = slice(half * HALF, SPAN)
-        within = decay_tile(row, column, half * HALF, HALF, half * HALF, SPAN - half * HALF)
-        along_solved = (within * dot_t(keys[mine], solved[after])).astype(BF16)
-        along = (within * dot_t(left[mine], right[after])).astype(BF16)
-        seen = dot(along_solved, both[after])
-        value_out[mine] = seen[:, :DH]
-        key_out[mine] = dot(along, solved[after]) - seen[:, DH:]
-
-
-def final_kernel(key_ref, value_ref, state_ref, second_ref, cumul_ref, key_local, value_local, out_ref):
-    block, head = pl.program_id(0), pl.program_id(1)
-    row = cumul_ref[0, pl.ds(block, 1), :]
-    last = cumul_ref[0, 1:2, SPAN - 1 :]
-    weight = column_of(jnp.exp(row[:, SPAN - 1 :] - row))
+def local_kernel(rows_ref, grad_ref, solved_ref, adjoint_ref, cumul_ref, key_out, value_out):
+    block = pl.program_id(0)
+    heads = cumul_ref.shape[0]
+    for head in range(heads):
+        here = slice(head * DH, (head + 1) * DH)
+        other = slice((heads + head) * DH, (heads + head + 1) * DH)
+        keys, values, grads = rows_ref[:, here], rows_ref[:, other], grad_ref[:, here]
+        solved, adjoint = solved_ref[:, here], adjoint_ref[:, here]
+        row = cumul_ref[head, pl.ds(block, 1), :]
+        column = column_of(row)
+        left = jnp.concatenate([values, keys], axis=1)
+        right = jnp.concatenate([grads, -adjoint], axis=1)
+        both = jnp.concatenate([grads, adjoint], axis=1)
+        for half in range(2):
+            mine = slice(half * HALF, (half + 1) * HALF)
+            after = slice(half * HALF, SPAN)
+            within = decay_tile(row, column, half * HALF, HALF, half * HALF, SPAN - half * HALF)
+            along_solved = (within * dot_t(keys[mine], solved[after])).astype(BF16)
+            along = (within * dot_t(left[mine], right[after])).astype(BF16)
+            seen = dot(along_solved, both[after])
+            value_out[mine, here] = seen[:, :DH]
+            key_out[mine, here] = dot(along, solved[after]) - seen[:, DH:]
+
+
+def final_kernel(rows_ref, state_ref, second_ref, cumul_ref, key_local, value_local, out_ref):
+    block = pl.program_id(0)
+    heads = cumul_ref.shape[0]
     is_early = block == 0
-    entry = jnp.where(is_early, jnp.exp(last), 1.0)
     local = jnp.where(is_early, 1.0, 0.0)
-    state = entry * state_ref[...] + local * second_ref[0]
-    value_t, gram = state[:, :DH], state[:, DH:]
-    upper = jnp.concatenate([value_t, gram + gram.T], axis=1)
-    lower = jnp.concatenate([jnp.zeros((DH, DH), F32), value_t.T], axis=1)
-    high, low = split(jnp.concatenate([upper, lower], axis=0))
-    both = jnp.concatenate([key_ref[...], value_ref[...]], axis=1)
-    seen = dot(both, high) + dot(both, low)
-    key_part = (key_local[...] + weight * seen[:, DH:]).astype(BF16)
-    value_part = (value_local[...] + weight * seen[:, :DH]).astype(BF16)
-
-    @pl.when(head == 0)
-    def _():
-        out_ref[:, :DH] = key_part
-        out_ref[:, 2 * DH : 3 * DH] = value_part
-
-    @pl.when(head == 1)
-    def _():
-        out_ref[:, DH : 2 * DH] = key_part
-        out_ref[:, 3 * DH :] = value_part
+    for head in range(heads):
+        mine = slice(head * DH, (head + 1) * DH)
+        other = slice((heads + head) * DH, (heads + head + 1) * DH)
+        row = cumul_ref[head, pl.ds(block, 1), :]
+        last = cumul_ref[head, 1:2, SPAN - 1 :]
+        weight = column_of(jnp.exp(row[:, SPAN - 1 :] - row))
+        entry = jnp.where(is_early, jnp.exp(last), 1.0)
+        state = entry * state_ref[mine] + local * second_ref[head]
+        value_t, gram = state[:, :DH], state[:, DH:]
+        upper = jnp.concatenate([value_t, gram + gram.T], axis=1)
+        lower = jnp.concatenate([jnp.zeros((DH, DH), F32), value_t.T], axis=1)
+        high, low = split(jnp.concatenate([upper, lower], axis=0))
+        both = jnp.concatenate([rows_ref[:, mine], rows_ref[:, other]], axis=1)
+        seen = dot(both, high) + dot(both, low)
+        out_ref[:, mine] = (key_local[:, mine] + weight * seen[:, DH:]).astype(BF16)
+        out_ref[:, other] = (value_local[:, mine] + weight * seen[:, :DH]).astype(BF16)
 
 
 def swap(pieces, axis):
@@ -461,19 +457,9 @@
     out, first_state = pl.pallas_call(
         gram_kernel,
         name="gram",
-        grid=grid,
-        in_specs=[
-            low_spec,
-            high_spec,
-            pl.BlockSpec((1, 1, SPAN), lambda h, b: (h * count + b, 0, 0)),
-        ],
-        out_specs=[
-            pl.BlockSpec((number // head_dev, piece + 8, 2 * DH), lambda h, b: (h, 0, 0)),
-            local_spec,
-        ],
         out_shape=[jax.ShapeDtypeStruct((number, piece + 8, 2 * DH), F32), local_hbm],
         compiler_params=grant(6),
-    )(first, first, cumul.reshape(head_dev * count, 1, SPAN))
+    )(first, cumul)
     prefix, factors = pl.pallas_call(
         scan_kernel,
         name="scan",
@@ -492,12 +478,11 @@
         grid=grid,
         in_specs=[
             pl.BlockSpec(memory_space=pltpu.SMEM),
-            low_spec,
-            high_spec,
-            cumul_spec,
+            pl.BlockSpec(memory_space=pltpu.VMEM),
+            pl.BlockSpec(memory_space=pltpu.VMEM),
             pl.BlockSpec(memory_space=pltpu.SMEM),
-            state_spec,
-            local_spec,
+            pl.BlockSpec(memory_space=pltpu.VMEM),
+            pl.BlockSpec(memory_space=pltpu.VMEM),
         ]
         + [pl.BlockSpec(memory_space=pltpu.VMEM)] * heads,
         out_specs=[low_spec, low_spec, low_spec, state_spec, local_spec],
@@ -505,13 +490,12 @@
         scratch_shapes=[
             pltpu.VMEM((HALF, HALF), F32),
             pltpu.VMEM((SPAN, HALF), F32),
-            pltpu.VMEM((SPAN, DH), BF16),
-            pltpu.VMEM((DH, SPAN + 3 * DH), BF16),
+            pltpu.VMEM((SPAN + 2 * DH, 2 * DH), BF16),
+            pltpu.VMEM((DH, SPAN), BF16),
             pltpu.VMEM((tokens, 2 * head_dev * DH), BF16),
         ]
         + [
-            pltpu.VMEM((DH, SPAN), BF16),
-            pltpu.VMEM((3 * DH, SPAN), BF16),
+            pltpu.VMEM((2 * DH, SPAN), BF16),
             pltpu.VMEM((DH, SPAN), F32),
             pltpu.VMEM((DH, SPAN), F32),
             pltpu.VMEM((DH, SPAN), F32),
@@ -520,19 +504,30 @@
         ]
         * 2,
         compiler_params=grant(12),
-    )(own, first, first, cumul, in_hbm(ridge), state, first_state, *parts)
+    )(own, first, cumul, in_hbm(ridge), state, first_state, *parts)
 
     grad_queries = spread(own, trade(row_parts(own, adjoint, heads), "head"))
 
+    def whole(*shape):
+        return pl.BlockSpec(shape, lambda b: (0,) * len(shape))
+
+    wide_spec = pl.BlockSpec((SPAN, 2 * head_dev * DH), lambda b: (b, 0))
+    narrow_spec = pl.BlockSpec((SPAN, head_dev * DH), lambda b: (b, 0))
     key_local, value_local = pl.pallas_call(
         local_kernel,
         name="local",
-        grid=grid,
-        in_specs=[low_spec, high_spec, low_spec, low_spec, low_spec, cumul_spec],
-        out_specs=[low_spec, low_spec],
+        grid=(count,),
+        in_specs=[
+            wide_spec,
+            narrow_spec,
+            narrow_spec,
+            narrow_spec,
+            whole(head_dev, count, SPAN),
+        ],
+        out_specs=[narrow_spec, narrow_spec],
         out_shape=[pltpu.HBM((tokens, head_dev * DH), F32)] * 2,
         compiler_params=grant(10),
-    )(first, first, grads_local, solved, adjoint, cumul)
+    )(first, grads_local, solved, adjoint, cumul)
 
     suffix = pl.pallas_call(
         scan_back_kernel,
@@ -542,29 +537,22 @@
     )(swap(delta.reshape(number, piece, 2 * DH), "ctx"), factors)
     state_after = swap(suffix, "ctx").reshape(head_dev * DH, 2 * DH)
 
-    def turned(spec):
-        return pl.BlockSpec(spec.block_shape, lambda b, h: spec.index_map(h, b))
-
     grads = pl.pallas_call(
         final_kernel,
         name="final",
-        grid=(count, head_dev),
+        grid=(count,),
         in_specs=[
-            turned(spec)
-            for spec in (
-                low_spec,
-                high_spec,
-                state_spec,
-                local_spec,
-                cumul_spec,
-                low_spec,
-                low_spec,
-            )
+            wide_spec,
+            whole(head_dev * DH, 2 * DH),
+            whole(head_dev, DH, 2 * DH),
+            whole(head_dev, count, SPAN),
+            narrow_spec,
+            narrow_spec,
         ],
-        out_specs=pl.BlockSpec((SPAN, 2 * head_dev * DH), lambda b, h: (b, 0)),
+        out_specs=wide_spec,
         out_shape=jax.ShapeDtypeStruct((tokens, 2 * head_dev * DH), BF16),
         compiler_params=grant(10),
-    )(first, first, state_after, second_state, cumul, in_hbm(key_local), in_hbm(value_local))
+    )(first, state_after, second_state, cumul, in_hbm(key_local), in_hbm(value_local))
     grads = swap(grads.reshape(heads, tokens // heads, 2 * head_dev * DH), "head")
     grad_keys, grad_values = unpack(grads)
     return (grad_queries, grad_keys, grad_values)

time: 156 us -> 151 us (0.968)
  Pallas kernels: 44.5 us -> 38.8 us
    pallas_call x3, Pallas kernels: 12 us -> 8.05 us  [the longest x1 3.35 us: shards(): pl.pallas_call(local_kernel, name='local', grid=(count,), in_specs=[wide_...]
    pallas_call x1, Pallas kernels: 25.9 us -> 24.1 us  [shards(): pl.pallas_call(solve_kernel, name='solve', grid=grid, in_specs=[pl.BlockS...]
where the time goes in v4:
time: 151 us; the launch traced here: 150 us
  waiting for transfers between devices  47.4 us (31%)
  starting transfers between devices  45.9 us (30%)
  Pallas kernels  38.8 us (26%)
  blocking collectives  14.8 us (10%)
  other arithmetic  1.65 us (1%)
    all_to_all x5, starting transfers between devices, swap(): return lax.all_to_all(pieces, axis, split_axis=0, concat_axis=0, tiled=True)  27.4 us
    ppermute x14, waiting for transfers between devices, trade(): out.append(lax.ppermute(parts[d], axis, [(i, i ^ d) for i in range(count)]))  24.3 us
    pallas_call x1, Pallas kernels, shards(): pl.pallas_call(solve_kernel, name='solve', grid=grid, in_specs=[pl.BlockS...  24.1 us
    all_to_all x5, waiting for transfers between devices, swap(): return lax.all_to_all(pieces, axis, split_axis=0, concat_axis=0, tiled=True)  23.1 us
    ppermute x14, starting transfers between devices, trade(): out.append(lax.ppermute(parts[d], axis, [(i, i ^ d) for i in range(count)]))  18.4 us
    all_to_all x1, blocking collectives, swap(): return lax.all_to_all(pieces, axis, split_axis=0, concat_axis=0, tiled=True)  14.8 us
    pallas_call x1, Pallas kernels, shards(): pl.pallas_call(local_kernel, name='local', grid=(count,), in_specs=[wide_...  3.35 us
    pallas_call x1, Pallas kernels, shards(): pl.pallas_call(final_kernel, name='final', grid=(count,), in_specs=[wide_...  3.34 us
  transfers between devices with their start and end apart: 19, of which 11 were waited for; matrix products, arithmetic and copies ran while one was open for 1% of the time, Pallas kernels for 4%

profile of v4, /device:TPU:1, one launch (start us, length us, event | category | flops | bytes accessed | tf_op | source)
XLA Modules:
  0.0 150.2 jit_solution(13065622590872154257)
XLA Ops:
  0.6 2.3 %pack.1 = bf16[8,128,512]{2,1,0:T(8,128)(2,1)} custom-call(bf16[128,2048]{1,0:T(8,128)(2,1)} %a_ref.2, bf16[128,2048]{1,0:T(8,128)(2,1)} %b_ref.2), custom_call_target="tpu_custom_call" | custom-call | tf_op jit(solution)/shard_map/pack/pallas_call | solution.py:70
  2.9 6.1 %all-to-all-start = ((bf16[8,128,512]{2,1,0:T(8,128)(2,1)}), bf16[8,128,512]{2,1,0:T(8,128)(2,1)S(1)}, u32[]{:S(2)}, u32[]{:S(2)}) async-start(bf16[8,128,512]{2,1,0:T(8,128)(2,1)} %pack.1), calls=%async_computation | async-start | bytes 2097152 | tf_op jit(solution)/shard_map/all_to_all | solution.py:432
  9.0 1.2 reduce-window.6
  10.2 0.2 slice_reduce_fusion
  10.4 0.3 reduce-window.9
  10.7 0.1 broadcast_add_fusion
  10.8 13.1 %all-to-all-done = bf16[8,128,512]{2,1,0:T(8,128)(2,1)S(1)} async-done(((bf16[8,128,512]{2,1,0:T(8,128)(2,1)}), bf16[8,128,512]{2,1,0:T(8,128)(2,1)S(1)}, u32[]{:S(2)}, u32[]{:S(2)}) %all-to-all-start) | async-done | bytes 1048608 | tf_op jit(solution)/shard_map/all_to_all | solution.py:432
  24.0 1.4 gram.1
  25.3 7.7 %all-to-all-start.1 = ((f32[16,24,256]{2,1,0:T(8,128)}), f32[16,24,256]{2,1,0:T(8,128)S(1)}, u32[]{:S(2)}, u32[]{:S(2)}) async-start(f32[16,24,256]{2,1,0:T(8,128)} %get-tuple-element.32), calls=%async_computation.1 | async-start | bytes 786432 | tf_op jit(solution)/shard_map/all_to_all | solution.py:432
  33.1 0.8 column_parts.1
  33.9 0.7 copy-done.7
  34.6 1.3 collective-permute-start
  35.8 0.3 collective-permute-start.1
  36.1 5.9 %all-to-all-done.1.in_ref = f32[16,24,256]{2,1,0:T(8,128)S(1)} async-done(((f32[16,24,256]{2,1,0:T(8,128)}), f32[16,24,256]{2,1,0:T(8,128)S(1)}, u32[]{:S(2)}, u32[]{:S(2)}) %all-to-all-start.1) | async-done | bytes 393248 | tf_op jit(solution)/shard_map/all_to_all | solution.py:432
  42.0 0.7 scan.1
  42.7 3.7 %all-to-all-start.2 = ((f32[16,16,256]{2,1,0:T(8,128)}), f32[16,16,256]{2,1,0:T(8,128)S(1)}, u32[]{:S(2)}, u32[]{:S(2)}) async-start(f32[16,16,256]{2,1,0:T(8,128)} %get-tuple-element.33), calls=%async_computation.2 | async-start | bytes 524288 | tf_op jit(solution)/shard_map/all_to_all | solution.py:432
  46.4 2.4 %collective-permute-start.2 = (bf16[128,512]{1,0:T(8,128)(2,1)}, bf16[128,512]{1,0:T(8,128)(2,1)S(1)}, u32[]{:S(2)}, u32[]{:S(2)}) collective-permute-start(bf16[128,512]{1,0:T(8,128)(2,1)} %get-tuple-element.38), channel_id=1, source_target_pairs={{0,3},{1,2},{2,1},{3,0},{4,7},{5,6},{6,5},{7,4},{8,11},{9,10},{10,... | collective-permute-start | bytes 393224 | tf_op jit(solution)/shard_map/ppermute | solution.py:117
  48.8 1.8 %collective-permute-start.3 = (bf16[128,512]{1,0:T(8,128)(2,1)S(1)}, bf16[128,512]{1,0:T(8,128)(2,1)S(1)}, u32[]{:S(2)}, u32[]{:S(2)}) collective-permute-start(bf16[128,512]{1,0:T(8,128)(2,1)S(1)} %copy-done.8), channel_id=1, source_target_pairs={{0,4},{1,5},{2,6},{3,7},{4,0},{5,1},{6,2},{7,3},{8,12},{9,13},{10,... | collective-permute-start | bytes 393224 | tf_op jit(solution)/shard_map/ppermute | solution.py:117
  50.6 1.3 collective-permute-start.4
  51.8 0.0 collective-permute-done.rest_1_
  51.8 0.9 collective-permute-start.5
  52.7 0.0 collective-permute-done.1.rest_2_
  52.7 2.3 %collective-permute-start.6 = (bf16[128,512]{1,0:T(8,128)(2,1)S(1)}, bf16[128,512]{1,0:T(8,128)(2,1)S(1)}, u32[]{:S(2)}, u32[]{:S(2)}) collective-permute-start(bf16[128,512]{1,0:T(8,128)(2,1)S(1)} %get-tuple-element.42), channel_id=1, source_target_pairs={{0,7},{1,6},{2,5},{3,4},{4,3},{5,2},{6,1},{7,0},{8,15},{9,14},{10,... | collective-permute-start | bytes 393224 | tf_op jit(solution)/shard_map/ppermute | solution.py:117
  55.0 1.5 %collective-permute-done.3.rest_4_ = bf16[128,512]{1,0:T(8,128)(2,1)S(1)} collective-permute-done((bf16[128,512]{1,0:T(8,128)(2,1)S(1)}, bf16[128,512]{1,0:T(8,128)(2,1)S(1)}, u32[]{:S(2)}, u32[]{:S(2)}) %collective-permute-start.3) | collective-permute-done | bytes 131104 | tf_op jit(solution)/shard_map/ppermute | solution.py:117
  56.5 2.5 %collective-permute-done.4.rest_5_ = bf16[128,512]{1,0:T(8,128)(2,1)S(1)} collective-permute-done((bf16[128,512]{1,0:T(8,128)(2,1)S(1)}, bf16[128,512]{1,0:T(8,128)(2,1)S(1)}, u32[]{:S(2)}, u32[]{:S(2)}) %collective-permute-start.4) | collective-permute-done | bytes 131104 | tf_op jit(solution)/shard_map/ppermute | solution.py:117
  59.0 2.9 %collective-permute-done.5.rest_6_ = bf16[128,512]{1,0:T(8,128)(2,1)S(1)} collective-permute-done((bf16[128,512]{1,0:T(8,128)(2,1)S(1)}, bf16[128,512]{1,0:T(8,128)(2,1)S(1)}, u32[]{:S(2)}, u32[]{:S(2)}) %collective-permute-start.5) | collective-permute-done | bytes 131104 | tf_op jit(solution)/shard_map/ppermute | solution.py:117
  61.9 2.8 %collective-permute-done.6.rest_7_ = bf16[128,512]{1,0:T(8,128)(2,1)S(1)} collective-permute-done((bf16[128,512]{1,0:T(8,128)(2,1)S(1)}, bf16[128,512]{1,0:T(8,128)(2,1)S(1)}, u32[]{:S(2)}, u32[]{:S(2)}) %collective-permute-start.6) | collective-permute-done | bytes 131104 | tf_op jit(solution)/shard_map/ppermute | solution.py:117
  64.7 24.1 %solve.1 = (bf16[1024,256]{1,0:T(8,128)(2,1)}, bf16[1024,256]{1,0:T(8,128)(2,1)}, bf16[1024,256]{1,0:T(8,128)(2,1)}, f32[256,256]{1,0:T(8,128)S(1)}, f32[2,128,256]{2,1,0:T(8,128)}) custom-call(s32[1]{0:T(128)} %bitcast.own_ref, bf16[1024,512]{1,0:T(8,128)(2,1)S(1)} %bitcast.8, f32[2,2,512]{2,1,0:T(2,128)S(1)} %reduce_window_sum.16.cumul_ref, f32[2]{0:T(128)} %ridge_ref.1, ...), custom_call_target="tpu_custom_call" | custom-call | tf_op jit(solution)/shard_map/solve/pallas_call | solution.py:475
  88.8 14.8 %all_to_all.30.in_ref = f32[16,16,256]{2,1,0:T(8,128)S(1)} all-to-all(f32[16,16,256]{2,1,0:T(8,128)S(1)} %bitcast.13), channel_id=1, replica_groups=mesh['ctx'=16,'head'=8] {'ctx'}, dimensions={0} | all-to-all | bytes 524288 | tf_op jit(solution)/shard_map/all_to_all | solution.py:432
  103.7 0.8 scan_back.1
  104.4 3.5 %all-to-all-start.4 = ((f32[16,16,256]{2,1,0:T(8,128)}), f32[16,16,256]{2,1,0:T(8,128)S(1)}, u32[]{:S(2)}, u32[]{:S(2)}) async-start(f32[16,16,256]{2,1,0:T(8,128)} %scan_back.1), calls=%async_computation.4 | async-start | bytes 524288 | tf_op jit(solution)/shard_map/all_to_all | solution.py:432
  108.0 3.4 %local.1 = (f32[1024,256]{1,0:T(8,128)}, f32[1024,256]{1,0:T(8,128)}) custom-call(bf16[1024,512]{1,0:T(8,128)(2,1)S(1)} %bitcast.9, bf16[1024,256]{1,0:T(8,128)(2,1)S(1)} %copy-done.2, bf16[1024,256]{1,0:T(8,128)(2,1)S(1)} %copy-done.1, bf16[1024,256]{1,0:T(8,128)(2,1)S(1)} %copy-done, f32[2,2,512]{2,1,0:T(2,128)S(1)} %reduce_window_sum.16.cumul_ref), custom_call_target="tpu_custom_call" | custom-call | tf_op jit(solution)/shard_map/local/pallas_call | solution.py:516
  111.4 4.1 %all-to-all-done.4 = f32[16,16,256]{2,1,0:T(8,128)S(1)} async-done(((f32[16,16,256]{2,1,0:T(8,128)}), f32[16,16,256]{2,1,0:T(8,128)S(1)}, u32[]{:S(2)}, u32[]{:S(2)}) %all-to-all-start.4) | async-done | bytes 262176 | tf_op jit(solution)/shard_map/all_to_all | solution.py:432
  115.5 3.3 %final.1 = bf16[1024,512]{1,0:T(8,128)(2,1)} custom-call(bf16[1024,512]{1,0:T(8,128)(2,1)S(1)} %bitcast.10, f32[256,256]{1,0:T(8,128)S(1)} %bitcast.12, f32[2,128,256]{2,1,0:T(8,128)S(1)} %copy-done.6, f32[2,2,512]{2,1,0:T(2,128)S(1)} %reduce_window_sum.16.cumul_ref, f32[1024,256]{1,0:T(8,128)} %get-tuple-element.57.key_local, ...), custom_call_target="tpu_custom_call" | custom-call | tf_op jit(solution)/shard_map/final/pallas_call | solution.py:540
  118.8 6.4 %all-to-all-start.5 = ((bf16[8,128,512]{2,1,0:T(8,128)(2,1)}), bf16[8,128,512]{2,1,0:T(8,128)(2,1)S(1)}, u32[]{:S(2)}, u32[]{:S(2)}) async-start(bf16[8,128,512]{2,1,0:T(8,128)(2,1)} %bitcast.5), calls=%async_computation.5 | async-start | bytes 2097152 | tf_op jit(solution)/shard_map/all_to_all | solution.py:432
  125.3 2.9 %collective-permute-start.10 = (bf16[128,256]{1,0:T(8,128)(2,1)S(1)}, bf16[128,256]{1,0:T(8,128)(2,1)S(1)}, u32[]{:S(2)}, u32[]{:S(2)}) collective-permute-start(bf16[128,256]{1,0:T(8,128)(2,1)S(1)} %get-tuple-element.48), channel_id=1, source_target_pairs={{0,4},{1,5},{2,6},{3,7},{4,0},{5,1},{6,2},{7,3},{8,12},{9,13},{10,... | collective-permute-start | bytes 196616 | tf_op jit(solution)/shard_map/ppermute | solution.py:117
  128.2 0.4 collective-permute-start.11
  128.6 2.9 %collective-permute-start.12 = (bf16[128,256]{1,0:T(8,128)(2,1)S(1)}, bf16[128,256]{1,0:T(8,128)(2,1)S(1)}, u32[]{:S(2)}, u32[]{:S(2)}) collective-permute-start(bf16[128,256]{1,0:T(8,128)(2,1)S(1)} %get-tuple-element.50), channel_id=1, source_target_pairs={{0,6},{1,7},{2,4},{3,5},{4,2},{5,3},{6,0},{7,1},{8,14},{9,15},{10,... | collective-permute-start | bytes 196616 | tf_op jit(solution)/shard_map/ppermute | solution.py:117
  131.5 0.3 collective-permute-start.13
  131.7 0.1 collective-permute-start.7
  131.8 9.8 %collective-permute-done.10.refs_4_ = bf16[128,256]{1,0:T(8,128)(2,1)S(1)} collective-permute-done((bf16[128,256]{1,0:T(8,128)(2,1)S(1)}, bf16[128,256]{1,0:T(8,128)(2,1)S(1)}, u32[]{:S(2)}, u32[]{:S(2)}) %collective-permute-start.10) | collective-permute-done | bytes 65568 | tf_op jit(solution)/shard_map/ppermute | solution.py:117
  141.7 0.3 collective-permute-start.8
  141.9 1.5 collective-permute-done.11.refs_5_
  143.4 1.5 collective-permute-start.9
  144.9 0.9 collective-permute-done.13.refs_7_
  145.8 2.4 %collective-permute-done.9.refs_3_ = bf16[128,256]{1,0:T(8,128)(2,1)S(1)} collective-permute-done((bf16[128,256]{1,0:T(8,128)(2,1)S(1)}, bf16[128,256]{1,0:T(8,128)(2,1)S(1)}, u32[]{:S(2)}, u32[]{:S(2)}) %collective-permute-start.9) | collective-permute-done | bytes 65568 | tf_op jit(solution)/shard_map/ppermute | solution.py:117
  148.2 0.8 spread.1
  149.1 1.1 unpack.1
  (28 shorter events, 0.1 us)
Async XLA Ops:
  2.9 6.1 %copy-start.9 = (f32[2,1024]{1,0:T(2,128)S(1)}, f32[2,1024]{1,0:T(2,128)}, u32[]{:S(2)}) copy-start(f32[2,1024]{1,0:T(2,128)} %param.10) | copy-start | bytes 24580
  2.9 21.1 %all-to-all-start = ((bf16[8,128,512]{2,1,0:T(8,128)(2,1)}), bf16[8,128,512]{2,1,0:T(8,128)(2,1)S(1)}, u32[]{:S(2)}, u32[]{:S(2)}) async-start(bf16[8,128,512]{2,1,0:T(8,128)(2,1)} %pack.1), calls=%async_computation | async-start | bytes 2097152 | tf_op jit(solution)/shard_map/all_to_all | solution.py:432
  24.0 9.1 %copy-start.4 = (bf16[128,2048]{1,0:T(8,128)(2,1)S(1)}, bf16[128,2048]{1,0:T(8,128)(2,1)}, u32[]{:S(2)}) copy-start(bf16[128,2048]{1,0:T(8,128)(2,1)} %b_ref.3) | copy-start | bytes 1572868
  25.3 7.8 %copy-start.3 = (bf16[128,2048]{1,0:T(8,128)(2,1)S(1)}, bf16[128,2048]{1,0:T(8,128)(2,1)}, u32[]{:S(2)}) copy-start(bf16[128,2048]{1,0:T(8,128)(2,1)} %a_ref.3) | copy-start | bytes 1572868
  25.3 16.7 %all-to-all-start.1 = ((f32[16,24,256]{2,1,0:T(8,128)}), f32[16,24,256]{2,1,0:T(8,128)S(1)}, u32[]{:S(2)}, u32[]{:S(2)}) async-start(f32[16,24,256]{2,1,0:T(8,128)} %get-tuple-element.32), calls=%async_computation.1 | async-start | bytes 786432 | tf_op jit(solution)/shard_map/all_to_all | solution.py:432
  33.9 0.7 copy-start.7
  34.6 17.3 %collective-permute-start = (bf16[128,512]{1,0:T(8,128)(2,1)}, bf16[128,512]{1,0:T(8,128)(2,1)S(1)}, u32[]{:S(2)}, u32[]{:S(2)}) collective-permute-start(bf16[128,512]{1,0:T(8,128)(2,1)} %get-tuple-element.36), channel_id=1, source_target_pairs={{0,1},{1,0},{2,3},{3,2},{4,5},{5,4},{6,7},{7,6},{8,9},{9,8},{10,11... | collective-permute-start | bytes 393224 | tf_op jit(solution)/shard_map/ppermute | solution.py:117
  35.8 16.9 %collective-permute-start.1 = (bf16[128,512]{1,0:T(8,128)(2,1)}, bf16[128,512]{1,0:T(8,128)(2,1)S(1)}, u32[]{:S(2)}, u32[]{:S(2)}) collective-permute-start(bf16[128,512]{1,0:T(8,128)(2,1)} %get-tuple-element.37), channel_id=1, source_target_pairs={{0,2},{1,3},{2,0},{3,1},{4,6},{5,7},{6,4},{7,5},{8,10},{9,11},{10,... | collective-permute-start | bytes 393224 | tf_op jit(solution)/shard_map/ppermute | solution.py:117
  42.7 6.0 %copy-start.8 = (bf16[128,512]{1,0:T(8,128)(2,1)S(1)}, bf16[128,512]{1,0:T(8,128)(2,1)}, u32[]{:S(2)}) copy-start(bf16[128,512]{1,0:T(8,128)(2,1)} %copy-done.7) | copy-start | bytes 393220
  42.7 22.0 %copy-start.5 = (f32[2,128,256]{2,1,0:T(8,128)S(1)}, f32[2,128,256]{2,1,0:T(8,128)}, u32[]{:S(2)}) copy-start(f32[2,128,256]{2,1,0:T(8,128)} %get-tuple-element.34.first_ref) | copy-start | bytes 786436
  42.7 22.0 %all-to-all-start.2 = ((f32[16,16,256]{2,1,0:T(8,128)}), f32[16,16,256]{2,1,0:T(8,128)S(1)}, u32[]{:S(2)}, u32[]{:S(2)}) async-start(f32[16,16,256]{2,1,0:T(8,128)} %get-tuple-element.33), calls=%async_computation.2 | async-start | bytes 524288 | tf_op jit(solution)/shard_map/all_to_all | solution.py:432
  46.4 8.6 %collective-permute-start.2 = (bf16[128,512]{1,0:T(8,128)(2,1)}, bf16[128,512]{1,0:T(8,128)(2,1)S(1)}, u32[]{:S(2)}, u32[]{:S(2)}) collective-permute-start(bf16[128,512]{1,0:T(8,128)(2,1)} %get-tuple-element.38), channel_id=1, source_target_pairs={{0,3},{1,2},{2,1},{3,0},{4,7},{5,6},{6,5},{7,4},{8,11},{9,10},{10,... | collective-permute-start | bytes 393224 | tf_op jit(solution)/shard_map/ppermute | solution.py:117
  48.8 7.8 %collective-permute-start.3 = (bf16[128,512]{1,0:T(8,128)(2,1)S(1)}, bf16[128,512]{1,0:T(8,128)(2,1)S(1)}, u32[]{:S(2)}, u32[]{:S(2)}) collective-permute-start(bf16[128,512]{1,0:T(8,128)(2,1)S(1)} %copy-done.8), channel_id=1, source_target_pairs={{0,4},{1,5},{2,6},{3,7},{4,0},{5,1},{6,2},{7,3},{8,12},{9,13},{10,... | collective-permute-start | bytes 393224 | tf_op jit(solution)/shard_map/ppermute | solution.py:117
  50.6 8.5 %collective-permute-start.4 = (bf16[128,512]{1,0:T(8,128)(2,1)S(1)}, bf16[128,512]{1,0:T(8,128)(2,1)S(1)}, u32[]{:S(2)}, u32[]{:S(2)}) collective-permute-start(bf16[128,512]{1,0:T(8,128)(2,1)S(1)} %get-tuple-element.40), channel_id=1, source_target_pairs={{0,5},{1,4},{2,7},{3,6},{4,1},{5,0},{6,3},{7,2},{8,13},{9,12},{10,... | collective-permute-start | bytes 393224 | tf_op jit(solution)/shard_map/ppermute | solution.py:117
  51.8 10.1 %collective-permute-start.5 = (bf16[128,512]{1,0:T(8,128)(2,1)S(1)}, bf16[128,512]{1,0:T(8,128)(2,1)S(1)}, u32[]{:S(2)}, u32[]{:S(2)}) collective-permute-start(bf16[128,512]{1,0:T(8,128)(2,1)S(1)} %get-tuple-element.41), channel_id=1, source_target_pairs={{0,6},{1,7},{2,4},{3,5},{4,2},{5,3},{6,0},{7,1},{8,14},{9,15},{10,... | collective-permute-start | bytes 393224 | tf_op jit(solution)/shard_map/ppermute | solution.py:117
  52.7 12.0 %collective-permute-start.6 = (bf16[128,512]{1,0:T(8,128)(2,1)S(1)}, bf16[128,512]{1,0:T(8,128)(2,1)S(1)}, u32[]{:S(2)}, u32[]{:S(2)}) collective-permute-start(bf16[128,512]{1,0:T(8,128)(2,1)S(1)} %get-tuple-element.42), channel_id=1, source_target_pairs={{0,7},{1,6},{2,5},{3,4},{4,3},{5,2},{6,1},{7,0},{8,15},{9,14},{10,... | collective-permute-start | bytes 393224 | tf_op jit(solution)/shard_map/ppermute | solution.py:117
  88.8 19.1 %copy-start.2 = (bf16[1024,256]{1,0:T(8,128)(2,1)S(1)}, bf16[1024,256]{1,0:T(8,128)(2,1)}, u32[]{:S(2)}) copy-start(bf16[1024,256]{1,0:T(8,128)(2,1)} %get-tuple-element.55.grad_ref) | copy-start | bytes 1572868
  103.7 4.3 %copy-start = (bf16[1024,256]{1,0:T(8,128)(2,1)S(1)}, bf16[1024,256]{1,0:T(8,128)(2,1)}, u32[]{:S(2)}) copy-start(bf16[1024,256]{1,0:T(8,128)(2,1)} %get-tuple-element.43.a_ref.adjoint_ref) | copy-start | bytes 1572868
  103.7 4.3 %copy-start.1 = (bf16[1024,256]{1,0:T(8,128)(2,1)S(1)}, bf16[1024,256]{1,0:T(8,128)(2,1)}, u32[]{:S(2)}) copy-start(bf16[1024,256]{1,0:T(8,128)(2,1)} %get-tuple-element.56.solved_ref) | copy-start | bytes 1572868
  104.4 11.0 %all-to-all-start.4 = ((f32[16,16,256]{2,1,0:T(8,128)}), f32[16,16,256]{2,1,0:T(8,128)S(1)}, u32[]{:S(2)}, u32[]{:S(2)}) async-start(f32[16,16,256]{2,1,0:T(8,128)} %scan_back.1), calls=%async_computation.4 | async-start | bytes 524288 | tf_op jit(solution)/shard_map/all_to_all | solution.py:432
  108.0 7.5 %copy-start.6 = (f32[2,128,256]{2,1,0:T(8,128)S(1)}, f32[2,128,256]{2,1,0:T(8,128)}, u32[]{:S(2)}) copy-start(f32[2,128,256]{2,1,0:T(8,128)} %get-tuple-element.54.second_ref) | copy-start | bytes 786436
  118.8 30.3 %all-to-all-start.5 = ((bf16[8,128,512]{2,1,0:T(8,128)(2,1)}), bf16[8,128,512]{2,1,0:T(8,128)(2,1)S(1)}, u32[]{:S(2)}, u32[]{:S(2)}) async-start(bf16[8,128,512]{2,1,0:T(8,128)(2,1)} %bitcast.5), calls=%async_computation.5 | async-start | bytes 2097152 | tf_op jit(solution)/shard_map/all_to_all | solution.py:432
  125.3 16.4 %collective-permute-start.10 = (bf16[128,256]{1,0:T(8,128)(2,1)S(1)}, bf16[128,256]{1,0:T(8,128)(2,1)S(1)}, u32[]{:S(2)}, u32[]{:S(2)}) collective-permute-start(bf16[128,256]{1,0:T(8,128)(2,1)S(1)} %get-tuple-element.48), channel_id=1, source_target_pairs={{0,4},{1,5},{2,6},{3,7},{4,0},{5,1},{6,2},{7,3},{8,12},{9,13},{10,... | collective-permute-start | bytes 196616 | tf_op jit(solution)/shard_map/ppermute | solution.py:117
  128.2 15.2 %collective-permute-start.11 = (bf16[128,256]{1,0:T(8,128)(2,1)S(1)}, bf16[128,256]{1,0:T(8,128)(2,1)S(1)}, u32[]{:S(2)}, u32[]{:S(2)}) collective-permute-start(bf16[128,256]{1,0:T(8,128)(2,1)S(1)} %get-tuple-element.49), channel_id=1, source_target_pairs={{0,5},{1,4},{2,7},{3,6},{4,1},{5,0},{6,3},{7,2},{8,13},{9,12},{10,... | collective-permute-start | bytes 196616 | tf_op jit(solution)/shard_map/ppermute | solution.py:117
  128.6 16.3 %collective-permute-start.12 = (bf16[128,256]{1,0:T(8,128)(2,1)S(1)}, bf16[128,256]{1,0:T(8,128)(2,1)S(1)}, u32[]{:S(2)}, u32[]{:S(2)}) collective-permute-start(bf16[128,256]{1,0:T(8,128)(2,1)S(1)} %get-tuple-element.50), channel_id=1, source_target_pairs={{0,6},{1,7},{2,4},{3,5},{4,2},{5,3},{6,0},{7,1},{8,14},{9,15},{10,... | collective-permute-start | bytes 196616 | tf_op jit(solution)/shard_map/ppermute | solution.py:117
  131.5 14.4 %collective-permute-start.13 = (bf16[128,256]{1,0:T(8,128)(2,1)S(1)}, bf16[128,256]{1,0:T(8,128)(2,1)S(1)}, u32[]{:S(2)}, u32[]{:S(2)}) collective-permute-start(bf16[128,256]{1,0:T(8,128)(2,1)S(1)} %get-tuple-element.51), channel_id=1, source_target_pairs={{0,7},{1,6},{2,5},{3,4},{4,3},{5,2},{6,1},{7,0},{8,15},{9,14},{10,... | collective-permute-start | bytes 196616 | tf_op jit(solution)/shard_map/ppermute | solution.py:117
  131.7 14.1 %collective-permute-start.7 = (bf16[128,256]{1,0:T(8,128)(2,1)S(1)}, bf16[128,256]{1,0:T(8,128)(2,1)S(1)}, u32[]{:S(2)}, u32[]{:S(2)}) collective-permute-start(bf16[128,256]{1,0:T(8,128)(2,1)S(1)} %get-tuple-element.45), channel_id=1, source_target_pairs={{0,1},{1,0},{2,3},{3,2},{4,5},{5,4},{6,7},{7,6},{8,9},{9,8},{10,11... | collective-permute-start | bytes 196616 | tf_op jit(solution)/shard_map/ppermute | solution.py:117
  141.7 4.2 %collective-permute-start.8 = (bf16[128,256]{1,0:T(8,128)(2,1)S(1)}, bf16[128,256]{1,0:T(8,128)(2,1)S(1)}, u32[]{:S(2)}, u32[]{:S(2)}) collective-permute-start(bf16[128,256]{1,0:T(8,128)(2,1)S(1)} %get-tuple-element.46), channel_id=1, source_target_pairs={{0,2},{1,3},{2,0},{3,1},{4,6},{5,7},{6,4},{7,5},{8,10},{9,11},{10,... | collective-permute-start | bytes 196616 | tf_op jit(solution)/shard_map/ppermute | solution.py:117
  143.4 4.8 %collective-permute-start.9 = (bf16[128,256]{1,0:T(8,128)(2,1)S(1)}, bf16[128,256]{1,0:T(8,128)(2,1)S(1)}, u32[]{:S(2)}, u32[]{:S(2)}) collective-permute-start(bf16[128,256]{1,0:T(8,128)(2,1)S(1)} %get-tuple-element.47), channel_id=1, source_target_pairs={{0,3},{1,2},{2,1},{3,0},{4,7},{5,6},{6,5},{7,4},{8,11},{9,10},{10,... | collective-permute-start | bytes 196616 | tf_op jit(solution)/shard_map/ppermute | solution.py:117

commit v5 on v4

--- a/solution.py
+++ b/solution.py
@@ -1,3 +1,5 @@
+import functools
+
 import jax
 import jax.numpy as jnp
 from jax import lax
@@ -67,9 +69,14 @@
 
 def pack(a, b, count):
     rows, columns = a.shape
+    step = rows // 2
+    in_spec = pl.BlockSpec((step, columns), lambda i: (i, 0))
     return pl.pallas_call(
         pack_kernel,
         name="pack",
+        grid=(2,),
+        in_specs=[in_spec, in_spec],
+        out_specs=pl.BlockSpec((count, step, 2 * columns // count), lambda i: (0, i, 0)),
         out_shape=jax.ShapeDtypeStruct((count, rows, 2 * columns // count), a.dtype),
     )(a, b)
 
@@ -149,6 +156,12 @@
         + [pl.BlockSpec(memory_space=pltpu.VMEM)] * len(parts),
         out_shape=jax.ShapeDtypeStruct((rows, len(parts) * width), parts[0].dtype),
     )(own, *parts)
+
+
+def is_mark(piece, width):
+    row = lax.broadcasted_iota(jnp.int32, (DH, width), 0)
+    column = lax.broadcasted_iota(jnp.int32, (DH, width), 1)
+    return jnp.logical_and(lax.rem(row, piece) == 1, column == 0)
 
 
 def gram_kernel(rows_ref, cumul_ref, out_ref, first_ref):
@@ -175,18 +188,19 @@
             else:
                 carry = jnp.exp(last) * carry + part
             total = total + last
-        out_ref[held, :piece, :] = carry.reshape(pieces, piece, 2 * DH)
-        out_ref[held, piece:, :] = jnp.broadcast_to(total[None], (pieces, 8, 2 * DH))
+        marked = jnp.where(is_mark(piece, 2 * DH), total, carry)
+        out_ref[held] = marked.reshape(pieces, piece, 2 * DH)
 
 
 def scan_kernel(in_ref, out_ref, total_ref):
-    number, piece = out_ref.shape[0], out_ref.shape[1]
+    number = out_ref.shape[0]
     carry = jnp.zeros(out_ref.shape[1:], F32)
     for j in range(number):
         out_ref[j] = carry
-        factor = jnp.exp(in_ref[j, piece:, :])
-        total_ref[j] = factor
-        carry = factor[:1] * carry + in_ref[j, :piece, :]
+        part = in_ref[j]
+        factor = jnp.exp(part[1:2, 0:1])
+        total_ref[j] = jnp.broadcast_to(factor, (8, out_ref.shape[2]))
+        carry = factor * carry + part
 
 
 def scan_back_kernel(in_ref, total_ref, out_ref):
@@ -197,6 +211,7 @@
 
 
 def solve_kernel(
+    piece,
     own_ref,
     rows_ref,
     cumul_ref,
@@ -236,7 +251,10 @@
     is_late = block == 1
     entry = jnp.where(is_late, jnp.exp(first_total), 1.0)
     local = jnp.where(is_late, 1.0, 0.0)
-    state = entry * state_ref[mine] + local * first_ref[head]
+    state = state_ref[mine]
+    gram = state[:, :DH]
+    gram = jnp.where(is_mark(piece, DH), gram.T, gram)
+    state = entry * jnp.concatenate([gram, state[:, DH:]], axis=1) + local * first_ref[head]
     gram_high, gram_low = split(state[:, :DH])
     value_high, value_low = split(state[:, DH:])
     zero = jnp.zeros((HALF, DH), BF16)
@@ -457,7 +475,7 @@
     out, first_state = pl.pallas_call(
         gram_kernel,
         name="gram",
-        out_shape=[jax.ShapeDtypeStruct((number, piece + 8, 2 * DH), F32), local_hbm],
+        out_shape=[jax.ShapeDtypeStruct((number, piece, 2 * DH), F32), local_hbm],
         compiler_params=grant(6),
     )(first, cumul)
     prefix, factors = pl.pallas_call(
@@ -473,7 +491,7 @@
 
     token_hbm = pltpu.HBM((tokens, head_dev * DH), BF16)
     adjoint, solved, grads_local, delta, second_state = pl.pallas_call(
-        solve_kernel,
+        functools.partial(solve_kernel, piece),
         name="solve",
         grid=grid,
         in_specs=[

time: 151 us -> 150 us (level)
  no operation moved by 1% of the time
where the time goes in v5:
time: 150 us; the launch traced here: 149 us
  waiting for transfers between devices  46.7 us (31%)
  starting transfers between devices  46.2 us (31%)
  Pallas kernels  38.7 us (26%)
  blocking collectives  14.8 us (10%)
  other arithmetic  1.65 us (1%)
    all_to_all x5, starting transfers between devices, swap(): return lax.all_to_all(pieces, axis, split_axis=0, concat_axis=0, tiled=True)  27.6 us
    pallas_call x1, Pallas kernels, shards(): pl.pallas_call(functools.partial(solve_kernel, piece), name='solve', grid...  24.2 us
    ppermute x14, waiting for transfers between devices, trade(): out.append(lax.ppermute(parts[d], axis, [(i, i ^ d) for i in range(count)]))  24.2 us
    all_to_all x5, waiting for transfers between devices, swap(): return lax.all_to_all(pieces, axis, split_axis=0, concat_axis=0, tiled=True)  22.5 us
    ppermute x14, starting transfers between devices, trade(): out.append(lax.ppermute(parts[d], axis, [(i, i ^ d) for i in range(count)]))  18.6 us
    all_to_all x1, blocking collectives, swap(): return lax.all_to_all(pieces, axis, split_axis=0, concat_axis=0, tiled=True)  14.8 us
    pallas_call x1, Pallas kernels, shards(): pl.pallas_call(final_kernel, name='final', grid=(count,), in_specs=[wide_...  3.34 us
    pallas_call x1, Pallas kernels, shards(): pl.pallas_call(local_kernel, name='local', grid=(count,), in_specs=[wide_...  3.33 us
  transfers between devices with their start and end apart: 19, of which 11 were waited for; matrix products, arithmetic and copies ran while one was open for 1% of the time, Pallas kernels for 4%

profile of v5, /device:TPU:1, one launch (start us, length us, event | category | flops | bytes accessed | tf_op | source)
XLA Modules:
  0.0 149.0 jit_solution(13938819195043638100)
XLA Ops:
  0.6 2.1 %pack.1 = bf16[8,128,512]{2,1,0:T(8,128)(2,1)} custom-call(bf16[128,2048]{1,0:T(8,128)(2,1)} %a_ref.2, bf16[128,2048]{1,0:T(8,128)(2,1)} %b_ref.2), custom_call_target="tpu_custom_call" | custom-call | tf_op jit(solution)/shard_map/pack/pallas_call | solution.py:74
  2.7 6.1 %all-to-all-start = ((bf16[8,128,512]{2,1,0:T(8,128)(2,1)}), bf16[8,128,512]{2,1,0:T(8,128)(2,1)S(1)}, u32[]{:S(2)}, u32[]{:S(2)}) async-start(bf16[8,128,512]{2,1,0:T(8,128)(2,1)} %pack.1), calls=%async_computation | async-start | bytes 2097152 | tf_op jit(solution)/shard_map/all_to_all | solution.py:450
  8.8 1.2 reduce-window.6
  10.0 0.2 slice_reduce_fusion
  10.2 0.3 reduce-window.9
  10.6 0.1 broadcast_add_fusion
  10.7 13.1 %all-to-all-done = bf16[8,128,512]{2,1,0:T(8,128)(2,1)S(1)} async-done(((bf16[8,128,512]{2,1,0:T(8,128)(2,1)}), bf16[8,128,512]{2,1,0:T(8,128)(2,1)S(1)}, u32[]{:S(2)}, u32[]{:S(2)}) %all-to-all-start) | async-done | bytes 1048608 | tf_op jit(solution)/shard_map/all_to_all | solution.py:450
  23.8 1.3 gram.1
  25.1 7.7 %all-to-all-start.1 = ((f32[16,16,256]{2,1,0:T(8,128)}), f32[16,16,256]{2,1,0:T(8,128)S(1)}, u32[]{:S(2)}, u32[]{:S(2)}) async-start(f32[16,16,256]{2,1,0:T(8,128)} %get-tuple-element.32), calls=%async_computation.1 | async-start | bytes 524288 | tf_op jit(solution)/shard_map/all_to_all | solution.py:450
  32.8 0.9 column_parts.1
  33.7 1.3 collective-permute-start
  35.0 0.3 collective-permute-start.1
  35.3 5.2 %all-to-all-done.1.in_ref = f32[16,16,256]{2,1,0:T(8,128)S(1)} async-done(((f32[16,16,256]{2,1,0:T(8,128)}), f32[16,16,256]{2,1,0:T(8,128)S(1)}, u32[]{:S(2)}, u32[]{:S(2)}) %all-to-all-start.1) | async-done | bytes 262176 | tf_op jit(solution)/shard_map/all_to_all | solution.py:450
  40.5 0.8 scan.1
  41.3 3.7 %all-to-all-start.2 = ((f32[16,16,256]{2,1,0:T(8,128)}), f32[16,16,256]{2,1,0:T(8,128)S(1)}, u32[]{:S(2)}, u32[]{:S(2)}) async-start(f32[16,16,256]{2,1,0:T(8,128)} %get-tuple-element.33), calls=%async_computation.2 | async-start | bytes 524288 | tf_op jit(solution)/shard_map/all_to_all | solution.py:450
  45.0 2.5 %collective-permute-start.2 = (bf16[128,512]{1,0:T(8,128)(2,1)}, bf16[128,512]{1,0:T(8,128)(2,1)S(1)}, u32[]{:S(2)}, u32[]{:S(2)}) collective-permute-start(bf16[128,512]{1,0:T(8,128)(2,1)} %get-tuple-element.38), channel_id=1, source_target_pairs={{0,3},{1,2},{2,1},{3,0},{4,7},{5,6},{6,5},{7,4},{8,11},{9,10},{10,... | collective-permute-start | bytes 393224 | tf_op jit(solution)/shard_map/ppermute | solution.py:124
  47.5 1.8 %collective-permute-start.3 = (bf16[128,512]{1,0:T(8,128)(2,1)}, bf16[128,512]{1,0:T(8,128)(2,1)S(1)}, u32[]{:S(2)}, u32[]{:S(2)}) collective-permute-start(bf16[128,512]{1,0:T(8,128)(2,1)} %get-tuple-element.39), channel_id=1, source_target_pairs={{0,4},{1,5},{2,6},{3,7},{4,0},{5,1},{6,2},{7,3},{8,12},{9,13},{10,... | collective-permute-start | bytes 393224 | tf_op jit(solution)/shard_map/ppermute | solution.py:124
  49.3 1.3 collective-permute-start.4
  50.5 0.0 collective-permute-done.rest_1_
  50.5 0.9 collective-permute-start.5
  51.4 0.0 collective-permute-done.1.rest_2_
  51.4 2.3 %collective-permute-start.6 = (bf16[128,512]{1,0:T(8,128)(2,1)S(1)}, bf16[128,512]{1,0:T(8,128)(2,1)S(1)}, u32[]{:S(2)}, u32[]{:S(2)}) collective-permute-start(bf16[128,512]{1,0:T(8,128)(2,1)S(1)} %get-tuple-element.42), channel_id=1, source_target_pairs={{0,7},{1,6},{2,5},{3,4},{4,3},{5,2},{6,1},{7,0},{8,15},{9,14},{10,... | collective-permute-start | bytes 393224 | tf_op jit(solution)/shard_map/ppermute | solution.py:124
  53.7 0.0 collective-permute-done.2.rest_3_
  53.7 1.1 collective-permute-done.3.rest_4_
  54.8 2.9 %collective-permute-done.4.rest_5_ = bf16[128,512]{1,0:T(8,128)(2,1)S(1)} collective-permute-done((bf16[128,512]{1,0:T(8,128)(2,1)S(1)}, bf16[128,512]{1,0:T(8,128)(2,1)S(1)}, u32[]{:S(2)}, u32[]{:S(2)}) %collective-permute-start.4) | collective-permute-done | bytes 131104 | tf_op jit(solution)/shard_map/ppermute | solution.py:124
  57.6 2.9 %collective-permute-done.5.rest_6_ = bf16[128,512]{1,0:T(8,128)(2,1)S(1)} collective-permute-done((bf16[128,512]{1,0:T(8,128)(2,1)S(1)}, bf16[128,512]{1,0:T(8,128)(2,1)S(1)}, u32[]{:S(2)}, u32[]{:S(2)}) %collective-permute-start.5) | collective-permute-done | bytes 131104 | tf_op jit(solution)/shard_map/ppermute | solution.py:124
  60.5 2.8 %collective-permute-done.6.rest_7_ = bf16[128,512]{1,0:T(8,128)(2,1)S(1)} collective-permute-done((bf16[128,512]{1,0:T(8,128)(2,1)S(1)}, bf16[128,512]{1,0:T(8,128)(2,1)S(1)}, u32[]{:S(2)}, u32[]{:S(2)}) %collective-permute-start.6) | collective-permute-done | bytes 131104 | tf_op jit(solution)/shard_map/ppermute | solution.py:124
  63.3 24.2 %solve.1 = (bf16[1024,256]{1,0:T(8,128)(2,1)}, bf16[1024,256]{1,0:T(8,128)(2,1)}, bf16[1024,256]{1,0:T(8,128)(2,1)}, f32[256,256]{1,0:T(8,128)S(1)}, f32[2,128,256]{2,1,0:T(8,128)}) custom-call(s32[1]{0:T(128)} %bitcast.own_ref, bf16[1024,512]{1,0:T(8,128)(2,1)S(1)} %bitcast.8, f32[2,2,512]{2,1,0:T(2,128)S(1)} %reduce_window_sum.16.cumul_ref, f32[2]{0:T(128)} %ridge_ref.1, ...), custom_call_target="tpu_custom_call" | custom-call | tf_op jit(solution)/shard_map/solve/pallas_call | solution.py:493
  87.5 14.8 %all_to_all.30.in_ref = f32[16,16,256]{2,1,0:T(8,128)S(1)} all-to-all(f32[16,16,256]{2,1,0:T(8,128)S(1)} %bitcast.13), channel_id=1, replica_groups=mesh['ctx'=16,'head'=8] {'ctx'}, dimensions={0} | all-to-all | bytes 524288 | tf_op jit(solution)/shard_map/all_to_all | solution.py:450
  102.3 0.7 scan_back.1
  103.1 3.5 %all-to-all-start.4 = ((f32[16,16,256]{2,1,0:T(8,128)}), f32[16,16,256]{2,1,0:T(8,128)S(1)}, u32[]{:S(2)}, u32[]{:S(2)}) async-start(f32[16,16,256]{2,1,0:T(8,128)} %scan_back.1), calls=%async_computation.4 | async-start | bytes 524288 | tf_op jit(solution)/shard_map/all_to_all | solution.py:450
  106.6 3.3 %local.1 = (f32[1024,256]{1,0:T(8,128)}, f32[1024,256]{1,0:T(8,128)}) custom-call(bf16[1024,512]{1,0:T(8,128)(2,1)S(1)} %bitcast.9, bf16[1024,256]{1,0:T(8,128)(2,1)S(1)} %copy-done.2, bf16[1024,256]{1,0:T(8,128)(2,1)S(1)} %copy-done.1, bf16[1024,256]{1,0:T(8,128)(2,1)S(1)} %copy-done, f32[2,2,512]{2,1,0:T(2,128)S(1)} %reduce_window_sum.16.cumul_ref), custom_call_target="tpu_custom_call" | custom-call | tf_op jit(solution)/shard_map/local/pallas_call | solution.py:534
  110.0 4.1 %all-to-all-done.4 = f32[16,16,256]{2,1,0:T(8,128)S(1)} async-done(((f32[16,16,256]{2,1,0:T(8,128)}), f32[16,16,256]{2,1,0:T(8,128)S(1)}, u32[]{:S(2)}, u32[]{:S(2)}) %all-to-all-start.4) | async-done | bytes 262176 | tf_op jit(solution)/shard_map/all_to_all | solution.py:450
  114.1 3.3 %final.1 = bf16[1024,512]{1,0:T(8,128)(2,1)} custom-call(bf16[1024,512]{1,0:T(8,128)(2,1)S(1)} %bitcast.10, f32[256,256]{1,0:T(8,128)S(1)} %bitcast.12, f32[2,128,256]{2,1,0:T(8,128)S(1)} %copy-done.6, f32[2,2,512]{2,1,0:T(2,128)S(1)} %reduce_window_sum.16.cumul_ref, f32[1024,256]{1,0:T(8,128)} %get-tuple-element.57.key_local, ...), custom_call_target="tpu_custom_call" | custom-call | tf_op jit(solution)/shard_map/final/pallas_call | solution.py:558
  117.4 6.6 %all-to-all-start.5 = ((bf16[8,128,512]{2,1,0:T(8,128)(2,1)}), bf16[8,128,512]{2,1,0:T(8,128)(2,1)S(1)}, u32[]{:S(2)}, u32[]{:S(2)}) async-start(bf16[8,128,512]{2,1,0:T(8,128)(2,1)} %bitcast.5), calls=%async_computation.5 | async-start | bytes 2097152 | tf_op jit(solution)/shard_map/all_to_all | solution.py:450
  124.1 2.9 %collective-permute-start.10 = (bf16[128,256]{1,0:T(8,128)(2,1)S(1)}, bf16[128,256]{1,0:T(8,128)(2,1)S(1)}, u32[]{:S(2)}, u32[]{:S(2)}) collective-permute-start(bf16[128,256]{1,0:T(8,128)(2,1)S(1)} %get-tuple-element.48), channel_id=1, source_target_pairs={{0,4},{1,5},{2,6},{3,7},{4,0},{5,1},{6,2},{7,3},{8,12},{9,13},{10,... | collective-permute-start | bytes 196616 | tf_op jit(solution)/shard_map/ppermute | solution.py:124
  127.0 0.4 collective-permute-start.11
  127.4 2.9 %collective-permute-start.12 = (bf16[128,256]{1,0:T(8,128)(2,1)S(1)}, bf16[128,256]{1,0:T(8,128)(2,1)S(1)}, u32[]{:S(2)}, u32[]{:S(2)}) collective-permute-start(bf16[128,256]{1,0:T(8,128)(2,1)S(1)} %get-tuple-element.50), channel_id=1, source_target_pairs={{0,6},{1,7},{2,4},{3,5},{4,2},{5,3},{6,0},{7,1},{8,14},{9,15},{10,... | collective-permute-start | bytes 196616 | tf_op jit(solution)/shard_map/ppermute | solution.py:124
  130.2 0.3 collective-permute-start.13
  130.5 0.1 collective-permute-start.7
  130.6 9.8 %collective-permute-done.10.refs_4_ = bf16[128,256]{1,0:T(8,128)(2,1)S(1)} collective-permute-done((bf16[128,256]{1,0:T(8,128)(2,1)S(1)}, bf16[128,256]{1,0:T(8,128)(2,1)S(1)}, u32[]{:S(2)}, u32[]{:S(2)}) %collective-permute-start.10) | collective-permute-done | bytes 65568 | tf_op jit(solution)/shard_map/ppermute | solution.py:124
  140.4 0.3 collective-permute-start.8
  140.7 1.5 collective-permute-done.11.refs_5_
  142.2 1.5 %collective-permute-start.9 = (bf16[128,256]{1,0:T(8,128)(2,1)S(1)}, bf16[128,256]{1,0:T(8,128)(2,1)S(1)}, u32[]{:S(2)}, u32[]{:S(2)}) collective-permute-start(bf16[128,256]{1,0:T(8,128)(2,1)S(1)} %get-tuple-element.47), channel_id=1, source_target_pairs={{0,3},{1,2},{2,1},{3,0},{4,7},{5,6},{6,5},{7,4},{8,11},{9,10},{10,... | collective-permute-start | bytes 196616 | tf_op jit(solution)/shard_map/ppermute | solution.py:124
  143.7 0.9 collective-permute-done.13.refs_7_
  144.6 2.4 %collective-permute-done.9.refs_3_ = bf16[128,256]{1,0:T(8,128)(2,1)S(1)} collective-permute-done((bf16[128,256]{1,0:T(8,128)(2,1)S(1)}, bf16[128,256]{1,0:T(8,128)(2,1)S(1)}, u32[]{:S(2)}, u32[]{:S(2)}) %collective-permute-start.9) | collective-permute-done | bytes 65568 | tf_op jit(solution)/shard_map/ppermute | solution.py:124
  147.0 0.8 spread.1
  147.9 1.1 unpack.1
  (24 shorter events, 0.1 us)
Async XLA Ops:
  2.7 6.1 %copy-start.7 = (f32[2,1024]{1,0:T(2,128)S(1)}, f32[2,1024]{1,0:T(2,128)}, u32[]{:S(2)}) copy-start(f32[2,1024]{1,0:T(2,128)} %param.10) | copy-start | bytes 24580
  2.7 21.1 %all-to-all-start = ((bf16[8,128,512]{2,1,0:T(8,128)(2,1)}), bf16[8,128,512]{2,1,0:T(8,128)(2,1)S(1)}, u32[]{:S(2)}, u32[]{:S(2)}) async-start(bf16[8,128,512]{2,1,0:T(8,128)(2,1)} %pack.1), calls=%async_computation | async-start | bytes 2097152 | tf_op jit(solution)/shard_map/all_to_all | solution.py:450
  23.8 9.1 %copy-start.4 = (bf16[128,2048]{1,0:T(8,128)(2,1)S(1)}, bf16[128,2048]{1,0:T(8,128)(2,1)}, u32[]{:S(2)}) copy-start(bf16[128,2048]{1,0:T(8,128)(2,1)} %b_ref.3) | copy-start | bytes 1572868
  25.1 7.8 %copy-start.3 = (bf16[128,2048]{1,0:T(8,128)(2,1)S(1)}, bf16[128,2048]{1,0:T(8,128)(2,1)}, u32[]{:S(2)}) copy-start(bf16[128,2048]{1,0:T(8,128)(2,1)} %a_ref.3) | copy-start | bytes 1572868
  25.1 15.4 %all-to-all-start.1 = ((f32[16,16,256]{2,1,0:T(8,128)}), f32[16,16,256]{2,1,0:T(8,128)S(1)}, u32[]{:S(2)}, u32[]{:S(2)}) async-start(f32[16,16,256]{2,1,0:T(8,128)} %get-tuple-element.32), calls=%async_computation.1 | async-start | bytes 524288 | tf_op jit(solution)/shard_map/all_to_all | solution.py:450
  33.7 16.8 %collective-permute-start = (bf16[128,512]{1,0:T(8,128)(2,1)}, bf16[128,512]{1,0:T(8,128)(2,1)S(1)}, u32[]{:S(2)}, u32[]{:S(2)}) collective-permute-start(bf16[128,512]{1,0:T(8,128)(2,1)} %get-tuple-element.36), channel_id=1, source_target_pairs={{0,1},{1,0},{2,3},{3,2},{4,5},{5,4},{6,7},{7,6},{8,9},{9,8},{10,11... | collective-permute-start | bytes 393224 | tf_op jit(solution)/shard_map/ppermute | solution.py:124
  35.0 16.4 %collective-permute-start.1 = (bf16[128,512]{1,0:T(8,128)(2,1)}, bf16[128,512]{1,0:T(8,128)(2,1)S(1)}, u32[]{:S(2)}, u32[]{:S(2)}) collective-permute-start(bf16[128,512]{1,0:T(8,128)(2,1)} %get-tuple-element.37), channel_id=1, source_target_pairs={{0,2},{1,3},{2,0},{3,1},{4,6},{5,7},{6,4},{7,5},{8,10},{9,11},{10,... | collective-permute-start | bytes 393224 | tf_op jit(solution)/shard_map/ppermute | solution.py:124
  41.3 22.0 %copy-start.5 = (f32[2,128,256]{2,1,0:T(8,128)S(1)}, f32[2,128,256]{2,1,0:T(8,128)}, u32[]{:S(2)}) copy-start(f32[2,128,256]{2,1,0:T(8,128)} %get-tuple-element.34.first_ref) | copy-start | bytes 786436
  41.3 22.0 %all-to-all-start.2 = ((f32[16,16,256]{2,1,0:T(8,128)}), f32[16,16,256]{2,1,0:T(8,128)S(1)}, u32[]{:S(2)}, u32[]{:S(2)}) async-start(f32[16,16,256]{2,1,0:T(8,128)} %get-tuple-element.33), calls=%async_computation.2 | async-start | bytes 524288 | tf_op jit(solution)/shard_map/all_to_all | solution.py:450
  45.0 8.7 %collective-permute-start.2 = (bf16[128,512]{1,0:T(8,128)(2,1)}, bf16[128,512]{1,0:T(8,128)(2,1)S(1)}, u32[]{:S(2)}, u32[]{:S(2)}) collective-permute-start(bf16[128,512]{1,0:T(8,128)(2,1)} %get-tuple-element.38), channel_id=1, source_target_pairs={{0,3},{1,2},{2,1},{3,0},{4,7},{5,6},{6,5},{7,4},{8,11},{9,10},{10,... | collective-permute-start | bytes 393224 | tf_op jit(solution)/shard_map/ppermute | solution.py:124
  47.5 7.3 %collective-permute-start.3 = (bf16[128,512]{1,0:T(8,128)(2,1)}, bf16[128,512]{1,0:T(8,128)(2,1)S(1)}, u32[]{:S(2)}, u32[]{:S(2)}) collective-permute-start(bf16[128,512]{1,0:T(8,128)(2,1)} %get-tuple-element.39), channel_id=1, source_target_pairs={{0,4},{1,5},{2,6},{3,7},{4,0},{5,1},{6,2},{7,3},{8,12},{9,13},{10,... | collective-permute-start | bytes 393224 | tf_op jit(solution)/shard_map/ppermute | solution.py:124
  49.3 8.4 %collective-permute-start.4 = (bf16[128,512]{1,0:T(8,128)(2,1)S(1)}, bf16[128,512]{1,0:T(8,128)(2,1)S(1)}, u32[]{:S(2)}, u32[]{:S(2)}) collective-permute-start(bf16[128,512]{1,0:T(8,128)(2,1)S(1)} %get-tuple-element.40), channel_id=1, source_target_pairs={{0,5},{1,4},{2,7},{3,6},{4,1},{5,0},{6,3},{7,2},{8,13},{9,12},{10,... | collective-permute-start | bytes 393224 | tf_op jit(solution)/shard_map/ppermute | solution.py:124
  50.5 9.9 %collective-permute-start.5 = (bf16[128,512]{1,0:T(8,128)(2,1)S(1)}, bf16[128,512]{1,0:T(8,128)(2,1)S(1)}, u32[]{:S(2)}, u32[]{:S(2)}) collective-permute-start(bf16[128,512]{1,0:T(8,128)(2,1)S(1)} %get-tuple-element.41), channel_id=1, source_target_pairs={{0,6},{1,7},{2,4},{3,5},{4,2},{5,3},{6,0},{7,1},{8,14},{9,15},{10,... | collective-permute-start | bytes 393224 | tf_op jit(solution)/shard_map/ppermute | solution.py:124
  51.4 11.9 %collective-permute-start.6 = (bf16[128,512]{1,0:T(8,128)(2,1)S(1)}, bf16[128,512]{1,0:T(8,128)(2,1)S(1)}, u32[]{:S(2)}, u32[]{:S(2)}) collective-permute-start(bf16[128,512]{1,0:T(8,128)(2,1)S(1)} %get-tuple-element.42), channel_id=1, source_target_pairs={{0,7},{1,6},{2,5},{3,4},{4,3},{5,2},{6,1},{7,0},{8,15},{9,14},{10,... | collective-permute-start | bytes 393224 | tf_op jit(solution)/shard_map/ppermute | solution.py:124
  87.5 19.1 %copy-start.2 = (bf16[1024,256]{1,0:T(8,128)(2,1)S(1)}, bf16[1024,256]{1,0:T(8,128)(2,1)}, u32[]{:S(2)}) copy-start(bf16[1024,256]{1,0:T(8,128)(2,1)} %get-tuple-element.55.grad_ref) | copy-start | bytes 1572868
  102.3 4.3 %copy-start = (bf16[1024,256]{1,0:T(8,128)(2,1)S(1)}, bf16[1024,256]{1,0:T(8,128)(2,1)}, u32[]{:S(2)}) copy-start(bf16[1024,256]{1,0:T(8,128)(2,1)} %get-tuple-element.43.a_ref.adjoint_ref) | copy-start | bytes 1572868
  102.3 4.3 %copy-start.1 = (bf16[1024,256]{1,0:T(8,128)(2,1)S(1)}, bf16[1024,256]{1,0:T(8,128)(2,1)}, u32[]{:S(2)}) copy-start(bf16[1024,256]{1,0:T(8,128)(2,1)} %get-tuple-element.56.solved_ref) | copy-start | bytes 1572868
  103.1 11.0 %all-to-all-start.4 = ((f32[16,16,256]{2,1,0:T(8,128)}), f32[16,16,256]{2,1,0:T(8,128)S(1)}, u32[]{:S(2)}, u32[]{:S(2)}) async-start(f32[16,16,256]{2,1,0:T(8,128)} %scan_back.1), calls=%async_computation.4 | async-start | bytes 524288 | tf_op jit(solution)/shard_map/all_to_all | solution.py:450
  106.6 7.5 %copy-start.6 = (f32[2,128,256]{2,1,0:T(8,128)S(1)}, f32[2,128,256]{2,1,0:T(8,128)}, u32[]{:S(2)}) copy-start(f32[2,128,256]{2,1,0:T(8,128)} %get-tuple-element.54.second_ref) | copy-start | bytes 786436
  117.4 30.4 %all-to-all-start.5 = ((bf16[8,128,512]{2,1,0:T(8,128)(2,1)}), bf16[8,128,512]{2,1,0:T(8,128)(2,1)S(1)}, u32[]{:S(2)}, u32[]{:S(2)}) async-start(bf16[8,128,512]{2,1,0:T(8,128)(2,1)} %bitcast.5), calls=%async_computation.5 | async-start | bytes 2097152 | tf_op jit(solution)/shard_map/all_to_all | solution.py:450
  124.1 16.4 %collective-permute-start.10 = (bf16[128,256]{1,0:T(8,128)(2,1)S(1)}, bf16[128,256]{1,0:T(8,128)(2,1)S(1)}, u32[]{:S(2)}, u32[]{:S(2)}) collective-permute-start(bf16[128,256]{1,0:T(8,128)(2,1)S(1)} %get-tuple-element.48), channel_id=1, source_target_pairs={{0,4},{1,5},{2,6},{3,7},{4,0},{5,1},{6,2},{7,3},{8,12},{9,13},{10,... | collective-permute-start | bytes 196616 | tf_op jit(solution)/shard_map/ppermute | solution.py:124
  127.0 15.2 %collective-permute-start.11 = (bf16[128,256]{1,0:T(8,128)(2,1)S(1)}, bf16[128,256]{1,0:T(8,128)(2,1)S(1)}, u32[]{:S(2)}, u32[]{:S(2)}) collective-permute-start(bf16[128,256]{1,0:T(8,128)(2,1)S(1)} %get-tuple-element.49), channel_id=1, source_target_pairs={{0,5},{1,4},{2,7},{3,6},{4,1},{5,0},{6,3},{7,2},{8,13},{9,12},{10,... | collective-permute-start | bytes 196616 | tf_op jit(solution)/shard_map/ppermute | solution.py:124
  127.4 16.3 %collective-permute-start.12 = (bf16[128,256]{1,0:T(8,128)(2,1)S(1)}, bf16[128,256]{1,0:T(8,128)(2,1)S(1)}, u32[]{:S(2)}, u32[]{:S(2)}) collective-permute-start(bf16[128,256]{1,0:T(8,128)(2,1)S(1)} %get-tuple-element.50), channel_id=1, source_target_pairs={{0,6},{1,7},{2,4},{3,5},{4,2},{5,3},{6,0},{7,1},{8,14},{9,15},{10,... | collective-permute-start | bytes 196616 | tf_op jit(solution)/shard_map/ppermute | solution.py:124
  130.2 14.4 %collective-permute-start.13 = (bf16[128,256]{1,0:T(8,128)(2,1)S(1)}, bf16[128,256]{1,0:T(8,128)(2,1)S(1)}, u32[]{:S(2)}, u32[]{:S(2)}) collective-permute-start(bf16[128,256]{1,0:T(8,128)(2,1)S(1)} %get-tuple-element.51), channel_id=1, source_target_pairs={{0,7},{1,6},{2,5},{3,4},{4,3},{5,2},{6,1},{7,0},{8,15},{9,14},{10,... | collective-permute-start | bytes 196616 | tf_op jit(solution)/shard_map/ppermute | solution.py:124
  130.5 14.1 %collective-permute-start.7 = (bf16[128,256]{1,0:T(8,128)(2,1)S(1)}, bf16[128,256]{1,0:T(8,128)(2,1)S(1)}, u32[]{:S(2)}, u32[]{:S(2)}) collective-permute-start(bf16[128,256]{1,0:T(8,128)(2,1)S(1)} %get-tuple-element.45), channel_id=1, source_target_pairs={{0,1},{1,0},{2,3},{3,2},{4,5},{5,4},{6,7},{7,6},{8,9},{9,8},{10,11... | collective-permute-start | bytes 196616 | tf_op jit(solution)/shard_map/ppermute | solution.py:124
  140.4 4.2 %collective-permute-start.8 = (bf16[128,256]{1,0:T(8,128)(2,1)S(1)}, bf16[128,256]{1,0:T(8,128)(2,1)S(1)}, u32[]{:S(2)}, u32[]{:S(2)}) collective-permute-start(bf16[128,256]{1,0:T(8,128)(2,1)S(1)} %get-tuple-element.46), channel_id=1, source_target_pairs={{0,2},{1,3},{2,0},{3,1},{4,6},{5,7},{6,4},{7,5},{8,10},{9,11},{10,... | collective-permute-start | bytes 196616 | tf_op jit(solution)/shard_map/ppermute | solution.py:124
  142.2 4.8 %collective-permute-start.9 = (bf16[128,256]{1,0:T(8,128)(2,1)S(1)}, bf16[128,256]{1,0:T(8,128)(2,1)S(1)}, u32[]{:S(2)}, u32[]{:S(2)}) collective-permute-start(bf16[128,256]{1,0:T(8,128)(2,1)S(1)} %get-tuple-element.47), channel_id=1, source_target_pairs={{0,3},{1,2},{2,1},{3,0},{4,7},{5,6},{6,5},{7,4},{8,11},{9,10},{10,... | collective-permute-start | bytes 196616 | tf_op jit(solution)/shard_map/ppermute | solution.py:124
